TPU v7x, 512 devices: a whole 4x4x16 slice. The times are simulated.
512 devices in a mesh: ep: 16 (over z), mx: 4 (over x), my: 8 (over y, core).
Axes of the slice: x: 4, y: 4, z: 16, core: 2. Of those that a mesh axis runs over, the one named last changes fastest.
Arguments:
- context: bfloat16 [16384, 2048], P(('ep', 'mx')), may hold values from -6 to 6
- resid_in: bfloat16 [16384, 2048], P(('ep', 'mx'), 'my'), may hold values from -70 to 70
- out_weight: bfloat16 [2048, 2048], P(None, 'my'), may hold values from -0.125 to 0.125
- norm_gain: float32 [2048], P('my'), may hold values from 0.5 to 1.5
- gate_weight: bfloat16 [8, 5632, 2048], P(None, ('ep', 'my'), 'mx'), may hold values from -0.125 to 0.125
- up_weight: bfloat16 [8, 5632, 2048], P(None, ('ep', 'my'), 'mx'), may hold values from -0.125 to 0.125
- down_weight: bfloat16 [8, 5632, 2048], P(None, ('ep', 'my'), 'mx'), may hold values from -0.078125 to 0.078125
- routes: int32 [16384, 2], P(('ep', 'mx')), may hold values from 0 to 7, all different within a row; in each aligned block of 256 rows (0 to 255, 256 to 511, ...) at most 96 rows name the same one
- gate_probs: float32 [16384, 2], P(('ep', 'mx')), may hold values from 0.05 to 1
- final_gain: float32 [2048], P('my'), may hold values from 0.5 to 1.5
Outputs:
- normed_out: bfloat16 [16384, 2048], P(('ep', 'mx'), 'my')
- stream_out: bfloat16 [16384, 2048], P(('ep', 'mx'), 'my')
Inputs may be any that keep to these rules, and one draw needn't show every extreme that they name: `routes`: each row names 2 different experts; in each aligned block of 256 rows no expert is named by more than 96 rows, a bound that some block reaches.
All inputs are finite; a program needn't handle non-finite values.
Results may differ from a plain program's by a relative error of at most 0.012.
Values may be sent and summed in bfloat16 or wider, within the bound.
A program may use at most 128 MiB of HBM per device.

v0:
```python
import jax
import jax.numpy as jnp
import numpy as np
from jax import lax
from jax.sharding import PartitionSpec as P

D = 2048
EXPERTS = 8
TOPK = 2
MOST = 96


EPSILON = 1e-06


def row_scale(stream_f):
    partial_sq = jnp.sum(stream_f * stream_f, axis=1)
    row_total = lax.psum(partial_sq, "my")
    return lax.rsqrt(row_total / D + EPSILON)


def shards(
    context,
    resid_in,
    out_weight,
    norm_gain,
    gate_weight,
    up_weight,
    down_weight,
    routes,
    gate_probs,
    final_gain,
):
    ep_count = lax.axis_size("ep")
    mx_count = lax.axis_size("mx")
    slot_dev = max(1, EXPERTS // ep_count)
    slot_total = slot_dev * ep_count
    replicas = slot_total // EXPERTS
    capacity = MOST // replicas
    tok_rows = context.shape[0]
    feat_block = resid_in.shape[1]
    piece_units = gate_weight.shape[1]
    width_block = gate_weight.shape[2]
    slot_rows = ep_count * capacity
    projected = jnp.dot(context, out_weight, preferred_element_type=jnp.float32)
    stream = (projected + resid_in.astype(jnp.float32)).astype(jnp.bfloat16)
    stream_f = stream.astype(jnp.float32)
    normed = (stream_f * row_scale(stream_f)[:, None] * norm_gain[None, :]).astype(jnp.bfloat16)
    chosen = routes.reshape(-1)
    onehot = (chosen[:, None] == jnp.arange(EXPERTS, dtype=jnp.int32)[None, :]).astype(jnp.int32)
    before = jnp.cumsum(onehot, axis=0) - onehot
    ranking = jnp.sum(before * onehot, axis=1)
    slot_index = chosen * replicas + ranking % replicas
    target = slot_index * capacity + ranking // replicas
    row_ids = jnp.arange(tok_rows * TOPK, dtype=jnp.int32) // TOPK
    source = jnp.full((slot_total * capacity,), tok_rows, jnp.int32).at[target].set(row_ids)
    padded = jnp.concatenate([normed, jnp.zeros((1, feat_block), jnp.bfloat16)], axis=0)
    packed = padded[source].reshape(ep_count, slot_dev, capacity, feat_block)
    landed = lax.all_to_all(packed, "ep", split_axis=0, concat_axis=0, tiled=True)
    gathered = lax.all_gather(landed, "my", axis=3, tiled=True)
    tokens_in = jnp.transpose(gathered, (1, 0, 2, 3)).reshape(slot_dev, slot_rows, D)
    split_rows = tokens_in.reshape(slot_dev, slot_rows, mx_count, width_block)
    expert_table = (
        np.arange(ep_count)[:, None] * slot_dev + np.arange(slot_dev)[None, :]
    ) // replicas

    def widen_pieces(weight):
        chosen_rows = weight[expert_table]
        wide = jnp.broadcast_to(
            chosen_rows[:, None], (ep_count, mx_count, slot_dev, piece_units, width_block)
        )
        return wide.reshape(ep_count * mx_count, slot_dev, piece_units, width_block)

    got_gate, got_up, got_down = (
        lax.all_to_all(
            widen_pieces(gate_weight), ("ep", "mx"), split_axis=0, concat_axis=0, tiled=True
        ),
        lax.all_to_all(
            widen_pieces(up_weight), ("ep", "mx"), split_axis=0, concat_axis=0, tiled=True
        ),
        lax.all_to_all(
            widen_pieces(down_weight), ("ep", "mx"), split_axis=0, concat_axis=0, tiled=True
        ),
    )
    dims_five = (ep_count, mx_count, slot_dev, piece_units, width_block)
    gate_proj = jnp.einsum(
        "jrad,sajfd->jrsf",
        split_rows,
        got_gate.reshape(dims_five),
        preferred_element_type=jnp.float32,
    )
    up_proj = jnp.einsum(
        "jrad,sajfd->jrsf",
        split_rows,
        got_up.reshape(dims_five),
        preferred_element_type=jnp.float32,
    )
    hidden = (jax.nn.silu(gate_proj) * up_proj).astype(jnp.bfloat16)
    expert_out = jnp.einsum(
        "jrsf,sajfd->jrad", hidden, got_down.reshape(dims_five), preferred_element_type=jnp.float32
    )
    expert_out = expert_out.reshape(slot_dev, slot_rows, D)
    summed = lax.psum_scatter(
        expert_out.astype(jnp.bfloat16), "my", scatter_dimension=2, tiled=True
    )
    sent_back = summed.reshape(slot_dev, ep_count, capacity, feat_block)
    sent_back = jnp.transpose(sent_back, (1, 0, 2, 3))
    returned = lax.all_to_all(sent_back, "ep", split_axis=0, concat_axis=0, tiled=True).reshape(
        slot_total * capacity, feat_block
    )
    picked = returned[target].reshape(tok_rows, TOPK, feat_block).astype(jnp.float32)
    weights_norm = gate_probs / jnp.sum(gate_probs, axis=1, keepdims=True)
    mixed = jnp.sum(weights_norm[:, :, None] * picked, axis=1)
    updated = stream_f + mixed
    normed_out = (updated * row_scale(updated)[:, None] * final_gain[None, :]).astype(jnp.bfloat16)
    return (normed_out, updated.astype(jnp.bfloat16))


def solution(mesh):
    placed = (
        P(("ep", "mx"), None),
        P(("ep", "mx"), "my"),
        P(None, "my"),
        P("my"),
        P(None, ("ep", "my"), "mx"),
        P(None, ("ep", "my"), "mx"),
        P(None, ("ep", "my"), "mx"),
        P(("ep", "mx"), None),
        P(("ep", "mx"), None),
        P("my"),
    )
    return jax.shard_map(
        shards,
        mesh=mesh,
        in_specs=placed,
        out_specs=(P(("ep", "mx"), "my"), P(("ep", "mx"), "my")),
        check_vma=False,
    )
```

profile of v0, /device:TPU:1, one launch (start us, length us, event | category | flops | bytes accessed | tf_op | source)
XLA Modules:
  0.0 641.5 jit_solution(12226968780941671538)
XLA Ops:
  7.2 0.0 copy-start
  7.2 0.0 copy-start.5
  7.2 0.9 copy.30
  8.1 0.1 eq.31
  8.2 0.1 eq.27
  8.4 0.7 broadcast_multiply_fusion
  9.1 1.1 reduce-window.6
  10.2 0.2 slice_reduce_fusion
  10.5 0.1 copy.29
  10.6 0.1 mul.97
  10.8 0.1 fusion.28
  10.9 2.4 scatter_custom_fusion
  13.4 0.0 copy-done
  13.4 0.0 copy-start.7
  13.4 0.0 copy-start.1
  13.4 1.8 multiply_reduce_fusion.2
  15.2 18.7 %psum.14 = f32[256]{0:T(256)S(1)} all-reduce(f32[256]{0:T(256)S(1)} %get-tuple-element.4), channel_id=1, replica_groups=mesh['ep'=16,'mx'=4,'my'=8] {'my'}, use_global_device_ids=true, to_apply=%region_2.0 | all-reduce | flops 256 | bytes 2048 | tf_op jit(solution)/shard_map/psum | solution.py:18
  33.9 0.0 copy-done.5
  33.9 0.1 multiply_convert_fusion.1
  34.0 3.3 gather_fusion
  37.3 9.8 %all-to-all-start = ((bf16[16,1,48,256]{3,2,1,0:T(8,128)(2,1)}), bf16[16,1,48,256]{3,2,1,0:T(8,128)(2,1)}, u32[]{:S(2)}, u32[]{:S(2)}) async-start(bf16[16,1,48,256]{3,2,1,0:T(8,128)(2,1)} %bitcast.5), calls=%async_computation | async-start | bytes 786432 | tf_op jit(solution)/shard_map/all_to_all | solution.py:59
  47.1 0.0 copy-done.7
  47.1 0.0 copy-done.1
  47.1 2.6 gather_fusion.1
  49.7 0.4 copy.33
  50.1 12.3 %all-to-all-done = bf16[16,1,48,256]{3,2,1,0:T(8,128)(2,1)} async-done(((bf16[16,1,48,256]{3,2,1,0:T(8,128)(2,1)}), bf16[16,1,48,256]{3,2,1,0:T(8,128)(2,1)}, u32[]{:S(2)}, u32[]{:S(2)}) %all-to-all-start) | async-done | bytes 393248 | tf_op jit(solution)/shard_map/all_to_all | solution.py:59
  62.4 2.1 broadcast_in_dim.59
  64.5 17.2 %all-to-all-start.1 = ((bf16[64,1,44,512]{3,2,1,0:T(8,128)(2,1)}), bf16[64,1,44,512]{3,2,1,0:T(8,128)(2,1)}, u32[]{:S(2)}, u32[]{:S(2)}) async-start(bf16[64,1,44,512]{3,2,1,0:T(8,128)(2,1)} %bitcast.87), calls=%async_computation.1 | async-start | bytes 6291456 | tf_op jit(solution)/shard_map/all_to_all | solution.py:75
  81.7 0.0 copy-done.2
  81.7 2.6 gather_fusion.3
  84.3 0.4 copy.37
  84.7 135.3 %all-to-all-done.1 = bf16[64,1,44,512]{3,2,1,0:T(8,128)(2,1)} async-done(((bf16[64,1,44,512]{3,2,1,0:T(8,128)(2,1)}), bf16[64,1,44,512]{3,2,1,0:T(8,128)(2,1)}, u32[]{:S(2)}, u32[]{:S(2)}) %all-to-all-start.1) | async-done | bytes 2883616 | tf_op jit(solution)/shard_map/all_to_all | solution.py:75
  220.0 2.1 broadcast_in_dim.67
  222.1 11.8 %all-to-all-start.3 = ((bf16[64,1,44,512]{3,2,1,0:T(8,128)(2,1)}), bf16[64,1,44,512]{3,2,1,0:T(8,128)(2,1)}, u32[]{:S(2)}, u32[]{:S(2)}) async-start(bf16[64,1,44,512]{3,2,1,0:T(8,128)(2,1)} %bitcast.86), calls=%async_computation.3 | async-start | bytes 6291456 | tf_op jit(solution)/shard_map/all_to_all | solution.py:81
  234.0 0.0 copy-done.3
  234.0 2.6 gather_fusion.2
  236.6 0.4 copy.35
  237.0 136.2 %all-to-all-done.3 = bf16[64,1,44,512]{3,2,1,0:T(8,128)(2,1)} async-done(((bf16[64,1,44,512]{3,2,1,0:T(8,128)(2,1)}), bf16[64,1,44,512]{3,2,1,0:T(8,128)(2,1)}, u32[]{:S(2)}, u32[]{:S(2)}) %all-to-all-start.3) | async-done | bytes 2883616 | tf_op jit(solution)/shard_map/all_to_all | solution.py:81
  373.2 2.1 broadcast_in_dim.63
  375.3 9.6 %all-to-all-start.2 = ((bf16[64,1,44,512]{3,2,1,0:T(8,128)(2,1)}), bf16[64,1,44,512]{3,2,1,0:T(8,128)(2,1)}, u32[]{:S(2)}, u32[]{:S(2)}) async-start(bf16[64,1,44,512]{3,2,1,0:T(8,128)(2,1)} %bitcast.85), calls=%async_computation.2 | async-start | bytes 6291456 | tf_op jit(solution)/shard_map/all_to_all | solution.py:78
  384.9 0.0 all-gather.2.cloned.1.call-start
  385.0 0.7 all-gather.2.cloned.1.call-update
  385.7 0.0 reduce-scatter.2.cloned.1.call-start
  385.7 46.4 %all-gather.2.cloned.1.call-done = bf16[16,1,48,2048]{3,2,1,0:T(8,128)(2,1)} async-done(((bf16[16,1,48,256]{3,2,1,0:T(8,128)(2,1)}), bf16[16,1,48,2048]{3,2,1,0:T(8,128)(2,1)}) %all-gather.2.cloned.1.call-update) | async-done | bytes 3145744 | tf_op jit(solution)/shard_map/all_gather | solution.py:60
  432.1 6.2 reshape.196
  438.2 5.7 copy.61
  443.9 6.7 %dot_general.20 = bf16[2048,44,16]{0,2,1:T(8,128)(2,1)} reshape(bf16[4,512,44,16]{1,0,3,2:T(4,128)(2,1)} %bitcast.88) | data formatting | bytes 5767168 | tf_op jit(solution)/shard_map/jrsf,sajfd->jrad/dot_general | solution.py:99
  450.6 6.9 %fusion.2 = f32[768,16,44,1]{0,2,3,1:T(8,128)} fusion(bf16[768,4,512]{2,1,0:T(4,128)(2,1)} %reshape.196, bf16[16,4,44,512]{3,2,1,0:T(8,128)(2,1)} %bitcast.80), kind=kOutput, calls=%fused_computation.9 | convolution fusion | flops 2214592512 | bytes 8192000 | tf_op jit(solution)/shard_map/jrad,sajfd->jrsf/dot_general | solution.py:86
  457.5 65.7 %all-to-all-done.2 = bf16[64,1,44,512]{3,2,1,0:T(8,128)(2,1)} async-done(((bf16[64,1,44,512]{3,2,1,0:T(8,128)(2,1)}), bf16[64,1,44,512]{3,2,1,0:T(8,128)(2,1)}, u32[]{:S(2)}, u32[]{:S(2)}) %all-to-all-start.2) | async-done | bytes 2883616 | tf_op jit(solution)/shard_map/all_to_all | solution.py:78
  523.2 16.1 %fusion.7 = bf16[1,768,2048]{2,1,0:T(8,128)(2,1)} fusion(bf16[2048,44,16]{0,2,1:T(8,128)(2,1)} %dot_general.20, f32[768,16,44,1]{0,2,3,1:T(8,128)} %fusion.2, bf16[768,4,512]{2,1,0:T(4,128)(2,1)} %reshape.196, bf16[16,4,44,512]{3,2,1,0:T(8,128)(2,1)} %bitcast.83), kind=kOutput, calls=%fused_computation.14 | convolution fusion | flops 4434001920 | bytes 14221312 | tf_op jit(solution)/shard_map/jrsf,sajfd->jrad/dot_general | solution.py:99
  539.4 0.0 reduce-scatter.2.cloned.1.call-update
  539.4 0.0 copy-start.6
  539.4 43.0 %reduce-scatter.2.cloned.1.call-done = bf16[1,768,256]{2,1,0:T(8,128)(2,1)} async-done(((bf16[1,768,2048]{2,1,0:T(8,128)(2,1)}), bf16[1,768,256]{2,1,0:T(8,128)(2,1)}) %reduce-scatter.2.cloned.1.call-update) | async-done | bytes 393232 | tf_op jit(solution)/shard_map/reduce_scatter | solution.py:103
  582.4 11.1 %all-to-all-start.4 = ((bf16[16,1,48,256]{3,2,1,0:T(8,128)(2,1)}), bf16[16,1,48,256]{3,2,1,0:T(8,128)(2,1)S(1)}, u32[]{:S(2)}, u32[]{:S(2)}) async-start(bf16[16,1,48,256]{3,2,1,0:T(8,128)(2,1)} %bitcast.89), calls=%async_computation.5 | async-start | bytes 786432 | tf_op jit(solution)/shard_map/all_to_all | solution.py:108
  593.4 0.0 copy-done.4
  593.5 0.1 copy.28
  593.6 14.5 %all-to-all-done.4 = bf16[16,1,48,256]{3,2,1,0:T(8,128)(2,1)S(1)} async-done(((bf16[16,1,48,256]{3,2,1,0:T(8,128)(2,1)}), bf16[16,1,48,256]{3,2,1,0:T(8,128)(2,1)S(1)}, u32[]{:S(2)}, u32[]{:S(2)}) %all-to-all-start.4) | async-done | bytes 393248 | tf_op jit(solution)/shard_map/all_to_all | solution.py:108
  608.2 1.9 gather_fusion.4
  610.1 0.3 reshape.201
  610.4 0.7 multiply_reduce_fusion
  611.1 0.7 fusion.37
  611.8 0.1 multiply_reduce_fusion.1
  611.9 22.0 %psum.15 = f32[256]{0:T(256)S(1)} all-reduce(f32[256]{0:T(256)S(1)} %multiply_reduce_fusion.1), channel_id=1, replica_groups=mesh['ep'=16,'mx'=4,'my'=8] {'my'}, use_global_device_ids=true, to_apply=%region_10.11 | all-reduce | flops 256 | bytes 2048 | tf_op jit(solution)/shard_map/psum | solution.py:18
  633.9 0.8 multiply_convert_fusion
  (18 shorter events, 0.2 us)
Async XLA Ops:
  7.2 6.2 copy-start
  7.2 26.7 %copy-start.5 = (f32[256]{0:T(256)S(1)}, f32[256]{0:T(256)}, u32[]{:S(2)}) copy-start(f32[256]{0:T(256)} %param.17) | copy-start | bytes 3076
  13.4 33.7 %copy-start.7 = (s32[16]{0:T(128)S(1)}, s32[16]{0:T(128)}, u32[]{:S(2)}) copy-start(s32[16]{0:T(128)} %constant.78) | copy-start | bytes 196
  13.4 33.7 %copy-start.1 = (bf16[8,44,512]{2,0,1:T(8,128)(2,1)S(1)}, bf16[8,44,512]{2,0,1:T(8,128)(2,1)}, u32[]{:S(2)}) copy-start(bf16[8,44,512]{2,0,1:T(8,128)(2,1)} %param.18) | copy-start | bytes 1081348
  37.3 25.1 %all-to-all-start = ((bf16[16,1,48,256]{3,2,1,0:T(8,128)(2,1)}), bf16[16,1,48,256]{3,2,1,0:T(8,128)(2,1)}, u32[]{:S(2)}, u32[]{:S(2)}) async-start(bf16[16,1,48,256]{3,2,1,0:T(8,128)(2,1)} %bitcast.5), calls=%async_computation | async-start | bytes 786432 | tf_op jit(solution)/shard_map/all_to_all | solution.py:59
  64.5 17.2 %copy-start.2 = (bf16[8,44,512]{2,0,1:T(8,128)(2,1)S(1)}, bf16[8,44,512]{2,0,1:T(8,128)(2,1)}, u32[]{:S(2)}) copy-start(bf16[8,44,512]{2,0,1:T(8,128)(2,1)} %param.20) | copy-start | bytes 1081348
  64.5 155.6 %all-to-all-start.1 = ((bf16[64,1,44,512]{3,2,1,0:T(8,128)(2,1)}), bf16[64,1,44,512]{3,2,1,0:T(8,128)(2,1)}, u32[]{:S(2)}, u32[]{:S(2)}) async-start(bf16[64,1,44,512]{3,2,1,0:T(8,128)(2,1)} %bitcast.87), calls=%async_computation.1 | async-start | bytes 6291456 | tf_op jit(solution)/shard_map/all_to_all | solution.py:75
  222.1 11.9 %copy-start.3 = (bf16[8,44,512]{2,0,1:T(8,128)(2,1)S(1)}, bf16[8,44,512]{2,0,1:T(8,128)(2,1)}, u32[]{:S(2)}) copy-start(bf16[8,44,512]{2,0,1:T(8,128)(2,1)} %param.19) | copy-start | bytes 1081348
  222.1 151.1 %all-to-all-start.3 = ((bf16[64,1,44,512]{3,2,1,0:T(8,128)(2,1)}), bf16[64,1,44,512]{3,2,1,0:T(8,128)(2,1)}, u32[]{:S(2)}, u32[]{:S(2)}) async-start(bf16[64,1,44,512]{3,2,1,0:T(8,128)(2,1)} %bitcast.86), calls=%async_computation.3 | async-start | bytes 6291456 | tf_op jit(solution)/shard_map/all_to_all | solution.py:81
  375.3 147.9 %all-to-all-start.2 = ((bf16[64,1,44,512]{3,2,1,0:T(8,128)(2,1)}), bf16[64,1,44,512]{3,2,1,0:T(8,128)(2,1)}, u32[]{:S(2)}, u32[]{:S(2)}) async-start(bf16[64,1,44,512]{3,2,1,0:T(8,128)(2,1)} %bitcast.85), calls=%async_computation.2 | async-start | bytes 6291456 | tf_op jit(solution)/shard_map/all_to_all | solution.py:78
  384.9 47.1 %all-gather.2.cloned.1.call-start = ((), (), s32[]{:S(2)}) async-start(), calls=%async_computation.6 | async-start | bytes 3538944 | tf_op jit(solution)/shard_map/all_gather | solution.py:60
  385.7 196.7 %reduce-scatter.2.cloned.1.call-start = ((), (), s32[]{:S(2)}) async-start(), calls=%async_computation.7 | async-start | bytes 3538944 | tf_op jit(solution)/shard_map/reduce_scatter | solution.py:103
  539.4 54.1 %copy-start.4 = (f32[256,2]{0,1:T(2,128)S(1)}, f32[256,2]{0,1:T(2,128)}, u32[]{:S(2)}) copy-start(f32[256,2]{0,1:T(2,128)} %param.22) | copy-start | bytes 6148
  539.4 94.5 %copy-start.6 = (f32[256]{0:T(256)S(1)}, f32[256]{0:T(256)}, u32[]{:S(2)}) copy-start(f32[256]{0:T(256)} %param.23) | copy-start | bytes 3076
  582.4 25.8 %all-to-all-start.4 = ((bf16[16,1,48,256]{3,2,1,0:T(8,128)(2,1)}), bf16[16,1,48,256]{3,2,1,0:T(8,128)(2,1)S(1)}, u32[]{:S(2)}, u32[]{:S(2)}) async-start(bf16[16,1,48,256]{3,2,1,0:T(8,128)(2,1)} %bitcast.89), calls=%async_computation.5 | async-start | bytes 786432 | tf_op jit(solution)/shard_map/all_to_all | solution.py:108
Sparse Core Ops, SparseCore 0:
  387.9 44.1 all-gather.1
  539.5 42.8 reduce-scatter.1
where the time goes:
time: 644 us; the launch traced here: 641 us
  waiting for transfers between devices  454 us (70%)
  starting transfers between devices  59.6 us (9%)
  local copies, waits for them, and re-layouts  43.7 us (7%)
  blocking collectives  40.6 us (6%)
  matrix products  24.8 us (4%)
  between operations  14.3 us (2%)
    all_to_all x1, waiting for transfers between devices, shards(): lax.all_to_all(widen_pieces(down_weight), ('ep', 'mx'), split_axis=0, con...  136 us
    all_to_all x1, waiting for transfers between devices, shards(): lax.all_to_all(widen_pieces(gate_weight), ('ep', 'mx'), split_axis=0, con...  135 us
    all_to_all x1, waiting for transfers between devices, shards(): lax.all_to_all(widen_pieces(up_weight), ('ep', 'mx'), split_axis=0, conca...  65.7 us
    all_gather x1, waiting for transfers between devices, shards(): gathered = lax.all_gather(landed, 'my', axis=3, tiled=True)  46.4 us
    reduce_scatter x1, waiting for transfers between devices, shards(): lax.psum_scatter(expert_out.astype(jnp.bfloat16), 'my', scatter_dimension...  43 us
    psum x2, blocking collectives, row_scale(): row_total = lax.psum(partial_sq, 'my')  40.6 us
    all_to_all x1, starting transfers between devices, shards(): lax.all_to_all(widen_pieces(gate_weight), ('ep', 'mx'), split_axis=0, con...  17.2 us
    dot_general x1, matrix products, shards(): jnp.einsum('jrsf,sajfd->jrad', hidden, got_down.reshape(dims_five), prefe...  16.1 us
  transfers between devices with their start and end apart: 7, of which 7 were waited for; matrix products, arithmetic and copies ran while one was open for 5% of the time, Pallas kernels for 0%

commit v1 on v0

--- a/solution.py
+++ b/solution.py
@@ -32,7 +32,6 @@
     final_gain,
 ):
     ep_count = lax.axis_size("ep")
-    mx_count = lax.axis_size("mx")
     slot_dev = max(1, EXPERTS // ep_count)
     slot_total = slot_dev * ep_count
     replicas = slot_total // EXPERTS
@@ -40,8 +39,18 @@
     tok_rows = context.shape[0]
     feat_block = resid_in.shape[1]
     piece_units = gate_weight.shape[1]
-    width_block = gate_weight.shape[2]
     slot_rows = ep_count * capacity
+
+    expert_table = (
+        np.arange(ep_count)[:, None] * slot_dev + np.arange(slot_dev)[None, :]
+    ) // replicas
+    stacked = jnp.stack([gate_weight, up_weight, down_weight], axis=0)
+    chosen_rows = stacked[:, expert_table]
+    got = lax.all_to_all(chosen_rows, "ep", split_axis=1, concat_axis=1, tiled=True)
+    got = lax.all_gather(got, "mx", axis=4, tiled=True)
+    got = jnp.transpose(got, (0, 2, 1, 3, 4)).reshape(3, slot_dev, ep_count * piece_units, D)
+    w_gate, w_up, w_down = got[0], got[1], got[2]
+
     projected = jnp.dot(context, out_weight, preferred_element_type=jnp.float32)
     stream = (projected + resid_in.astype(jnp.float32)).astype(jnp.bfloat16)
     stream_f = stream.astype(jnp.float32)
@@ -59,47 +68,11 @@
     landed = lax.all_to_all(packed, "ep", split_axis=0, concat_axis=0, tiled=True)
     gathered = lax.all_gather(landed, "my", axis=3, tiled=True)
     tokens_in = jnp.transpose(gathered, (1, 0, 2, 3)).reshape(slot_dev, slot_rows, D)
-    split_rows = tokens_in.reshape(slot_dev, slot_rows, mx_count, width_block)
-    expert_table = (
-        np.arange(ep_count)[:, None] * slot_dev + np.arange(slot_dev)[None, :]
-    ) // replicas
 
-    def widen_pieces(weight):
-        chosen_rows = weight[expert_table]
-        wide = jnp.broadcast_to(
-            chosen_rows[:, None], (ep_count, mx_count, slot_dev, piece_units, width_block)
-        )
-        return wide.reshape(ep_count * mx_count, slot_dev, piece_units, width_block)
-
-    got_gate, got_up, got_down = (
-        lax.all_to_all(
-            widen_pieces(gate_weight), ("ep", "mx"), split_axis=0, concat_axis=0, tiled=True
-        ),
-        lax.all_to_all(
-            widen_pieces(up_weight), ("ep", "mx"), split_axis=0, concat_axis=0, tiled=True
-        ),
-        lax.all_to_all(
-            widen_pieces(down_weight), ("ep", "mx"), split_axis=0, concat_axis=0, tiled=True
-        ),
-    )
-    dims_five = (ep_count, mx_count, slot_dev, piece_units, width_block)
-    gate_proj = jnp.einsum(
-        "jrad,sajfd->jrsf",
-        split_rows,
-        got_gate.reshape(dims_five),
-        preferred_element_type=jnp.float32,
-    )
-    up_proj = jnp.einsum(
-        "jrad,sajfd->jrsf",
-        split_rows,
-        got_up.reshape(dims_five),
-        preferred_element_type=jnp.float32,
-    )
+    gate_proj = jnp.einsum("srd,sfd->srf", tokens_in, w_gate, preferred_element_type=jnp.float32)
+    up_proj = jnp.einsum("srd,sfd->srf", tokens_in, w_up, preferred_element_type=jnp.float32)
     hidden = (jax.nn.silu(gate_proj) * up_proj).astype(jnp.bfloat16)
-    expert_out = jnp.einsum(
-        "jrsf,sajfd->jrad", hidden, got_down.reshape(dims_five), preferred_element_type=jnp.float32
-    )
-    expert_out = expert_out.reshape(slot_dev, slot_rows, D)
+    expert_out = jnp.einsum("srf,sfd->srd", hidden, w_down, preferred_element_type=jnp.float32)
     summed = lax.psum_scatter(
         expert_out.astype(jnp.bfloat16), "my", scatter_dimension=2, tiled=True
     )

time: 644 us -> 398 us (0.62)
  waiting for transfers between devices: 454 us -> 134 us
  blocking collectives: 40.6 us -> 179 us
  starting transfers between devices: 59.6 us -> 11.3 us
  local copies, waits for them, and re-layouts: 43.7 us -> 32.7 us
    all_to_all x4 -> x0, waiting for transfers between devices: 349 us -> none  [the longest x1 136 us: shards(): lax.all_to_all(widen_pieces(down_weight), ('ep', 'mx'), split_axis=0, con...]
    all_to_all x0 -> x2, blocking collectives: none -> 138 us  [the longest x1 118 us: shards(): lax.all_to_all(chosen_rows, 'ep', split_axis=1, concat_axis=1, tiled=True)]
    all_gather x0 -> x1, waiting for transfers between devices: none -> 53.7 us  [shards(): got = lax.all_gather(got, 'mx', axis=4, tiled=True)]
    all_to_all x4 -> x0, starting transfers between devices: 48.4 us -> none  [the longest x1 17.2 us: shards(): lax.all_to_all(widen_pieces(gate_weight), ('ep', 'mx'), split_axis=0, con...]
    all_gather x1, waiting for transfers between devices: 46.4 us -> 23.3 us  [shards(): gathered = lax.all_gather(landed, 'my', axis=3, tiled=True)]
    gather x6 -> x1, local copies, waits for them, and re-layouts: 9.04 us -> 2.11 us  [shards(): chosen_rows = stacked[:, expert_table]]
    dot_general x1 -> x0, local copies, waits for them, and re-layouts: 6.67 us -> none  [shards(): jnp.einsum('jrsf,sajfd->jrad', hidden, got_down.reshape(dims_five), prefe...]
    slice x1 -> x2, local copies, waits for them, and re-layouts: 0.21 us -> 6.82 us  [the longest x1 6.6 us: shards(): w_gate, w_up, w_down = (got[0], got[1], got[2])]
  transfers between devices with their start and end apart: 7 -> 4, of which waited for: 7 -> 4; matrix products, arithmetic and copies ran while one was open for 5% -> 7% of each run, Pallas kernels for 0% -> 0%
where the time goes in v1:
time: 398 us; the launch traced here: 395 us
  blocking collectives  179 us (45%)
  waiting for transfers between devices  134 us (34%)
  local copies, waits for them, and re-layouts  32.7 us (8%)
  matrix products  19.5 us (5%)
  between operations  14 us (4%)
  starting transfers between devices  11.3 us (3%)
  other arithmetic  4.55 us (1%)
    all_to_all x1, blocking collectives, shards(): lax.all_to_all(chosen_rows, 'ep', split_axis=1, concat_axis=1, tiled=True)  118 us
    all_gather x1, waiting for transfers between devices, shards(): got = lax.all_gather(got, 'mx', axis=4, tiled=True)  53.7 us
    reduce_scatter x1, waiting for transfers between devices, shards(): lax.psum_scatter(expert_out.astype(jnp.bfloat16), 'my', scatter_dimension...  42.2 us
    psum x2, blocking collectives, row_scale(): row_total = lax.psum(partial_sq, 'my')  41.2 us
    all_gather x1, waiting for transfers between devices, shards(): gathered = lax.all_gather(landed, 'my', axis=3, tiled=True)  23.3 us
    all_to_all x1, blocking collectives, shards(): lax.all_to_all(packed, 'ep', split_axis=0, concat_axis=0, tiled=True)  19.7 us
    all_to_all x1, waiting for transfers between devices, shards(): lax.all_to_all(sent_back, 'ep', split_axis=0, concat_axis=0, tiled=True)  14.5 us
    another operation x4, local copies, waits for them, and re-layouts  13.1 us
  transfers between devices with their start and end apart: 4, of which 4 were waited for; matrix products, arithmetic and copies ran while one was open for 7% of the time, Pallas kernels for 0%

profile of v1, /device:TPU:1, one launch (start us, length us, event | category | flops | bytes accessed | tf_op | source)
XLA Modules:
  0.0 394.9 jit_solution(5395408487092102578)
XLA Ops:
  7.2 0.0 copy-start
  7.2 0.0 all-gather.5.cloned.1.call-start
  7.2 1.2 copy.35
  8.4 0.7 pad_clamp_fusion.1
  9.1 1.3 copy_bitcast_fusion
  10.4 0.1 pad_maximum_fusion
  10.5 2.1 gather_fusion.1
  12.6 0.0 copy-start.3
  12.6 0.0 copy-start.1
  12.6 0.0 copy-start.2
  12.6 118.3 %all_to_all.15 = bf16[3,16,1,44,512]{4,3,0,2,1:T(8,128)(2,1)} all-to-all(bf16[3,16,1,44,512]{4,3,0,2,1:T(8,128)(2,1)} %bitcast.46), channel_id=1, replica_groups=mesh['ep'=16,'mx'=4,'my'=8] {'ep'}, dimensions={1} | all-to-all | bytes 4325376 | tf_op jit(solution)/shard_map/all_to_all | solution.py:49
  131.0 0.0 copy-start.5
  131.0 0.0 all-gather.5.cloned.1.call-update
  131.0 0.0 all-gather.3.cloned.1.call-start
  131.1 0.0 copy-done.3
  131.1 0.1 copy.24
  131.2 0.1 eq.31
  131.3 0.1 eq.27
  131.5 0.1 copy.23
  131.6 0.1 mul.97
  131.8 1.1 reduce-window.6
  133.0 0.2 slice_reduce_fusion
  133.2 0.0 copy-done
  133.2 0.0 copy-done.1
  133.2 0.0 copy-done.2
  133.2 0.5 multiply_reduce_fusion.2
  133.7 19.3 %psum.14 = f32[256]{0:T(256)S(1)} all-reduce(f32[256]{0:T(256)S(1)} %get-tuple-element.7), channel_id=1, replica_groups=mesh['ep'=16,'mx'=4,'my'=8] {'my'}, use_global_device_ids=true, to_apply=%region_2.0 | all-reduce | flops 256 | bytes 2048 | tf_op jit(solution)/shard_map/psum | solution.py:18
  153.1 0.0 copy-done.5
  153.1 0.1 multiply_convert_fusion.2
  153.2 0.1 fusion.4
  153.3 2.4 scatter_custom_fusion
  155.8 2.7 gather_fusion
  158.5 19.7 %all_to_all.16 = bf16[16,1,48,256]{3,2,1,0:T(8,128)(2,1)} all-to-all(bf16[16,1,48,256]{3,2,1,0:T(8,128)(2,1)S(1)} %bitcast.48), channel_id=1, replica_groups=mesh['ep'=16,'mx'=4,'my'=8] {'ep'}, dimensions={0} | all-to-all | bytes 786432 | tf_op jit(solution)/shard_map/all_to_all | solution.py:68
  178.2 0.0 all-gather.3.cloned.1.call-update
  178.2 0.2 reduce-scatter.2.cloned.1.call-start
  178.4 53.7 %all-gather.5.cloned.1.call-done = bf16[3,16,1,44,2048]{4,3,0,2,1:T(8,128)(2,1)} async-done(((bf16[3,16,1,44,512]{4,3,0,2,1:T(8,128)(2,1)}), bf16[3,16,1,44,2048]{4,3,0,2,1:T(8,128)(2,1)}) %all-gather.5.cloned.1.call-update) | async-done | bytes 8650768 | tf_op jit(solution)/shard_map/all_gather | solution.py:50
  232.1 6.6 %fusion.14 = (bf16[1,16,1,44,2048]{4,3,0,2,1:T(8,128)(2,1)}, bf16[1,16,1,44,2048]{4,3,0,2,1:T(8,128)(2,1)}, bf16[1,16,1,44,2048]{4,3,0,2,1:T(8,128)(2,1)}) fusion(bf16[3,16,1,44,2048]{4,3,0,2,1:T(8,128)(2,1)} %all-gather.5.cloned.1.call-done), kind=kLoop, calls=%fused_computation.52 | loop fusion | bytes 17301504 | tf_op jit(solution)/shard_map/slice | solution.py:52
  238.7 4.4 %reshape.177 = bf16[704,2048]{1,0:T(8,128)(2,1)} reshape(bf16[1,16,1,44,2048]{4,3,0,2,1:T(8,128)(2,1)} %get-tuple-element.5) | data formatting | bytes 5767168 | tf_op jit(solution)/shard_map/reshape.24
  243.1 4.3 %reshape.175 = bf16[704,2048]{1,0:T(8,128)(2,1)} reshape(bf16[1,16,1,44,2048]{4,3,0,2,1:T(8,128)(2,1)} %get-tuple-element.6) | data formatting | bytes 5767168 | tf_op jit(solution)/shard_map/reshape.12
  247.4 4.4 %reshape.176 = bf16[704,2048]{1,0:T(8,128)(2,1)} reshape(bf16[1,16,1,44,2048]{4,3,0,2,1:T(8,128)(2,1)} %get-tuple-element.4) | data formatting | bytes 5767168 | tf_op jit(solution)/shard_map/reshape.19
  251.8 23.3 %all-gather.3.cloned.1.call-done = bf16[16,1,48,2048]{3,2,1,0:T(8,128)(2,1)} async-done(((bf16[16,1,48,256]{3,2,1,0:T(8,128)(2,1)}), bf16[16,1,48,2048]{3,2,1,0:T(8,128)(2,1)}) %all-gather.3.cloned.1.call-update) | async-done | bytes 3145744 | tf_op jit(solution)/shard_map/all_gather | solution.py:69
  275.1 6.6 %fusion.15 = f32[768,704]{0,1:T(8,128)} fusion(bf16[768,2048]{1,0:T(8,128)(2,1)} %bitcast.53, bf16[704,2048]{1,0:T(8,128)(2,1)} %reshape.175), kind=kOutput, calls=%fused_computation.53 | convolution fusion | flops 2214592512 | bytes 8192000 | tf_op jit(solution)/shard_map/srd,sfd->srf/dot_general | solution.py:72
  281.6 12.4 %fusion = bf16[1,768,2048]{2,1,0:T(8,128)(2,1)} fusion(bf16[704,2048]{1,0:T(8,128)(2,1)} %reshape.177, f32[768,704]{0,1:T(8,128)} %fusion.15, bf16[768,2048]{1,0:T(8,128)(2,1)} %bitcast.54, bf16[704,2048]{1,0:T(8,128)(2,1)} %reshape.176), kind=kOutput, calls=%fused_computation.5 | convolution fusion | flops 4434001920 | bytes 14221312 | tf_op jit(solution)/shard_map/srf,sfd->srd/dot_general | solution.py:75
  294.0 0.0 copy-start.4
  294.0 0.0 reduce-scatter.2.cloned.1.call-update
  294.1 42.2 %reduce-scatter.2.cloned.1.call-done = bf16[1,768,256]{2,1,0:T(8,128)(2,1)} async-done(((bf16[1,768,2048]{2,1,0:T(8,128)(2,1)}), bf16[1,768,256]{2,1,0:T(8,128)(2,1)}) %reduce-scatter.2.cloned.1.call-update) | async-done | bytes 393232 | tf_op jit(solution)/shard_map/reduce_scatter | solution.py:76
  336.3 11.0 %all-to-all-start.2 = ((bf16[16,1,48,256]{3,2,1,0:T(8,128)(2,1)}), bf16[16,1,48,256]{3,2,1,0:T(8,128)(2,1)S(1)}, u32[]{:S(2)}, u32[]{:S(2)}) async-start(bf16[16,1,48,256]{3,2,1,0:T(8,128)(2,1)} %bitcast.49), calls=%async_computation.3 | async-start | bytes 786432 | tf_op jit(solution)/shard_map/all_to_all | solution.py:81
  347.3 0.0 copy-done.4
  347.3 0.0 copy-start.6
  347.4 0.1 copy.22
  347.5 14.5 %all-to-all-done.2 = bf16[16,1,48,256]{3,2,1,0:T(8,128)(2,1)S(1)} async-done(((bf16[16,1,48,256]{3,2,1,0:T(8,128)(2,1)}), bf16[16,1,48,256]{3,2,1,0:T(8,128)(2,1)S(1)}, u32[]{:S(2)}, u32[]{:S(2)}) %all-to-all-start.2) | async-done | bytes 393248 | tf_op jit(solution)/shard_map/all_to_all | solution.py:81
  362.1 1.9 gather_fusion.2
  364.0 0.3 reshape.179
  364.3 0.7 multiply_reduce_fusion
  365.0 0.7 fusion.13
  365.7 0.1 multiply_reduce_fusion.1
  365.8 21.9 %psum.15 = f32[256]{0:T(256)S(1)} all-reduce(f32[256]{0:T(256)S(1)} %multiply_reduce_fusion.1), channel_id=1, replica_groups=mesh['ep'=16,'mx'=4,'my'=8] {'my'}, use_global_device_ids=true, to_apply=%region_10.11 | all-reduce | flops 256 | bytes 2048 | tf_op jit(solution)/shard_map/psum | solution.py:18
  387.7 0.0 copy-done.6
  387.7 0.8 multiply_convert_fusion.1
  (14 shorter events, 0.2 us)
Async XLA Ops:
  7.2 126.0 %copy-start = (bf16[256,2048]{1,0:T(8,128)(2,1)S(1)}, bf16[256,2048]{1,0:T(8,128)(2,1)}, u32[]{:S(2)}) copy-start(bf16[256,2048]{1,0:T(8,128)(2,1)} %param.12) | copy-start | bytes 3145732
  7.2 224.9 %all-gather.5.cloned.1.call-start = ((), (), s32[]{:S(2)}) async-start(), calls=%async_computation.5 | async-start | bytes 11796480 | tf_op jit(solution)/shard_map/all_gather | solution.py:50
  12.6 118.4 %copy-start.3 = (s32[256,2]{0,1:T(2,128)S(1)}, s32[256,2]{0,1:T(2,128)}, u32[]{:S(2)}) copy-start(s32[256,2]{0,1:T(2,128)} %param.19) | copy-start | bytes 6148
  12.6 120.6 %copy-start.1 = (bf16[2048,256]{1,0:T(8,128)(2,1)S(1)}, bf16[2048,256]{1,0:T(8,128)(2,1)}, u32[]{:S(2)}) copy-start(bf16[2048,256]{1,0:T(8,128)(2,1)} %param.14) | copy-start | bytes 3145732
  12.6 120.6 %copy-start.2 = (bf16[256,256]{1,0:T(8,128)(2,1)S(1)}, bf16[256,256]{1,0:T(8,128)(2,1)}, u32[]{:S(2)}) copy-start(bf16[256,256]{1,0:T(8,128)(2,1)} %param.13) | copy-start | bytes 393220
  131.0 22.1 %copy-start.5 = (f32[256]{0:T(256)S(1)}, f32[256]{0:T(256)}, u32[]{:S(2)}) copy-start(f32[256]{0:T(256)} %param.15) | copy-start | bytes 3076
  131.0 144.1 %all-gather.3.cloned.1.call-start = ((), (), s32[]{:S(2)}) async-start(), calls=%async_computation.4 | async-start | bytes 3538944 | tf_op jit(solution)/shard_map/all_gather | solution.py:69
  178.2 158.1 %reduce-scatter.2.cloned.1.call-start = ((), (), s32[]{:S(2)}) async-start(), calls=%async_computation.6 | async-start | bytes 3538944 | tf_op jit(solution)/shard_map/reduce_scatter | solution.py:76
  294.0 53.3 %copy-start.4 = (f32[256,2]{0,1:T(2,128)S(1)}, f32[256,2]{0,1:T(2,128)}, u32[]{:S(2)}) copy-start(f32[256,2]{0,1:T(2,128)} %param.20) | copy-start | bytes 6148
  336.3 25.8 %all-to-all-start.2 = ((bf16[16,1,48,256]{3,2,1,0:T(8,128)(2,1)}), bf16[16,1,48,256]{3,2,1,0:T(8,128)(2,1)S(1)}, u32[]{:S(2)}, u32[]{:S(2)}) async-start(bf16[16,1,48,256]{3,2,1,0:T(8,128)(2,1)} %bitcast.49), calls=%async_computation.3 | async-start | bytes 786432 | tf_op jit(solution)/shard_map/all_to_all | solution.py:81
  347.3 40.3 %copy-start.6 = (f32[256]{0:T(256)S(1)}, f32[256]{0:T(256)}, u32[]{:S(2)}) copy-start(f32[256]{0:T(256)} %param.21) | copy-start | bytes 3076
Sparse Core Ops, SparseCore 0:
  131.1 100.9 all-gather.4
  234.2 40.8 all-gather.2
  294.2 42.0 reduce-scatter.1

commit v2 on v1

--- a/solution.py
+++ b/solution.py
@@ -41,16 +41,6 @@
     piece_units = gate_weight.shape[1]
     slot_rows = ep_count * capacity
 
-    expert_table = (
-        np.arange(ep_count)[:, None] * slot_dev + np.arange(slot_dev)[None, :]
-    ) // replicas
-    stacked = jnp.stack([gate_weight, up_weight, down_weight], axis=0)
-    chosen_rows = stacked[:, expert_table]
-    got = lax.all_to_all(chosen_rows, "ep", split_axis=1, concat_axis=1, tiled=True)
-    got = lax.all_gather(got, "mx", axis=4, tiled=True)
-    got = jnp.transpose(got, (0, 2, 1, 3, 4)).reshape(3, slot_dev, ep_count * piece_units, D)
-    w_gate, w_up, w_down = got[0], got[1], got[2]
-
     projected = jnp.dot(context, out_weight, preferred_element_type=jnp.float32)
     stream = (projected + resid_in.astype(jnp.float32)).astype(jnp.bfloat16)
     stream_f = stream.astype(jnp.float32)
@@ -67,6 +57,19 @@
     packed = padded[source].reshape(ep_count, slot_dev, capacity, feat_block)
     landed = lax.all_to_all(packed, "ep", split_axis=0, concat_axis=0, tiled=True)
     gathered = lax.all_gather(landed, "my", axis=3, tiled=True)
+    expert_table = (
+        np.arange(ep_count)[:, None] * slot_dev + np.arange(slot_dev)[None, :]
+    ) // replicas
+
+    def fetch(weight, after):
+        chosen_rows, _ = lax.optimization_barrier((weight[expert_table], after))
+        got = lax.all_to_all(chosen_rows, "ep", split_axis=0, concat_axis=0, tiled=True)
+        wide = lax.all_gather(got, "mx", axis=3, tiled=True)
+        return got, jnp.transpose(wide, (1, 0, 2, 3)).reshape(slot_dev, ep_count * piece_units, D)
+
+    raw_gate, w_gate = fetch(gate_weight, landed)
+    raw_up, w_up = fetch(up_weight, raw_gate)
+    _, w_down = fetch(down_weight, raw_up)
     tokens_in = jnp.transpose(gathered, (1, 0, 2, 3)).reshape(slot_dev, slot_rows, D)
 
     gate_proj = jnp.einsum("srd,sfd->srf", tokens_in, w_gate, preferred_element_type=jnp.float32)

time: 398 us -> 422 us (1.060)
  waiting for transfers between devices: 134 us -> 144 us
  starting transfers between devices: 11.3 us -> 21.1 us
    all_gather x1, waiting for transfers between devices: 23.3 us -> 0.01 us  [shards(): gathered = lax.all_gather(landed, 'my', axis=3, tiled=True)]
    all_gather x1 -> x3, waiting for transfers between devices: 53.7 us -> 74.6 us  [fetch(): wide = lax.all_gather(got, 'mx', axis=3, tiled=True)]
    all_to_all x0 -> x1, waiting for transfers between devices: none -> 12.5 us  [shards(): lax.all_to_all(packed, 'ep', split_axis=0, concat_axis=0, tiled=True)]
    all_to_all x0 -> x1, starting transfers between devices: none -> 9.72 us  [shards(): lax.all_to_all(packed, 'ep', split_axis=0, concat_axis=0, tiled=True)]
    slice x2 -> x1, local copies, waits for them, and re-layouts: 6.82 us -> 0.21 us  [the longest x1 6.6 us: shards(): w_gate, w_up, w_down = (got[0], got[1], got[2])]
    gather x1 -> x3, local copies, waits for them, and re-layouts: 2.11 us -> 7.83 us  [fetch(): chosen_rows, _ = lax.optimization_barrier((weight[expert_table], after))]
    all_to_all x2 -> x3, blocking collectives: 138 us -> 142 us  [fetch(): lax.all_to_all(chosen_rows, 'ep', split_axis=0, concat_axis=0, tiled=True)]
    another operation x5 -> x4, local copies, waits for them, and re-layouts: 14.4 us -> 13.1 us
  transfers between devices with their start and end apart: 4 -> 7, of which waited for: 4 -> 5; matrix products, arithmetic and copies ran while one was open for 7% -> 6% of each run, Pallas kernels for 0% -> 0%
where the time goes in v2:
time: 422 us; the launch traced here: 419 us
  blocking collectives  182 us (43%)
  waiting for transfers between devices  144 us (34%)
  local copies, waits for them, and re-layouts  31.9 us (8%)
  starting transfers between devices  21.1 us (5%)
  matrix products  20.7 us (5%)
  between operations  14.1 us (3%)
  other arithmetic  4.43 us (1%)
    all_to_all x3, blocking collectives, fetch(): lax.all_to_all(chosen_rows, 'ep', split_axis=0, concat_axis=0, tiled=True)  142 us
    all_gather x3, waiting for transfers between devices, fetch(): wide = lax.all_gather(got, 'mx', axis=3, tiled=True)  74.6 us
    reduce_scatter x1, waiting for transfers between devices, shards(): lax.psum_scatter(expert_out.astype(jnp.bfloat16), 'my', scatter_dimension...  42 us
    psum x2, blocking collectives, row_scale(): row_total = lax.psum(partial_sq, 'my')  40.7 us
    all_to_all x1, waiting for transfers between devices, shards(): lax.all_to_all(sent_back, 'ep', split_axis=0, concat_axis=0, tiled=True)  14.5 us
    another operation x4, local copies, waits for them, and re-layouts  13.1 us
    all_to_all x1, waiting for transfers between devices, shards(): lax.all_to_all(packed, 'ep', split_axis=0, concat_axis=0, tiled=True)  12.5 us
    dot_general x1, matrix products, shards(): jnp.einsum('srf,sfd->srd', hidden, w_down, preferred_element_type=jnp.flo...  12.4 us
  transfers between devices with their start and end apart: 7, of which 5 were waited for; matrix products, arithmetic and copies ran while one was open for 6% of the time, Pallas kernels for 0%

profile of v2, /device:TPU:1, one launch (start us, length us, event | category | flops | bytes accessed | tf_op | source)
XLA Modules:
  0.0 419.1 jit_solution(16044243208929844896)
XLA Ops:
  7.2 0.0 copy-start
  7.2 0.0 copy-start.6
  7.2 0.9 copy.26
  8.1 0.1 eq.31
  8.2 0.1 eq.27
  8.4 0.7 broadcast_multiply_fusion
  9.1 1.1 reduce-window.6
  10.2 0.2 slice_reduce_fusion
  10.5 0.1 copy.25
  10.6 0.1 mul.97
  10.8 0.1 fusion.4
  10.9 2.4 scatter_custom_fusion
  13.4 0.0 copy-done
  13.4 1.7 multiply_reduce_fusion.2
  15.1 0.0 copy-start.8
  15.1 0.0 copy-start.1
  15.2 18.8 %psum.14 = f32[256]{0:T(256)S(1)} all-reduce(f32[256]{0:T(256)S(1)} %get-tuple-element.10), channel_id=1, replica_groups=mesh['ep'=16,'mx'=4,'my'=8] {'my'}, use_global_device_ids=true, to_apply=%region_2.0 | all-reduce | flops 256 | bytes 2048 | tf_op jit(solution)/shard_map/psum | solution.py:18
  34.0 0.1 multiply_convert_fusion.2
  34.1 3.3 gather_fusion
  37.4 9.7 %all-to-all-start = ((bf16[16,1,48,256]{3,2,1,0:T(8,128)(2,1)}), bf16[16,1,48,256]{3,2,1,0:T(8,128)(2,1)S(1)}, u32[]{:S(2)}, u32[]{:S(2)}) async-start(bf16[16,1,48,256]{3,2,1,0:T(8,128)(2,1)} %bitcast.5), calls=%async_computation | async-start | bytes 786432 | tf_op jit(solution)/shard_map/all_to_all | solution.py:58
  47.1 0.0 all-gather.7.cloned.1.call-start
  47.2 2.6 gather_fusion.1
  49.8 0.0 copy-start.2
  49.8 12.5 %all-to-all-done = bf16[16,1,48,256]{3,2,1,0:T(8,128)(2,1)S(1)} async-done(((bf16[16,1,48,256]{3,2,1,0:T(8,128)(2,1)}), bf16[16,1,48,256]{3,2,1,0:T(8,128)(2,1)S(1)}, u32[]{:S(2)}, u32[]{:S(2)}) %all-to-all-start) | async-done | bytes 393248 | tf_op jit(solution)/shard_map/all_to_all | solution.py:58
  62.3 0.4 copy.29
  62.8 48.4 %all_to_all.25 = bf16[16,1,44,512]{3,2,1,0:T(8,128)(2,1)} all-to-all(bf16[16,1,44,512]{3,2,1,0:T(8,128)(2,1)S(1)} %copy.29), channel_id=1, replica_groups=mesh['ep'=16,'mx'=4,'my'=8] {'ep'}, dimensions={0} | all-to-all | bytes 1441792 | tf_op jit(solution)/shard_map/all_to_all | solution.py:66
  111.2 0.0 all-gather.7.cloned.1.call-update
  111.2 0.0 all-gather.5.cloned.1.call-start
  111.3 0.0 copy-done.4
  111.3 0.7 all-gather.5.cloned.1.call-update
  112.0 0.0 all-gather.9.cloned.1.call-start
  112.0 2.6 gather_fusion.2
  114.6 0.0 copy-start.3
  114.7 0.4 copy.30
  115.1 46.1 %all_to_all.26 = bf16[16,1,44,512]{3,2,1,0:T(8,128)(2,1)} all-to-all(bf16[16,1,44,512]{3,2,1,0:T(8,128)(2,1)S(1)} %copy.30), channel_id=1, replica_groups=mesh['ep'=16,'mx'=4,'my'=8] {'ep'}, dimensions={0} | all-to-all | bytes 1441792 | tf_op jit(solution)/shard_map/all_to_all | solution.py:66
  161.2 0.0 all-gather.9.cloned.1.call-update
  161.2 0.2 all-gather.11.cloned.1.call-start
  161.4 2.6 gather_fusion.3
  164.1 0.4 copy.31
  164.5 47.2 %all_to_all.27 = bf16[16,1,44,512]{3,2,1,0:T(8,128)(2,1)} all-to-all(bf16[16,1,44,512]{3,2,1,0:T(8,128)(2,1)S(1)} %copy.31), channel_id=1, replica_groups=mesh['ep'=16,'mx'=4,'my'=8] {'ep'}, dimensions={0} | all-to-all | bytes 1441792 | tf_op jit(solution)/shard_map/all_to_all | solution.py:66
  211.7 0.0 all-gather.11.cloned.1.call-update
  211.7 0.0 reduce-scatter.2.cloned.1.call-start
  211.8 0.0 all-gather.7.cloned.1.call-done
  211.8 4.4 %reshape.169 = bf16[704,2048]{1,0:T(8,128)(2,1)} reshape(bf16[16,1,44,2048]{3,2,1,0:T(8,128)(2,1)} %all-gather.7.cloned.1.call-done) | data formatting | bytes 5767168 | tf_op jit(solution)/shard_map/reshape.8
  216.2 6.5 %fusion.14 = f32[768,704]{0,1:T(8,128)} fusion(bf16[768,2048]{1,0:T(8,128)(2,1)} %bitcast.38, bf16[704,2048]{1,0:T(8,128)(2,1)} %reshape.169), kind=kOutput, calls=%fused_computation.50 | convolution fusion | flops 2214592512 | bytes 8192000 | tf_op jit(solution)/shard_map/srd,sfd->srf/dot_general | solution.py:75
  222.7 29.5 %all-gather.9.cloned.1.call-done = bf16[16,1,44,2048]{3,2,1,0:T(8,128)(2,1)} async-done(((bf16[16,1,44,512]{3,2,1,0:T(8,128)(2,1)}), bf16[16,1,44,2048]{3,2,1,0:T(8,128)(2,1)}) %all-gather.9.cloned.1.call-update) | async-done | bytes 2883600 | tf_op jit(solution)/shard_map/all_gather | solution.py:67
  252.2 4.3 %reshape.170 = bf16[704,2048]{1,0:T(8,128)(2,1)} reshape(bf16[16,1,44,2048]{3,2,1,0:T(8,128)(2,1)} %all-gather.9.cloned.1.call-done) | data formatting | bytes 5767168 | tf_op jit(solution)/shard_map/reshape.15
  256.5 45.1 %all-gather.11.cloned.1.call-done = bf16[16,1,44,2048]{3,2,1,0:T(8,128)(2,1)} async-done(((bf16[16,1,44,512]{3,2,1,0:T(8,128)(2,1)}), bf16[16,1,44,2048]{3,2,1,0:T(8,128)(2,1)}) %all-gather.11.cloned.1.call-update) | async-done | bytes 2883600 | tf_op jit(solution)/shard_map/all_gather | solution.py:67
  301.6 4.4 %reshape.171 = bf16[704,2048]{1,0:T(8,128)(2,1)} reshape(bf16[16,1,44,2048]{3,2,1,0:T(8,128)(2,1)} %all-gather.11.cloned.1.call-done) | data formatting | bytes 5767168 | tf_op jit(solution)/shard_map/reshape.18
  306.0 12.4 %fusion = bf16[1,768,2048]{2,1,0:T(8,128)(2,1)} fusion(bf16[704,2048]{1,0:T(8,128)(2,1)} %reshape.171, f32[768,704]{0,1:T(8,128)} %fusion.14, bf16[768,2048]{1,0:T(8,128)(2,1)} %bitcast.39, bf16[704,2048]{1,0:T(8,128)(2,1)} %reshape.170), kind=kOutput, calls=%fused_computation.7 | convolution fusion | flops 4434001920 | bytes 14221312 | tf_op jit(solution)/shard_map/srf,sfd->srd/dot_general | solution.py:78
  318.4 0.0 reduce-scatter.2.cloned.1.call-update
  318.5 42.0 %reduce-scatter.2.cloned.1.call-done = bf16[1,768,256]{2,1,0:T(8,128)(2,1)} async-done(((bf16[1,768,2048]{2,1,0:T(8,128)(2,1)}), bf16[1,768,256]{2,1,0:T(8,128)(2,1)}) %reduce-scatter.2.cloned.1.call-update) | async-done | bytes 393232 | tf_op jit(solution)/shard_map/reduce_scatter | solution.py:79
  360.5 11.0 %all-to-all-start.4 = ((bf16[16,1,48,256]{3,2,1,0:T(8,128)(2,1)}), bf16[16,1,48,256]{3,2,1,0:T(8,128)(2,1)S(1)}, u32[]{:S(2)}, u32[]{:S(2)}) async-start(bf16[16,1,48,256]{3,2,1,0:T(8,128)(2,1)} %bitcast.34), calls=%async_computation.5 | async-start | bytes 786432 | tf_op jit(solution)/shard_map/all_to_all | solution.py:84
  371.5 0.0 copy-done.5
  371.5 0.0 copy-start.7
  371.5 0.1 copy.24
  371.7 14.5 %all-to-all-done.4 = bf16[16,1,48,256]{3,2,1,0:T(8,128)(2,1)S(1)} async-done(((bf16[16,1,48,256]{3,2,1,0:T(8,128)(2,1)}), bf16[16,1,48,256]{3,2,1,0:T(8,128)(2,1)S(1)}, u32[]{:S(2)}, u32[]{:S(2)}) %all-to-all-start.4) | async-done | bytes 393248 | tf_op jit(solution)/shard_map/all_to_all | solution.py:84
  386.2 1.9 gather_fusion.4
  388.2 0.3 reshape.173
  388.4 0.7 multiply_reduce_fusion
  389.1 0.7 fusion.13
  389.8 0.1 multiply_reduce_fusion.1
  389.9 21.9 %psum.15 = f32[256]{0:T(256)S(1)} all-reduce(f32[256]{0:T(256)S(1)} %multiply_reduce_fusion.1), channel_id=1, replica_groups=mesh['ep'=16,'mx'=4,'my'=8] {'my'}, use_global_device_ids=true, to_apply=%region_10.11 | all-reduce | flops 256 | bytes 2048 | tf_op jit(solution)/shard_map/psum | solution.py:18
  411.8 0.8 multiply_convert_fusion.1
  (23 shorter events, 0.2 us)
Async XLA Ops:
  7.2 6.2 %copy-start = (bf16[256,2048]{1,0:T(8,128)(2,1)S(1)}, bf16[256,2048]{1,0:T(8,128)(2,1)}, u32[]{:S(2)}) copy-start(bf16[256,2048]{1,0:T(8,128)(2,1)} %param.14) | copy-start | bytes 3145732
  7.2 26.8 %copy-start.6 = (f32[256]{0:T(256)S(1)}, f32[256]{0:T(256)}, u32[]{:S(2)}) copy-start(f32[256]{0:T(256)} %param.17) | copy-start | bytes 3076
  15.1 32.0 %copy-start.8 = (s32[16]{0:T(128)S(1)}, s32[16]{0:T(128)}, u32[]{:S(2)}) copy-start(s32[16]{0:T(128)} %constant.78) | copy-start | bytes 196
  15.1 32.0 %copy-start.1 = (bf16[8,44,512]{2,0,1:T(8,128)(2,1)S(1)}, bf16[8,44,512]{2,0,1:T(8,128)(2,1)}, u32[]{:S(2)}) copy-start(bf16[8,44,512]{2,0,1:T(8,128)(2,1)} %param.18) | copy-start | bytes 1081348
  37.4 25.0 %all-to-all-start = ((bf16[16,1,48,256]{3,2,1,0:T(8,128)(2,1)}), bf16[16,1,48,256]{3,2,1,0:T(8,128)(2,1)S(1)}, u32[]{:S(2)}, u32[]{:S(2)}) async-start(bf16[16,1,48,256]{3,2,1,0:T(8,128)(2,1)} %bitcast.5), calls=%async_computation | async-start | bytes 786432 | tf_op jit(solution)/shard_map/all_to_all | solution.py:58
  47.1 164.7 %all-gather.7.cloned.1.call-start = ((), (), s32[]{:S(2)}) async-start(), calls=%async_computation.7 | async-start | bytes 3932160 | tf_op jit(solution)/shard_map/all_gather | solution.py:67
  49.8 62.2 %copy-start.2 = (bf16[8,44,512]{2,0,1:T(8,128)(2,1)S(1)}, bf16[8,44,512]{2,0,1:T(8,128)(2,1)}, u32[]{:S(2)}) copy-start(bf16[8,44,512]{2,0,1:T(8,128)(2,1)} %param.19) | copy-start | bytes 1081348
  62.3 48.9 %copy-start.4 = (bf16[16,1,48,256]{3,2,1,0:T(8,128)(2,1)}, bf16[16,1,48,256]{3,2,1,0:T(8,128)(2,1)S(1)}, u32[]{:S(2)}) copy-start(bf16[16,1,48,256]{3,2,1,0:T(8,128)(2,1)S(1)} %all-to-all-done) | copy-start | bytes 1179652
  111.2 105.0 %all-gather.5.cloned.1.call-start = ((), (), s32[]{:S(2)}) async-start(), calls=%async_computation.6 | async-start | bytes 3538944 | tf_op jit(solution)/shard_map/all_gather | solution.py:59
  112.0 140.2 %all-gather.9.cloned.1.call-start = ((), (), s32[]{:S(2)}) async-start(), calls=%async_computation.8 | async-start | bytes 3932160 | tf_op jit(solution)/shard_map/all_gather | solution.py:67
  114.6 46.8 %copy-start.3 = (bf16[8,44,512]{2,0,1:T(8,128)(2,1)S(1)}, bf16[8,44,512]{2,0,1:T(8,128)(2,1)}, u32[]{:S(2)}) copy-start(bf16[8,44,512]{2,0,1:T(8,128)(2,1)} %param.20) | copy-start | bytes 1081348
  161.2 140.4 %all-gather.11.cloned.1.call-start = ((), (), s32[]{:S(2)}) async-start(), calls=%async_computation.9 | async-start | bytes 3932160 | tf_op jit(solution)/shard_map/all_gather | solution.py:67
  211.7 148.7 %reduce-scatter.2.cloned.1.call-start = ((), (), s32[]{:S(2)}) async-start(), calls=%async_computation.10 | async-start | bytes 3538944 | tf_op jit(solution)/shard_map/reduce_scatter | solution.py:79
  318.4 53.0 %copy-start.5 = (f32[256,2]{0,1:T(2,128)S(1)}, f32[256,2]{0,1:T(2,128)}, u32[]{:S(2)}) copy-start(f32[256,2]{0,1:T(2,128)} %param.22) | copy-start | bytes 6148
  360.5 25.8 %all-to-all-start.4 = ((bf16[16,1,48,256]{3,2,1,0:T(8,128)(2,1)}), bf16[16,1,48,256]{3,2,1,0:T(8,128)(2,1)S(1)}, u32[]{:S(2)}, u32[]{:S(2)}) async-start(bf16[16,1,48,256]{3,2,1,0:T(8,128)(2,1)} %bitcast.34), calls=%async_computation.5 | async-start | bytes 786432 | tf_op jit(solution)/shard_map/all_to_all | solution.py:84
  371.5 40.3 %copy-start.7 = (f32[256]{0:T(256)S(1)}, f32[256]{0:T(256)}, u32[]{:S(2)}) copy-start(f32[256]{0:T(256)} %param.23) | copy-start | bytes 3076
Sparse Core Ops, SparseCore 0:
  111.3 48.6 all-gather.6
  162.1 40.0 all-gather.4
  204.4 47.7 all-gather.8
  254.1 47.4 all-gather.10
  318.6 41.8 reduce-scatter.1

commit v3 on v1

--- a/solution.py
+++ b/solution.py
@@ -1,7 +1,11 @@
+import functools
+
 import jax
 import jax.numpy as jnp
 import numpy as np
 from jax import lax
+from jax.experimental import pallas as pl
+from jax.experimental.pallas import tpu as pltpu
 from jax.sharding import PartitionSpec as P
 
 D = 2048
@@ -11,6 +15,77 @@
 
 
 EPSILON = 1e-06
+MESH = pl.DeviceIdType.MESH
+
+
+def move_kernel(n_ep, n_mx, w_ref, out_ref, send_z, recv_z, send_x, recv_x, local_sem):
+    j = lax.axis_index("ep")
+    a = lax.axis_index("mx")
+    m = lax.axis_index("my")
+    pending = []
+    for k in range(w_ref.shape[0]):
+        local = pltpu.make_async_copy(w_ref.at[k, j], out_ref.at[k, a, j], local_sem.at[k])
+        local.start()
+        along_z = []
+        for d in range(1, n_ep):
+            t = lax.rem(j + d, n_ep)
+            copy = pltpu.make_async_remote_copy(
+                src_ref=w_ref.at[k, t],
+                dst_ref=out_ref.at[k, a, j],
+                send_sem=send_z.at[k, d],
+                recv_sem=recv_z.at[k, d],
+                device_id=(t, a, m),
+                device_id_type=MESH,
+            )
+            copy.start()
+            along_z.append(copy)
+        local.wait()
+        for copy in along_z:
+            copy.wait_recv()
+        pending.extend(along_z)
+        for e in range(1, n_mx):
+            b = lax.rem(a + e, n_mx)
+            copy = pltpu.make_async_remote_copy(
+                src_ref=out_ref.at[k, a],
+                dst_ref=out_ref.at[k, a],
+                send_sem=send_x.at[k, e],
+                recv_sem=recv_x.at[k, e],
+                device_id=(j, b, m),
+                device_id_type=MESH,
+            )
+            copy.start()
+            pending.append(copy)
+    for copy in pending:
+        copy.wait_send()
+    for k in range(w_ref.shape[0]):
+        for e in range(1, n_mx):
+            b = lax.rem(a + e, n_mx)
+            pltpu.make_async_remote_copy(
+                src_ref=out_ref.at[k, a],
+                dst_ref=out_ref.at[k, a],
+                send_sem=send_x.at[k, e],
+                recv_sem=recv_x.at[k, e],
+                device_id=(j, b, m),
+                device_id_type=MESH,
+            ).wait_recv()
+
+
+def move_weights(stacked, n_ep, n_mx):
+    count, _, units, wb = stacked.shape
+    return pl.pallas_call(
+        functools.partial(move_kernel, n_ep, n_mx),
+        out_shape=jax.ShapeDtypeStruct((count, n_mx, n_ep, units, wb), stacked.dtype),
+        in_specs=[pl.BlockSpec(memory_space=pl.ANY)],
+        out_specs=pl.BlockSpec(memory_space=pl.ANY),
+        scratch_shapes=[
+            pltpu.SemaphoreType.DMA((count, n_ep)),
+            pltpu.SemaphoreType.DMA((count, n_ep)),
+            pltpu.SemaphoreType.DMA((count, n_mx)),
+            pltpu.SemaphoreType.DMA((count, n_mx)),
+            pltpu.SemaphoreType.DMA((count,)),
+        ],
+        compiler_params=pltpu.CompilerParams(has_side_effects=True),
+    )(stacked)
 
 
 def row_scale(stream_f):
@@ -41,16 +116,6 @@
     piece_units = gate_weight.shape[1]
     slot_rows = ep_count * capacity
 
-    expert_table = (
-        np.arange(ep_count)[:, None] * slot_dev + np.arange(slot_dev)[None, :]
-    ) // replicas
-    stacked = jnp.stack([gate_weight, up_weight, down_weight], axis=0)
-    chosen_rows = stacked[:, expert_table]
-    got = lax.all_to_all(chosen_rows, "ep", split_axis=1, concat_axis=1, tiled=True)
-    got = lax.all_gather(got, "mx", axis=4, tiled=True)
-    got = jnp.transpose(got, (0, 2, 1, 3, 4)).reshape(3, slot_dev, ep_count * piece_units, D)
-    w_gate, w_up, w_down = got[0], got[1], got[2]
-
     projected = jnp.dot(context, out_weight, preferred_element_type=jnp.float32)
     stream = (projected + resid_in.astype(jnp.float32)).astype(jnp.bfloat16)
     stream_f = stream.astype(jnp.float32)
@@ -67,12 +132,18 @@
     packed = padded[source].reshape(ep_count, slot_dev, capacity, feat_block)
     landed = lax.all_to_all(packed, "ep", split_axis=0, concat_axis=0, tiled=True)
     gathered = lax.all_gather(landed, "my", axis=3, tiled=True)
+    expert_of_slot = np.arange(ep_count) // replicas
+    stacked = jnp.stack([gate_weight, up_weight, down_weight], axis=0)[:, expert_of_slot]
+    moved = move_weights(stacked, ep_count, lax.axis_size("mx"))
+    w_gate, w_up, w_down = moved[0], moved[1], moved[2]
     tokens_in = jnp.transpose(gathered, (1, 0, 2, 3)).reshape(slot_dev, slot_rows, D)
 
-    gate_proj = jnp.einsum("srd,sfd->srf", tokens_in, w_gate, preferred_element_type=jnp.float32)
-    up_proj = jnp.einsum("srd,sfd->srf", tokens_in, w_up, preferred_element_type=jnp.float32)
+    split_rows = tokens_in.reshape(slot_rows, w_gate.shape[0], w_gate.shape[3])
+    gate_proj = jnp.einsum("rac,aspc->rsp", split_rows, w_gate, preferred_element_type=jnp.float32)
+    up_proj = jnp.einsum("rac,aspc->rsp", split_rows, w_up, preferred_element_type=jnp.float32)
     hidden = (jax.nn.silu(gate_proj) * up_proj).astype(jnp.bfloat16)
-    expert_out = jnp.einsum("srf,sfd->srd", hidden, w_down, preferred_element_type=jnp.float32)
+    expert_out = jnp.einsum("rsp,aspc->rac", hidden, w_down, preferred_element_type=jnp.float32)
+    expert_out = expert_out.reshape(slot_dev, slot_rows, D)
     summed = lax.psum_scatter(
         expert_out.astype(jnp.bfloat16), "my", scatter_dimension=2, tiled=True
     )

time: 398 us -> 384 us (0.965)
  Pallas kernels: 0 us -> 173 us
  blocking collectives: 179 us -> 65.5 us
  waiting for transfers between devices: 134 us -> 53.8 us
  matrix products: 19.5 us -> 24.6 us
    pallas_call x0 -> x1, Pallas kernels: none -> 173 us  [move_weights(): pl.pallas_call(functools.partial(move_kernel, n_ep, n_mx), out_shape=jax....]
    all_to_all x1 -> x0, blocking collectives: 118 us -> none  [shards(): lax.all_to_all(chosen_rows, 'ep', split_axis=1, concat_axis=1, tiled=True)]
    all_gather x1 -> x0, waiting for transfers between devices: 53.7 us -> none  [shards(): got = lax.all_gather(got, 'mx', axis=4, tiled=True)]
    all_gather x1, waiting for transfers between devices: 23.3 us -> 0.01 us  [shards(): gathered = lax.all_gather(landed, 'my', axis=3, tiled=True)]
    dot_general x0 -> x3, local copies, waits for them, and re-layouts: none -> 12.8 us  [shards(): jnp.einsum('rsp,aspc->rac', hidden, w_down, preferred_element_type=jnp.fl...]
    another operation x5 -> x3, local copies, waits for them, and re-layouts: 14.4 us -> 6.39 us  [the longest x1 6.17 us: shards(): split_rows = tokens_in.reshape(slot_rows, w_gate.shape[0], w_gate.shape[3])]
    slice x2 -> x1, local copies, waits for them, and re-layouts: 6.82 us -> 0.21 us  [the longest x1 6.6 us: shards(): w_gate, w_up, w_down = (got[0], got[1], got[2])]
    all_to_all x1, blocking collectives: 19.7 us -> 24.9 us  [shards(): lax.all_to_all(packed, 'ep', split_axis=0, concat_axis=0, tiled=True)]
  transfers between devices with their start and end apart: 4 -> 3, of which waited for: 4 -> 2; matrix products, arithmetic and copies ran while one was open for 7% -> 5% of each run, Pallas kernels for 0% -> 45%
where the time goes in v3:
time: 384 us; the launch traced here: 381 us
  Pallas kernels  173 us (45%)
  blocking collectives  65.5 us (17%)
  waiting for transfers between devices  53.8 us (14%)
  local copies, waits for them, and re-layouts  33.9 us (9%)
  matrix products  24.6 us (6%)
  between operations  14.3 us (4%)
  starting transfers between devices  11.1 us (3%)
  other arithmetic  4.57 us (1%)
    pallas_call x1, Pallas kernels, move_weights(): pl.pallas_call(functools.partial(move_kernel, n_ep, n_mx), out_shape=jax....  173 us
    psum x2, blocking collectives, row_scale(): row_total = lax.psum(partial_sq, 'my')  40.7 us
    reduce_scatter x1, waiting for transfers between devices, shards(): lax.psum_scatter(expert_out.astype(jnp.bfloat16), 'my', scatter_dimension...  39.2 us
    all_to_all x1, blocking collectives, shards(): lax.all_to_all(packed, 'ep', split_axis=0, concat_axis=0, tiled=True)  24.9 us
    dot_general x1, matrix products, shards(): jnp.einsum('rsp,aspc->rac', hidden, w_down, preferred_element_type=jnp.fl...  15.9 us
    all_to_all x1, waiting for transfers between devices, shards(): lax.all_to_all(sent_back, 'ep', split_axis=0, concat_axis=0, tiled=True)  14.5 us
    dot_general x3, local copies, waits for them, and re-layouts, shards(): jnp.einsum('rsp,aspc->rac', hidden, w_down, preferred_element_type=jnp.fl...  12.8 us
    all_to_all x1, starting transfers between devices, shards(): lax.all_to_all(sent_back, 'ep', split_axis=0, concat_axis=0, tiled=True)  11 us
  transfers between devices with their start and end apart: 3, of which 2 were waited for; matrix products, arithmetic and copies ran while one was open for 5% of the time, Pallas kernels for 45%

profile of v3, /device:TPU:1, one launch (start us, length us, event | category | flops | bytes accessed | tf_op | source)
XLA Modules:
  0.0 381.0 jit_solution(15575224579803820796)
XLA Ops:
  7.2 0.0 copy-start
  7.2 0.0 copy-start.5
  7.2 0.0 all-gather.2.cloned.1.call-start
  7.2 0.9 copy.30
  8.1 0.1 eq.31
  8.3 0.1 eq.27
  8.4 0.7 broadcast_multiply_fusion
  9.1 1.1 reduce-window.6
  10.3 0.2 slice_reduce_fusion
  10.5 0.1 copy.29
  10.7 0.1 mul.95
  10.8 0.1 fusion.27
  10.9 2.4 scatter_custom_fusion
  13.4 0.0 copy-done
  13.4 1.7 multiply_reduce_fusion.2
  15.2 0.0 copy-start.1
  15.2 0.0 copy-start.7
  15.2 0.0 copy-start.2
  15.2 0.0 copy-start.3
  15.2 18.8 %psum.14 = f32[256]{0:T(256)S(1)} all-reduce(f32[256]{0:T(256)S(1)} %get-tuple-element.4), channel_id=1, replica_groups=mesh['ep'=16,'mx'=4,'my'=8] {'my'}, use_global_device_ids=true, to_apply=%region_2.0 | all-reduce | flops 256 | bytes 2048 | tf_op jit(solution)/shard_map/psum | solution.py:93
  34.0 0.0 copy-done.5
  34.0 0.1 multiply_convert_fusion.1
  34.1 2.7 gather_fusion
  36.8 24.9 %all_to_all.10 = bf16[16,1,48,256]{3,2,1,0:T(8,128)(2,1)} all-to-all(bf16[16,1,48,256]{3,2,1,0:T(8,128)(2,1)S(1)} %bitcast.97), channel_id=1, replica_groups=mesh['ep'=16,'mx'=4,'my'=8] {'ep'}, dimensions={0} | all-to-all | bytes 786432 | tf_op jit(solution)/shard_map/all_to_all | solution.py:133
  61.7 0.0 all-gather.2.cloned.1.call-update
  61.7 0.0 reduce-scatter.2.cloned.1.call-start
  61.8 0.0 copy-done.1
  61.8 0.1 copy.65
  61.9 0.0 copy-done.7
  61.9 0.0 copy-done.2
  61.9 0.0 copy-done.3
  61.9 0.2 copy_bitcast_fusion.1
  62.2 0.1 pad_maximum_fusion
  62.3 2.1 gather_fusion.1
  64.4 3.3 copy.64
  67.7 173.2 %shard_map.131 = bf16[3,4,16,44,512]{4,3,2,1,0:T(8,128)(2,1)} custom-call(bf16[3,16,44,512]{3,2,1,0:T(8,128)(2,1)} %bitcast.95), custom_call_target="tpu_custom_call" | custom-call | tf_op jit(solution)/shard_map/pallas_call | solution.py:75
  240.9 2.2 slice_bitcast_fusion
  243.1 4.0 %copy.46 = bf16[4,512,44,16]{1,0,2,3:T(4,128)(2,1)} copy(bf16[4,512,44,16]{1,2,3,0:T(8,128)(2,1)S(1)} %slice_bitcast_fusion) | data formatting | bytes 5767168 | tf_op jit(solution)/shard_map/rsp,aspc->rac/dot_general | solution.py:145
  247.1 6.7 %reshape.181 = bf16[2048,44,16]{0,1,2:T(8,128)(2,1)} reshape(bf16[4,512,44,16]{1,0,2,3:T(4,128)(2,1)} %copy.46) | data formatting | bytes 5767168 | tf_op jit(solution)/shard_map/rsp,aspc->rac/dot_general | solution.py:145
  253.7 0.0 all-gather.2.cloned.1.call-done
  253.7 6.2 %reshape_reshape_transpose.3 = bf16[768,4,512]{2,1,0:T(4,128)(2,1)} reshape(bf16[16,1,48,2048]{3,2,1,0:T(8,128)(2,1)} %all-gather.2.cloned.1.call-done) | data formatting | bytes 6291456 | tf_op jit(solution)/shard_map/reshape;reshape;transpose | solution.py:141
  259.9 6.9 %fusion.2 = f32[768,16,44,1]{0,2,1,3:T(8,128)} fusion(bf16[3,4,16,44,512]{4,3,2,1,0:T(8,128)(2,1)} %shard_map.131, bf16[768,4,512]{2,1,0:T(4,128)(2,1)} %reshape_reshape_transpose.3), kind=kOutput, calls=%fused_computation.7 | convolution fusion | flops 2214592512 | bytes 8454144 | tf_op jit(solution)/shard_map/rac,aspc->rsp/dot_general | solution.py:142
  266.8 15.9 %fusion.8 = bf16[1,768,2048]{2,1,0:T(8,128)(2,1)} fusion(bf16[2048,44,16]{0,1,2:T(8,128)(2,1)} %reshape.181, f32[768,16,44,1]{0,2,1,3:T(8,128)} %fusion.2, bf16[3,4,16,44,512]{4,3,2,1,0:T(8,128)(2,1)} %shard_map.131, bf16[768,4,512]{2,1,0:T(4,128)(2,1)} %reshape_reshape_transpose.3), kind=kOutput, calls=%fused_computation.14 | convolution fusion | flops 4434001920 | bytes 14942208 | tf_op jit(solution)/shard_map/rsp,aspc->rac/dot_general | solution.py:145
  282.7 0.0 copy-start.4
  282.7 0.0 reduce-scatter.2.cloned.1.call-update
  282.8 0.0 copy-start.6
  282.8 39.2 %reduce-scatter.2.cloned.1.call-done = bf16[1,768,256]{2,1,0:T(8,128)(2,1)} async-done(((bf16[1,768,2048]{2,1,0:T(8,128)(2,1)}), bf16[1,768,256]{2,1,0:T(8,128)(2,1)}) %reduce-scatter.2.cloned.1.call-update) | async-done | bytes 393232 | tf_op jit(solution)/shard_map/reduce_scatter | solution.py:147
  322.0 11.0 %all-to-all-start.1 = ((bf16[16,1,48,256]{3,2,1,0:T(8,128)(2,1)}), bf16[16,1,48,256]{3,2,1,0:T(8,128)(2,1)S(1)}, u32[]{:S(2)}, u32[]{:S(2)}) async-start(bf16[16,1,48,256]{3,2,1,0:T(8,128)(2,1)} %bitcast.98), calls=%async_computation.2 | async-start | bytes 786432 | tf_op jit(solution)/shard_map/all_to_all | solution.py:152
  333.0 0.0 copy-done.4
  333.0 0.1 copy.28
  333.2 14.5 %all-to-all-done.1 = bf16[16,1,48,256]{3,2,1,0:T(8,128)(2,1)S(1)} async-done(((bf16[16,1,48,256]{3,2,1,0:T(8,128)(2,1)}), bf16[16,1,48,256]{3,2,1,0:T(8,128)(2,1)S(1)}, u32[]{:S(2)}, u32[]{:S(2)}) %all-to-all-start.1) | async-done | bytes 393248 | tf_op jit(solution)/shard_map/all_to_all | solution.py:152
  347.7 1.9 gather_fusion.2
  349.7 0.3 reshape.142
  349.9 0.7 multiply_reduce_fusion
  350.7 0.7 fusion.36
  351.3 0.1 multiply_reduce_fusion.1
  351.5 21.9 %psum.15 = f32[256]{0:T(256)S(1)} all-reduce(f32[256]{0:T(256)S(1)} %multiply_reduce_fusion.1), channel_id=1, replica_groups=mesh['ep'=16,'mx'=4,'my'=8] {'my'}, use_global_device_ids=true, to_apply=%region_10.11 | all-reduce | flops 256 | bytes 2048 | tf_op jit(solution)/shard_map/psum | solution.py:93
  373.3 0.0 copy-done.6
  373.3 0.8 multiply_convert_fusion
  (14 shorter events, 0.2 us)
Async XLA Ops:
  7.2 6.3 %copy-start = (bf16[256,2048]{1,0:T(8,128)(2,1)S(1)}, bf16[256,2048]{1,0:T(8,128)(2,1)}, u32[]{:S(2)}) copy-start(bf16[256,2048]{1,0:T(8,128)(2,1)} %param.12) | copy-start | bytes 3145732
  7.2 26.8 %copy-start.5 = (f32[256]{0:T(256)S(1)}, f32[256]{0:T(256)}, u32[]{:S(2)}) copy-start(f32[256]{0:T(256)} %param.15) | copy-start | bytes 3076
  7.2 246.6 %all-gather.2.cloned.1.call-start = ((), (), s32[]{:S(2)}) async-start(), calls=%async_computation.3 | async-start | bytes 3538944 | tf_op jit(solution)/shard_map/all_gather | solution.py:134
  15.2 46.6 %copy-start.1 = (bf16[8,44,512]{2,0,1:T(8,128)(2,1)S(1)}, bf16[8,44,512]{2,0,1:T(8,128)(2,1)}, u32[]{:S(2)}) copy-start(bf16[8,44,512]{2,0,1:T(8,128)(2,1)} %param.16) | copy-start | bytes 1081348
  15.2 46.7 %copy-start.7 = (s32[16]{0:T(128)S(1)}, s32[16]{0:T(128)}, u32[]{:S(2)}) copy-start(s32[16]{0:T(128)} %constant.78) | copy-start | bytes 196
  15.2 46.7 %copy-start.2 = (bf16[8,44,512]{2,0,1:T(8,128)(2,1)S(1)}, bf16[8,44,512]{2,0,1:T(8,128)(2,1)}, u32[]{:S(2)}) copy-start(bf16[8,44,512]{2,0,1:T(8,128)(2,1)} %param.18) | copy-start | bytes 1081348
  15.2 46.7 %copy-start.3 = (bf16[8,44,512]{2,0,1:T(8,128)(2,1)S(1)}, bf16[8,44,512]{2,0,1:T(8,128)(2,1)}, u32[]{:S(2)}) copy-start(bf16[8,44,512]{2,0,1:T(8,128)(2,1)} %param.17) | copy-start | bytes 1081348
  61.7 260.2 %reduce-scatter.2.cloned.1.call-start = ((), (), s32[]{:S(2)}) async-start(), calls=%async_computation.4 | async-start | bytes 3538944 | tf_op jit(solution)/shard_map/reduce_scatter | solution.py:147
  282.7 50.3 %copy-start.4 = (f32[256,2]{0,1:T(2,128)S(1)}, f32[256,2]{0,1:T(2,128)}, u32[]{:S(2)}) copy-start(f32[256,2]{0,1:T(2,128)} %param.20) | copy-start | bytes 6148
  282.8 90.6 %copy-start.6 = (f32[256]{0:T(256)S(1)}, f32[256]{0:T(256)}, u32[]{:S(2)}) copy-start(f32[256]{0:T(256)} %param.21) | copy-start | bytes 3076
  322.0 25.8 %all-to-all-start.1 = ((bf16[16,1,48,256]{3,2,1,0:T(8,128)(2,1)}), bf16[16,1,48,256]{3,2,1,0:T(8,128)(2,1)S(1)}, u32[]{:S(2)}, u32[]{:S(2)}) async-start(bf16[16,1,48,256]{3,2,1,0:T(8,128)(2,1)} %bitcast.98), calls=%async_computation.2 | async-start | bytes 786432 | tf_op jit(solution)/shard_map/all_to_all | solution.py:152
Sparse Core Ops, SparseCore 0:
  61.8 42.8 all-gather.1
  282.9 39.0 reduce-scatter.1

commit v4 on v1

--- a/solution.py
+++ b/solution.py
@@ -1,7 +1,11 @@
+import functools
+
 import jax
 import jax.numpy as jnp
 import numpy as np
 from jax import lax
+from jax.experimental import pallas as pl
+from jax.experimental.pallas import tpu as pltpu
 from jax.sharding import PartitionSpec as P
 
 D = 2048
@@ -11,6 +15,103 @@
 
 
 EPSILON = 1e-06
+MESH = pl.DeviceIdType.MESH
+
+
+def remote(src, dst, send, recv, device):
+    return pltpu.make_async_remote_copy(
+        src_ref=src, dst_ref=dst, send_sem=send, recv_sem=recv,
+        device_id=device, device_id_type=MESH,
+    )
+
+
+def move_kernel(n_ep, n_mx, n_my, replicas, packed_ref, gate_ref, up_ref, down_ref,
+                tok_ref, out_ref, tok_sems, send_z, recv_z, send_x, recv_x, local_sem):
+    j = lax.axis_index("ep")
+    a = lax.axis_index("mx")
+    m = lax.axis_index("my")
+    fb = packed_ref.shape[2]
+    wb = gate_ref.shape[2]
+    cols_m = pl.ds(pl.multiple_of(m * fb, fb), fb)
+    cols_a = pl.ds(pl.multiple_of(a * wb, wb), wb)
+    pending = []
+    tok_local = pltpu.make_async_copy(packed_ref.at[j], tok_ref.at[j, :, cols_m], tok_sems.at[0, 0])
+    tok_local.start()
+    tok_z = []
+    for d in range(1, n_ep):
+        t = lax.rem(j + d, n_ep)
+        copy = remote(packed_ref.at[t], tok_ref.at[j, :, cols_m], tok_sems.at[1, d], tok_sems.at[2, d], (t, a, m))
+        copy.start()
+        tok_z.append(copy)
+    weights = (gate_ref, up_ref, down_ref)
+
+    def start_z(k):
+        local = pltpu.make_async_copy(
+            weights[k].at[j // replicas], out_ref.at[k, j, :, cols_a], local_sem.at[k])
+        local.start()
+        along_z = [local]
+        for d in range(1, n_ep):
+            t = lax.rem(j + d, n_ep)
+            copy = remote(weights[k].at[t // replicas], out_ref.at[k, j, :, cols_a],
+                          send_z.at[k, d], recv_z.at[k, d], (t, a, m))
+            copy.start()
+            along_z.append(copy)
+        return along_z
+
+    along_z = start_z(0)
+    tok_local.wait()
+    for copy in tok_z:
+        copy.wait_recv()
+    pending.extend(tok_z)
+    tok_my = []
+    for e in range(1, n_my):
+        b = lax.rem(m + e, n_my)
+        copy = remote(tok_ref.at[:, :, cols_m], tok_ref.at[:, :, cols_m], tok_sems.at[3, e], tok_sems.at[4, e], (j, a, b))
+        copy.start()
+        tok_my.append(copy)
+    pending.extend(tok_my)
+    x_copies = []
+    for k in range(3):
+        along_z[0].wait()
+        for copy in along_z[1:]:
+            copy.wait_recv()
+        pending.extend(along_z[1:])
+        if k + 1 < 3:
+            along_z = start_z(k + 1)
+        for e in range(1, n_mx):
+            b = lax.rem(a + e, n_mx)
+            copy = remote(out_ref.at[k, :, :, cols_a], out_ref.at[k, :, :, cols_a],
+                          send_x.at[k, e], recv_x.at[k, e], (j, b, m))
+            copy.start()
+            x_copies.append(copy)
+    pending.extend(x_copies)
+    for copy in pending:
+        copy.wait_send()
+    for copy in tok_my + x_copies:
+        copy.wait_recv()
+
+
+def move_all(packed, gate_weight, up_weight, down_weight, n_ep, n_mx, n_my, replicas):
+    _, rows, fb = packed.shape
+    _, units, wb = gate_weight.shape
+    return pl.pallas_call(
+        functools.partial(move_kernel, n_ep, n_mx, n_my, replicas),
+        out_shape=(
+            jax.ShapeDtypeStruct((n_ep, rows, n_my * fb), packed.dtype),
+            jax.ShapeDtypeStruct((3, n_ep, units, n_mx * wb), gate_weight.dtype),
+        ),
+        in_specs=[pl.BlockSpec(memory_space=pl.ANY)] * 4,
+        out_specs=(pl.BlockSpec(memory_space=pl.ANY), pl.BlockSpec(memory_space=pl.ANY)),
+        scratch_shapes=[
+            pltpu.SemaphoreType.DMA((5, max(n_ep, n_my))),
+            pltpu.SemaphoreType.DMA((3, n_ep)),
+            pltpu.SemaphoreType.DMA((3, n_ep)),
+            pltpu.SemaphoreType.DMA((3, n_mx)),
+            pltpu.SemaphoreType.DMA((3, n_mx)),
+            pltpu.SemaphoreType.DMA((3,)),
+        ],
+        compiler_params=pltpu.CompilerParams(has_side_effects=True),
+    )(packed, gate_weight, up_weight, down_weight)
 
 
 def row_scale(stream_f):
@@ -41,16 +142,6 @@
     piece_units = gate_weight.shape[1]
     slot_rows = ep_count * capacity
 
-    expert_table = (
-        np.arange(ep_count)[:, None] * slot_dev + np.arange(slot_dev)[None, :]
-    ) // replicas
-    stacked = jnp.stack([gate_weight, up_weight, down_weight], axis=0)
-    chosen_rows = stacked[:, expert_table]
-    got = lax.all_to_all(chosen_rows, "ep", split_axis=1, concat_axis=1, tiled=True)
-    got = lax.all_gather(got, "mx", axis=4, tiled=True)
-    got = jnp.transpose(got, (0, 2, 1, 3, 4)).reshape(3, slot_dev, ep_count * piece_units, D)
-    w_gate, w_up, w_down = got[0], got[1], got[2]
-
     projected = jnp.dot(context, out_weight, preferred_element_type=jnp.float32)
     stream = (projected + resid_in.astype(jnp.float32)).astype(jnp.bfloat16)
     stream_f = stream.astype(jnp.float32)
@@ -64,15 +155,19 @@
     row_ids = jnp.arange(tok_rows * TOPK, dtype=jnp.int32) // TOPK
     source = jnp.full((slot_total * capacity,), tok_rows, jnp.int32).at[target].set(row_ids)
     padded = jnp.concatenate([normed, jnp.zeros((1, feat_block), jnp.bfloat16)], axis=0)
-    packed = padded[source].reshape(ep_count, slot_dev, capacity, feat_block)
-    landed = lax.all_to_all(packed, "ep", split_axis=0, concat_axis=0, tiled=True)
-    gathered = lax.all_gather(landed, "my", axis=3, tiled=True)
-    tokens_in = jnp.transpose(gathered, (1, 0, 2, 3)).reshape(slot_dev, slot_rows, D)
-
-    gate_proj = jnp.einsum("srd,sfd->srf", tokens_in, w_gate, preferred_element_type=jnp.float32)
-    up_proj = jnp.einsum("srd,sfd->srf", tokens_in, w_up, preferred_element_type=jnp.float32)
+    packed = padded[source].reshape(ep_count, capacity, feat_block)
+    tok, moved = move_all(
+        packed, gate_weight, up_weight, down_weight,
+        ep_count, lax.axis_size("mx"), lax.axis_size("my"), replicas,
+    )
+    tokens_in = tok.reshape(slot_rows, D)
+    flat = moved.reshape(3, ep_count * piece_units, D)
+    w_gate, w_up, w_down = flat[0], flat[1], flat[2]
+    gate_proj = jnp.dot(tokens_in, w_gate.T, preferred_element_type=jnp.float32)
+    up_proj = jnp.dot(tokens_in, w_up.T, preferred_element_type=jnp.float32)
     hidden = (jax.nn.silu(gate_proj) * up_proj).astype(jnp.bfloat16)
-    expert_out = jnp.einsum("srf,sfd->srd", hidden, w_down, preferred_element_type=jnp.float32)
+    expert_out = jnp.dot(hidden, w_down, preferred_element_type=jnp.float32)
+    expert_out = expert_out.reshape(slot_dev, slot_rows, D)
     summed = lax.psum_scatter(
         expert_out.astype(jnp.bfloat16), "my", scatter_dimension=2, tiled=True
     )

time: 398 us -> 364 us (0.915)
  Pallas kernels: 0 us -> 186 us
  blocking collectives: 179 us -> 40.5 us
  waiting for transfers between devices: 134 us -> 53 us
    pallas_call x0 -> x1, Pallas kernels: none -> 186 us  [move_all(): pl.pallas_call(functools.partial(move_kernel, n_ep, n_mx, n_my, replicas)...]
    all_to_all x2 -> x0, blocking collectives: 138 us -> none  [the longest x1 118 us: shards(): lax.all_to_all(chosen_rows, 'ep', split_axis=1, concat_axis=1, tiled=True)]
    all_gather x2 -> x0, waiting for transfers between devices: 77 us -> none  [the longest x1 53.7 us: shards(): got = lax.all_gather(got, 'mx', axis=4, tiled=True)]
    another operation x5 -> x1, local copies, waits for them, and re-layouts: 14.4 us -> 0.01 us
    squeeze x0 -> x3, local copies, waits for them, and re-layouts: none -> 13.1 us  [shards(): w_gate, w_up, w_down = (flat[0], flat[1], flat[2])]
  transfers between devices with their start and end apart: 4 -> 2, of which waited for: 4 -> 2; matrix products, arithmetic and copies ran while one was open for 7% -> 0% of each run, Pallas kernels for 0% -> 0%
where the time goes in v4:
time: 364 us; the launch traced here: 362 us
  Pallas kernels  186 us (51%)
  waiting for transfers between devices  53 us (15%)
  blocking collectives  40.5 us (11%)
  local copies, waits for them, and re-layouts  32.2 us (9%)
  matrix products  20.7 us (6%)
  between operations  14.2 us (4%)
  starting transfers between devices  11.1 us (3%)
  other arithmetic  4.43 us (1%)
    pallas_call x1, Pallas kernels, move_all(): pl.pallas_call(functools.partial(move_kernel, n_ep, n_mx, n_my, replicas)...  186 us
    psum x2, blocking collectives, row_scale(): row_total = lax.psum(partial_sq, 'my')  40.5 us
    reduce_scatter x1, waiting for transfers between devices, shards(): lax.psum_scatter(expert_out.astype(jnp.bfloat16), 'my', scatter_dimension...  38.4 us
    all_to_all x1, waiting for transfers between devices, shards(): lax.all_to_all(sent_back, 'ep', split_axis=0, concat_axis=0, tiled=True)  14.5 us
    squeeze x3, local copies, waits for them, and re-layouts, shards(): w_gate, w_up, w_down = (flat[0], flat[1], flat[2])  13.1 us
    dot_general x1, matrix products, shards(): expert_out = jnp.dot(hidden, w_down, preferred_element_type=jnp.float32)  12.4 us
    all_to_all x1, starting transfers between devices, shards(): lax.all_to_all(sent_back, 'ep', split_axis=0, concat_axis=0, tiled=True)  11 us
  transfers between devices with their start and end apart: 2, of which 2 were waited for; matrix products, arithmetic and copies ran while one was open for 0% of the time, Pallas kernels for 0%

profile of v4, /device:TPU:1, one launch (start us, length us, event | category | flops | bytes accessed | tf_op | source)
XLA Modules:
  0.0 361.7 jit_solution(9106297754218393753)
XLA Ops:
  7.2 0.0 copy-start
  7.2 0.0 copy-start.1
  7.2 0.0 copy-start.2
  7.2 0.0 copy-start.3
  7.2 0.0 copy-start.5
  7.2 0.0 reduce-scatter.2.cloned.1.call-start
  7.3 0.9 copy.25
  8.2 0.1 eq.31
  8.4 0.1 eq.27
  8.5 0.7 broadcast_multiply_fusion
  9.2 1.1 reduce-window.6
  10.4 0.2 slice_reduce_fusion
  10.6 0.1 copy.24
  10.8 0.1 mul.95
  10.9 0.1 fusion.4
  11.0 2.4 scatter_custom_fusion
  13.5 0.0 copy-done
  13.5 1.7 multiply_reduce_fusion.2
  15.3 18.7 %psum.14 = f32[256]{0:T(256)S(1)} all-reduce(f32[256]{0:T(256)S(1)} %get-tuple-element.11), channel_id=1, replica_groups=mesh['ep'=16,'mx'=4,'my'=8] {'my'}, use_global_device_ids=true, to_apply=%region_2.0 | all-reduce | flops 256 | bytes 2048 | tf_op jit(solution)/shard_map/psum | solution.py:119
  33.9 0.0 copy-done.1
  33.9 0.9 copy.27.gate_ref
  34.8 0.0 copy-done.2
  34.8 0.9 copy.28.up_ref
  35.7 0.0 copy-done.3
  35.7 0.8 copy.29.down_ref
  36.5 0.0 copy-done.5
  36.5 0.1 multiply_convert_fusion.2
  36.7 3.3 gather_fusion
  39.9 185.6 %shard_map.113 = (bf16[16,48,2048]{2,1,0:T(8,128)(2,1)}, bf16[3,16,44,2048]{3,2,1,0:T(8,128)(2,1)}) custom-call(bf16[16,48,256]{2,1,0:T(8,128)(2,1)} %bitcast.26, bf16[8,44,512]{2,1,0:T(8,128)(2,1)} %copy.27.gate_ref, bf16[8,44,512]{2,1,0:T(8,128)(2,1)} %copy.28.up_ref, bf16[8,44,512]{2,1,0:T(8,128)(2,1)} %copy.29.down_ref), custom_call_target="tpu_custom_call" | custom-call | tf_op jit(solution)/shard_map/pallas_call | solution.py:97
  225.6 6.7 %fusion.14 = (bf16[1,16,44,2048]{3,2,1,0:T(8,128)(2,1)}, bf16[1,16,44,2048]{3,2,1,0:T(8,128)(2,1)}, bf16[1,16,44,2048]{3,2,1,0:T(8,128)(2,1)}) fusion(bf16[3,16,44,2048]{3,2,1,0:T(8,128)(2,1)} %get-tuple-element.5), kind=kLoop, calls=%fused_computation.46 | loop fusion | bytes 17301504 | tf_op jit(solution)/shard_map/slice | solution.py:165
  232.2 4.3 %squeeze.9 = bf16[704,2048]{1,0:T(8,128)(2,1)} reshape(bf16[1,16,44,2048]{3,2,1,0:T(8,128)(2,1)} %get-tuple-element.10) | data formatting | bytes 5767168 | tf_op jit(solution)/shard_map/squeeze | solution.py:165
  236.6 4.4 %squeeze.10 = bf16[704,2048]{1,0:T(8,128)(2,1)} reshape(bf16[1,16,44,2048]{3,2,1,0:T(8,128)(2,1)} %get-tuple-element.8) | data formatting | bytes 5767168 | tf_op jit(solution)/shard_map/squeeze | solution.py:165
  240.9 4.4 %squeeze.11 = bf16[704,2048]{1,0:T(8,128)(2,1)} reshape(bf16[1,16,44,2048]{3,2,1,0:T(8,128)(2,1)} %get-tuple-element.9) | data formatting | bytes 5767168 | tf_op jit(solution)/shard_map/squeeze | solution.py:165
  245.3 6.6 %fusion.15 = f32[768,704]{0,1:T(8,128)} fusion(bf16[768,2048]{1,0:T(8,128)(2,1)} %bitcast.31, bf16[704,2048]{1,0:T(8,128)(2,1)} %squeeze.9), kind=kOutput, calls=%fused_computation.47 | convolution fusion | flops 2214592512 | bytes 8192000 | tf_op jit(solution)/shard_map/dot_general | solution.py:166
  251.9 12.4 %fusion = bf16[1,768,2048]{2,1,0:T(8,128)(2,1)} fusion(bf16[704,2048]{1,0:T(8,128)(2,1)} %squeeze.11, f32[768,704]{0,1:T(8,128)} %fusion.15, bf16[768,2048]{1,0:T(8,128)(2,1)} %bitcast.32, bf16[704,2048]{1,0:T(8,128)(2,1)} %squeeze.10), kind=kOutput, calls=%fused_computation.4 | convolution fusion | flops 4434001920 | bytes 14221312 | tf_op jit(solution)/shard_map/dot_general | solution.py:169
  264.3 0.0 copy-start.4
  264.3 0.0 reduce-scatter.2.cloned.1.call-update
  264.3 38.4 %reduce-scatter.2.cloned.1.call-done = bf16[1,768,256]{2,1,0:T(8,128)(2,1)} async-done(((bf16[1,768,2048]{2,1,0:T(8,128)(2,1)}), bf16[1,768,256]{2,1,0:T(8,128)(2,1)}) %reduce-scatter.2.cloned.1.call-update) | async-done | bytes 393232 | tf_op jit(solution)/shard_map/reduce_scatter | solution.py:171
  302.8 11.0 %all-to-all-start = ((bf16[16,1,48,256]{3,2,1,0:T(8,128)(2,1)}), bf16[16,1,48,256]{3,2,1,0:T(8,128)(2,1)S(1)}, u32[]{:S(2)}, u32[]{:S(2)}) async-start(bf16[16,1,48,256]{3,2,1,0:T(8,128)(2,1)} %bitcast.27), calls=%async_computation.1 | async-start | bytes 786432 | tf_op jit(solution)/shard_map/all_to_all | solution.py:176
  313.8 0.0 copy-done.4
  313.8 0.0 copy-start.6
  313.8 0.1 copy.23
  314.0 14.5 %all-to-all-done = bf16[16,1,48,256]{3,2,1,0:T(8,128)(2,1)S(1)} async-done(((bf16[16,1,48,256]{3,2,1,0:T(8,128)(2,1)}), bf16[16,1,48,256]{3,2,1,0:T(8,128)(2,1)S(1)}, u32[]{:S(2)}, u32[]{:S(2)}) %all-to-all-start) | async-done | bytes 393248 | tf_op jit(solution)/shard_map/all_to_all | solution.py:176
  328.5 1.9 gather_fusion.1
  330.5 0.3 reshape.151
  330.7 0.7 multiply_reduce_fusion
  331.4 0.7 fusion.13
  332.1 0.1 multiply_reduce_fusion.1
  332.2 21.9 %psum.15 = f32[256]{0:T(256)S(1)} all-reduce(f32[256]{0:T(256)S(1)} %multiply_reduce_fusion.1), channel_id=1, replica_groups=mesh['ep'=16,'mx'=4,'my'=8] {'my'}, use_global_device_ids=true, to_apply=%region_10.11 | all-reduce | flops 256 | bytes 2048 | tf_op jit(solution)/shard_map/psum | solution.py:119
  354.1 0.0 copy-done.6
  354.1 0.8 multiply_convert_fusion.1
  (13 shorter events, 0.1 us)
Async XLA Ops:
  7.2 6.3 %copy-start = (bf16[256,2048]{1,0:T(8,128)(2,1)S(1)}, bf16[256,2048]{1,0:T(8,128)(2,1)}, u32[]{:S(2)}) copy-start(bf16[256,2048]{1,0:T(8,128)(2,1)} %param.10) | copy-start | bytes 3145732
  7.2 26.7 %copy-start.1 = (bf16[8,44,512]{2,0,1:T(8,128)(2,1)S(1)}, bf16[8,44,512]{2,0,1:T(8,128)(2,1)}, u32[]{:S(2)}) copy-start(bf16[8,44,512]{2,0,1:T(8,128)(2,1)} %param.14) | copy-start | bytes 1081348
  7.2 27.6 %copy-start.2 = (bf16[8,44,512]{2,0,1:T(8,128)(2,1)S(1)}, bf16[8,44,512]{2,0,1:T(8,128)(2,1)}, u32[]{:S(2)}) copy-start(bf16[8,44,512]{2,0,1:T(8,128)(2,1)} %param.15) | copy-start | bytes 1081348
  7.2 28.5 %copy-start.3 = (bf16[8,44,512]{2,0,1:T(8,128)(2,1)S(1)}, bf16[8,44,512]{2,0,1:T(8,128)(2,1)}, u32[]{:S(2)}) copy-start(bf16[8,44,512]{2,0,1:T(8,128)(2,1)} %param.16) | copy-start | bytes 1081348
  7.2 29.3 %copy-start.5 = (f32[256]{0:T(256)S(1)}, f32[256]{0:T(256)}, u32[]{:S(2)}) copy-start(f32[256]{0:T(256)} %param.13) | copy-start | bytes 3076
  7.2 295.5 %reduce-scatter.2.cloned.1.call-start = ((), (), s32[]{:S(2)}) async-start(), calls=%async_computation.2 | async-start | bytes 3538944 | tf_op jit(solution)/shard_map/reduce_scatter | solution.py:171
  264.3 49.5 %copy-start.4 = (f32[256,2]{0,1:T(2,128)S(1)}, f32[256,2]{0,1:T(2,128)}, u32[]{:S(2)}) copy-start(f32[256,2]{0,1:T(2,128)} %param.18) | copy-start | bytes 6148
  302.8 25.7 %all-to-all-start = ((bf16[16,1,48,256]{3,2,1,0:T(8,128)(2,1)}), bf16[16,1,48,256]{3,2,1,0:T(8,128)(2,1)S(1)}, u32[]{:S(2)}, u32[]{:S(2)}) async-start(bf16[16,1,48,256]{3,2,1,0:T(8,128)(2,1)} %bitcast.27), calls=%async_computation.1 | async-start | bytes 786432 | tf_op jit(solution)/shard_map/all_to_all | solution.py:176
  313.8 40.3 %copy-start.6 = (f32[256]{0:T(256)S(1)}, f32[256]{0:T(256)}, u32[]{:S(2)}) copy-start(f32[256]{0:T(256)} %param.19) | copy-start | bytes 3076
Sparse Core Ops, SparseCore 0:
  264.4 38.2 reduce-scatter.1

commit v5 on v4

--- a/solution.py
+++ b/solution.py
@@ -26,7 +26,7 @@
 
 
 def move_kernel(n_ep, n_mx, n_my, replicas, packed_ref, gate_ref, up_ref, down_ref,
-                tok_ref, out_ref, tok_sems, send_z, recv_z, send_x, recv_x, local_sem):
+                tok_ref, gate_out, up_out, down_out, tok_sems, send_z, recv_z, send_x, recv_x, local_sem):
     j = lax.axis_index("ep")
     a = lax.axis_index("mx")
     m = lax.axis_index("my")
@@ -44,15 +44,16 @@
         copy.start()
         tok_z.append(copy)
     weights = (gate_ref, up_ref, down_ref)
+    outs = (gate_out, up_out, down_out)
 
     def start_z(k):
         local = pltpu.make_async_copy(
-            weights[k].at[j // replicas], out_ref.at[k, j, :, cols_a], local_sem.at[k])
+            weights[k].at[j // replicas], outs[k].at[j, :, cols_a], local_sem.at[k])
         local.start()
         along_z = [local]
         for d in range(1, n_ep):
             t = lax.rem(j + d, n_ep)
-            copy = remote(weights[k].at[t // replicas], out_ref.at[k, j, :, cols_a],
+            copy = remote(weights[k].at[t // replicas], outs[k].at[j, :, cols_a],
                           send_z.at[k, d], recv_z.at[k, d], (t, a, m))
             copy.start()
             along_z.append(copy)
@@ -78,12 +79,35 @@
         pending.extend(along_z[1:])
         if k + 1 < 3:
             along_z = start_z(k + 1)
-        for e in range(1, n_mx):
-            b = lax.rem(a + e, n_mx)
-            copy = remote(out_ref.at[k, :, :, cols_a], out_ref.at[k, :, :, cols_a],
-                          send_x.at[k, e], recv_x.at[k, e], (j, b, m))
-            copy.start()
-            x_copies.append(copy)
+        if n_mx == 4:
+            right = lax.rem(a + 1, n_mx)
+            left = lax.rem(a + n_mx - 1, n_mx)
+            half = n_ep // 2
+            to_right = remote(outs[k].at[:, :, cols_a], outs[k].at[:, :, cols_a],
+                              send_x.at[k, 0], recv_x.at[k, 0], (j, right, m))
+            to_left = remote(outs[k].at[:, :, cols_a], outs[k].at[:, :, cols_a],
+                             send_x.at[k, 1], recv_x.at[k, 1], (j, left, m))
+            to_right.start()
+            to_left.start()
+            cols_l = pl.ds(pl.multiple_of(left * wb, wb), wb)
+            cols_r = pl.ds(pl.multiple_of(right * wb, wb), wb)
+            to_right.wait_recv()
+            fwd_right = remote(outs[k].at[pl.ds(0, half), :, cols_l], outs[k].at[pl.ds(0, half), :, cols_l],
+                               send_x.at[k, 2], recv_x.at[k, 2], (j, right, m))
+            fwd_right.start()
+            to_left.wait_recv()
+            fwd_left = remote(outs[k].at[pl.ds(half, half), :, cols_r], outs[k].at[pl.ds(half, half), :, cols_r],
+                              send_x.at[k, 3], recv_x.at[k, 3], (j, left, m))
+            fwd_left.start()
+            pending.extend([to_right, to_left])
+            x_copies.extend([fwd_right, fwd_left])
+        else:
+            for e in range(1, n_mx):
+                b = lax.rem(a + e, n_mx)
+                copy = remote(outs[k].at[:, :, cols_a], outs[k].at[:, :, cols_a],
+                              send_x.at[k, e], recv_x.at[k, e], (j, b, m))
+                copy.start()
+                x_copies.append(copy)
     pending.extend(x_copies)
     for copy in pending:
         copy.wait_send()
@@ -98,16 +122,15 @@
         functools.partial(move_kernel, n_ep, n_mx, n_my, replicas),
         out_shape=(
             jax.ShapeDtypeStruct((n_ep, rows, n_my * fb), packed.dtype),
-            jax.ShapeDtypeStruct((3, n_ep, units, n_mx * wb), gate_weight.dtype),
-        ),
+        ) + (jax.ShapeDtypeStruct((n_ep, units, n_mx * wb), gate_weight.dtype),) * 3,
         in_specs=[pl.BlockSpec(memory_space=pl.ANY)] * 4,
-        out_specs=(pl.BlockSpec(memory_space=pl.ANY), pl.BlockSpec(memory_space=pl.ANY)),
+        out_specs=(pl.BlockSpec(memory_space=pl.ANY),) * 4,
         scratch_shapes=[
             pltpu.SemaphoreType.DMA((5, max(n_ep, n_my))),
             pltpu.SemaphoreType.DMA((3, n_ep)),
             pltpu.SemaphoreType.DMA((3, n_ep)),
-            pltpu.SemaphoreType.DMA((3, n_mx)),
-            pltpu.SemaphoreType.DMA((3, n_mx)),
+            pltpu.SemaphoreType.DMA((3, max(n_mx, 4))),
+            pltpu.SemaphoreType.DMA((3, max(n_mx, 4))),
             pltpu.SemaphoreType.DMA((3,)),
         ],
         compiler_params=pltpu.CompilerParams(has_side_effects=True),
@@ -156,13 +179,14 @@
     source = jnp.full((slot_total * capacity,), tok_rows, jnp.int32).at[target].set(row_ids)
     padded = jnp.concatenate([normed, jnp.zeros((1, feat_block), jnp.bfloat16)], axis=0)
     packed = padded[source].reshape(ep_count, capacity, feat_block)
-    tok, moved = move_all(
+    tok, w_gate, w_up, w_down = move_all(
         packed, gate_weight, up_weight, down_weight,
         ep_count, lax.axis_size("mx"), lax.axis_size("my"), replicas,
     )
     tokens_in = tok.reshape(slot_rows, D)
-    flat = moved.reshape(3, ep_count * piece_units, D)
-    w_gate, w_up, w_down = flat[0], flat[1], flat[2]
+    w_gate, w_up, w_down = (
+        w.reshape(ep_count * piece_units, D) for w in (w_gate, w_up, w_down)
+    )
     gate_proj = jnp.dot(tokens_in, w_gate.T, preferred_element_type=jnp.float32)
     up_proj = jnp.dot(tokens_in, w_up.T, preferred_element_type=jnp.float32)
     hidden = (jax.nn.silu(gate_proj) * up_proj).astype(jnp.bfloat16)

time: 364 us -> 350 us (0.962)
  Pallas kernels: 186 us -> 173 us
  local copies, waits for them, and re-layouts: 32.2 us -> 25.5 us
  waiting for transfers between devices: 53 us -> 58.2 us
    squeeze x3 -> x0, local copies, waits for them, and re-layouts: 13.1 us -> none  [shards(): w_gate, w_up, w_down = (flat[0], flat[1], flat[2])]
    reshape x0 -> x3, local copies, waits for them, and re-layouts: none -> 13.1 us  [shards(): w.reshape(ep_count * piece_units, D)]
    pallas_call x1, Pallas kernels: 186 us -> 173 us  [move_all(): pl.pallas_call(functools.partial(move_kernel, n_ep, n_mx, n_my, replicas)...]
    slice x2 -> x1, local copies, waits for them, and re-layouts: 6.87 us -> 0.21 us  [the longest x1 6.65 us: shards(): w_gate, w_up, w_down = (flat[0], flat[1], flat[2])]
    reduce_scatter x1, waiting for transfers between devices: 38.4 us -> 43.7 us  [shards(): lax.psum_scatter(expert_out.astype(jnp.bfloat16), 'my', scatter_dimension...]
where the time goes in v5:
time: 350 us; the launch traced here: 348 us
  Pallas kernels  173 us (49%)
  waiting for transfers between devices  58.2 us (17%)
  blocking collectives  40.6 us (12%)
  local copies, waits for them, and re-layouts  25.5 us (7%)
  matrix products  20.7 us (6%)
  between operations  14.2 us (4%)
  starting transfers between devices  11.1 us (3%)
  other arithmetic  4.43 us (1%)
    pallas_call x1, Pallas kernels, move_all(): pl.pallas_call(functools.partial(move_kernel, n_ep, n_mx, n_my, replicas)...  173 us
    reduce_scatter x1, waiting for transfers between devices, shards(): lax.psum_scatter(expert_out.astype(jnp.bfloat16), 'my', scatter_dimension...  43.7 us
    psum x2, blocking collectives, row_scale(): row_total = lax.psum(partial_sq, 'my')  40.6 us
    all_to_all x1, waiting for transfers between devices, shards(): lax.all_to_all(sent_back, 'ep', split_axis=0, concat_axis=0, tiled=True)  14.5 us
    reshape x3, local copies, waits for them, and re-layouts, shards(): w.reshape(ep_count * piece_units, D)  13.1 us
    dot_general x1, matrix products, shards(): expert_out = jnp.dot(hidden, w_down, preferred_element_type=jnp.float32)  12.4 us
    all_to_all x1, starting transfers between devices, shards(): lax.all_to_all(sent_back, 'ep', split_axis=0, concat_axis=0, tiled=True)  11 us
  transfers between devices with their start and end apart: 2, of which 2 were waited for; matrix products, arithmetic and copies ran while one was open for 0% of the time, Pallas kernels for 0%

profile of v5, /device:TPU:1, one launch (start us, length us, event | category | flops | bytes accessed | tf_op | source)
XLA Modules:
  0.0 347.9 jit_solution(5514335376438410334)
XLA Ops:
  7.2 0.0 copy-start
  7.2 0.0 copy-start.1
  7.2 0.0 copy-start.2
  7.2 0.0 copy-start.3
  7.2 0.0 copy-start.5
  7.2 0.0 reduce-scatter.2.cloned.1.call-start
  7.3 0.9 copy.25
  8.2 0.1 eq.31
  8.4 0.1 eq.27
  8.5 0.7 broadcast_multiply_fusion
  9.2 1.1 reduce-window.6
  10.4 0.2 slice_reduce_fusion
  10.6 0.1 copy.24
  10.8 0.1 mul.95
  10.9 0.1 fusion.4
  11.0 2.4 scatter_custom_fusion
  13.5 0.0 copy-done
  13.5 1.7 multiply_reduce_fusion.2
  15.3 18.7 %psum.14 = f32[256]{0:T(256)S(1)} all-reduce(f32[256]{0:T(256)S(1)} %get-tuple-element.12), channel_id=1, replica_groups=mesh['ep'=16,'mx'=4,'my'=8] {'my'}, use_global_device_ids=true, to_apply=%region_2.0 | all-reduce | flops 256 | bytes 2048 | tf_op jit(solution)/shard_map/psum | solution.py:142
  33.9 0.0 copy-done.1
  33.9 0.9 copy.27.gate_ref
  34.8 0.0 copy-done.2
  34.8 0.9 copy.28.up_ref
  35.7 0.0 copy-done.3
  35.7 0.8 copy.29.down_ref
  36.5 0.0 copy-done.5
  36.5 0.1 multiply_convert_fusion.2
  36.7 3.3 gather_fusion
  39.9 173.1 %shard_map.113 = (bf16[16,48,2048]{2,1,0:T(8,128)(2,1)}, bf16[16,44,2048]{2,1,0:T(8,128)(2,1)}, bf16[16,44,2048]{2,1,0:T(8,128)(2,1)}, bf16[16,44,2048]{2,1,0:T(8,128)(2,1)}) custom-call(bf16[16,48,256]{2,1,0:T(8,128)(2,1)} %bitcast.26, bf16[8,44,512]{2,1,0:T(8,128)(2,1)} %copy.27.gate_ref, bf16[8,44,512]{2,1,0:T(8,128)(2,1)} %copy.28.up_ref, ...), custom_call_target="tpu_custom_call" | custom-call | tf_op jit(solution)/shard_map/pallas_call | solution.py:121
  213.1 4.4 %reshape.152 = bf16[704,2048]{1,0:T(8,128)(2,1)} reshape(bf16[16,44,2048]{2,1,0:T(8,128)(2,1)} %get-tuple-element.7) | data formatting | bytes 5767168 | tf_op jit(solution)/shard_map/reshape | solution.py:188
  217.4 4.3 %reshape.153 = bf16[704,2048]{1,0:T(8,128)(2,1)} reshape(bf16[16,44,2048]{2,1,0:T(8,128)(2,1)} %get-tuple-element.8) | data formatting | bytes 5767168 | tf_op jit(solution)/shard_map/reshape | solution.py:188
  221.8 4.4 %reshape.154 = bf16[704,2048]{1,0:T(8,128)(2,1)} reshape(bf16[16,44,2048]{2,1,0:T(8,128)(2,1)} %get-tuple-element.9) | data formatting | bytes 5767168 | tf_op jit(solution)/shard_map/reshape | solution.py:188
  226.1 6.5 %fusion.14 = f32[768,704]{0,1:T(8,128)} fusion(bf16[768,2048]{1,0:T(8,128)(2,1)} %bitcast.31, bf16[704,2048]{1,0:T(8,128)(2,1)} %reshape.152), kind=kOutput, calls=%fused_computation.46 | convolution fusion | flops 2214592512 | bytes 8192000 | tf_op jit(solution)/shard_map/dot_general | solution.py:190
  232.6 12.4 %fusion = bf16[1,768,2048]{2,1,0:T(8,128)(2,1)} fusion(bf16[704,2048]{1,0:T(8,128)(2,1)} %reshape.154, f32[768,704]{0,1:T(8,128)} %fusion.14, bf16[768,2048]{1,0:T(8,128)(2,1)} %bitcast.32, bf16[704,2048]{1,0:T(8,128)(2,1)} %reshape.153), kind=kOutput, calls=%fused_computation.4 | convolution fusion | flops 4434001920 | bytes 14221312 | tf_op jit(solution)/shard_map/dot_general | solution.py:193
  245.1 0.0 copy-start.4
  245.1 0.0 reduce-scatter.2.cloned.1.call-update
  245.1 43.7 %reduce-scatter.2.cloned.1.call-done = bf16[1,768,256]{2,1,0:T(8,128)(2,1)} async-done(((bf16[1,768,2048]{2,1,0:T(8,128)(2,1)}), bf16[1,768,256]{2,1,0:T(8,128)(2,1)}) %reduce-scatter.2.cloned.1.call-update) | async-done | bytes 393232 | tf_op jit(solution)/shard_map/reduce_scatter | solution.py:195
  288.8 11.0 %all-to-all-start = ((bf16[16,1,48,256]{3,2,1,0:T(8,128)(2,1)}), bf16[16,1,48,256]{3,2,1,0:T(8,128)(2,1)S(1)}, u32[]{:S(2)}, u32[]{:S(2)}) async-start(bf16[16,1,48,256]{3,2,1,0:T(8,128)(2,1)} %bitcast.27), calls=%async_computation.1 | async-start | bytes 786432 | tf_op jit(solution)/shard_map/all_to_all | solution.py:200
  299.8 0.0 copy-done.4
  299.8 0.0 copy-start.6
  299.9 0.1 copy.23
  300.0 14.5 %all-to-all-done = bf16[16,1,48,256]{3,2,1,0:T(8,128)(2,1)S(1)} async-done(((bf16[16,1,48,256]{3,2,1,0:T(8,128)(2,1)}), bf16[16,1,48,256]{3,2,1,0:T(8,128)(2,1)S(1)}, u32[]{:S(2)}, u32[]{:S(2)}) %all-to-all-start) | async-done | bytes 393248 | tf_op jit(solution)/shard_map/all_to_all | solution.py:200
  314.5 1.9 gather_fusion.1
  316.5 0.3 reshape.156
  316.8 0.7 multiply_reduce_fusion
  317.5 0.7 fusion.13
  318.2 0.1 multiply_reduce_fusion.1
  318.3 22.0 %psum.15 = f32[256]{0:T(256)S(1)} all-reduce(f32[256]{0:T(256)S(1)} %multiply_reduce_fusion.1), channel_id=1, replica_groups=mesh['ep'=16,'mx'=4,'my'=8] {'my'}, use_global_device_ids=true, to_apply=%region_10.11 | all-reduce | flops 256 | bytes 2048 | tf_op jit(solution)/shard_map/psum | solution.py:142
  340.3 0.0 copy-done.6
  340.3 0.8 multiply_convert_fusion.1
  (13 shorter events, 0.1 us)
Async XLA Ops:
  7.2 6.3 %copy-start = (bf16[256,2048]{1,0:T(8,128)(2,1)S(1)}, bf16[256,2048]{1,0:T(8,128)(2,1)}, u32[]{:S(2)}) copy-start(bf16[256,2048]{1,0:T(8,128)(2,1)} %param.10) | copy-start | bytes 3145732
  7.2 26.7 %copy-start.1 = (bf16[8,44,512]{2,0,1:T(8,128)(2,1)S(1)}, bf16[8,44,512]{2,0,1:T(8,128)(2,1)}, u32[]{:S(2)}) copy-start(bf16[8,44,512]{2,0,1:T(8,128)(2,1)} %param.14) | copy-start | bytes 1081348
  7.2 27.6 %copy-start.2 = (bf16[8,44,512]{2,0,1:T(8,128)(2,1)S(1)}, bf16[8,44,512]{2,0,1:T(8,128)(2,1)}, u32[]{:S(2)}) copy-start(bf16[8,44,512]{2,0,1:T(8,128)(2,1)} %param.15) | copy-start | bytes 1081348
  7.2 28.5 %copy-start.3 = (bf16[8,44,512]{2,0,1:T(8,128)(2,1)S(1)}, bf16[8,44,512]{2,0,1:T(8,128)(2,1)}, u32[]{:S(2)}) copy-start(bf16[8,44,512]{2,0,1:T(8,128)(2,1)} %param.16) | copy-start | bytes 1081348
  7.2 29.3 %copy-start.5 = (f32[256]{0:T(256)S(1)}, f32[256]{0:T(256)}, u32[]{:S(2)}) copy-start(f32[256]{0:T(256)} %param.13) | copy-start | bytes 3076
  7.2 281.6 %reduce-scatter.2.cloned.1.call-start = ((), (), s32[]{:S(2)}) async-start(), calls=%async_computation.2 | async-start | bytes 3538944 | tf_op jit(solution)/shard_map/reduce_scatter | solution.py:195
  245.1 54.8 %copy-start.4 = (f32[256,2]{0,1:T(2,128)S(1)}, f32[256,2]{0,1:T(2,128)}, u32[]{:S(2)}) copy-start(f32[256,2]{0,1:T(2,128)} %param.18) | copy-start | bytes 6148
  288.8 25.8 %all-to-all-start = ((bf16[16,1,48,256]{3,2,1,0:T(8,128)(2,1)}), bf16[16,1,48,256]{3,2,1,0:T(8,128)(2,1)S(1)}, u32[]{:S(2)}, u32[]{:S(2)}) async-start(bf16[16,1,48,256]{3,2,1,0:T(8,128)(2,1)} %bitcast.27), calls=%async_computation.1 | async-start | bytes 786432 | tf_op jit(solution)/shard_map/all_to_all | solution.py:200
  299.8 40.5 %copy-start.6 = (f32[256]{0:T(256)S(1)}, f32[256]{0:T(256)}, u32[]{:S(2)}) copy-start(f32[256]{0:T(256)} %param.19) | copy-start | bytes 3076
Sparse Core Ops, SparseCore 0:
  245.2 43.5 reduce-scatter.1

commit v6 on v5

--- a/solution.py
+++ b/solution.py
@@ -26,7 +26,8 @@
 
 
 def move_kernel(n_ep, n_mx, n_my, replicas, packed_ref, gate_ref, up_ref, down_ref,
-                tok_ref, gate_out, up_out, down_out, tok_sems, send_z, recv_z, send_x, recv_x, local_sem):
+                tok_ref, gate_out, up_out, down_out, tok_sems, send_z, recv_z, fwd_send, fwd_recv,
+                send_x, recv_x, local_sem):
     j = lax.axis_index("ep")
     a = lax.axis_index("mx")
     m = lax.axis_index("my")
@@ -46,20 +47,36 @@
     weights = (gate_ref, up_ref, down_ref)
     outs = (gate_out, up_out, down_out)
 
-    def start_z(k):
+    half_ring = n_ep // 2
+    side = half_ring - 1
+    parity = lax.rem(j, 2)
+    partner = j + 1 - 2 * parity
+
+    def start_direct(k):
         local = pltpu.make_async_copy(
             weights[k].at[j // replicas], outs[k].at[j, :, cols_a], local_sem.at[k])
         local.start()
-        along_z = [local]
-        for d in range(1, n_ep):
-            t = lax.rem(j + d, n_ep)
+        direct = []
+        for d in range(1, side + 1):
+            sign = 1 - 2 * lax.rem(j + d, 2)
+            t = lax.rem(j + n_ep + sign * d, n_ep)
             copy = remote(weights[k].at[t // replicas], outs[k].at[j, :, cols_a],
                           send_z.at[k, d], recv_z.at[k, d], (t, a, m))
             copy.start()
-            along_z.append(copy)
-        return along_z
-
-    along_z = start_z(0)
+            direct.append(copy)
+        return local, direct
+
+    def start_forward(k):
+        forward = []
+        for d in range(0, side + 1):
+            src = lax.rem(j + n_ep - d + 2 * parity * d, n_ep)
+            copy = remote(outs[k].at[src, :, cols_a], outs[k].at[src, :, cols_a],
+                          fwd_send.at[k, d], fwd_recv.at[k, d], (partner, a, m))
+            copy.start()
+            forward.append(copy)
+        return forward
+
+    local, direct = start_direct(0)
     tok_local.wait()
     for copy in tok_z:
         copy.wait_recv()
@@ -73,12 +90,16 @@
     pending.extend(tok_my)
     x_copies = []
     for k in range(3):
-        along_z[0].wait()
-        for copy in along_z[1:]:
+        local.wait()
+        for copy in direct:
             copy.wait_recv()
-        pending.extend(along_z[1:])
+        pending.extend(direct)
+        forward = start_forward(k)
         if k + 1 < 3:
-            along_z = start_z(k + 1)
+            local, direct = start_direct(k + 1)
+        for copy in forward:
+            copy.wait_recv()
+        pending.extend(forward)
         if n_mx == 4:
             right = lax.rem(a + 1, n_mx)
             left = lax.rem(a + n_mx - 1, n_mx)
@@ -129,6 +150,8 @@
             pltpu.SemaphoreType.DMA((5, max(n_ep, n_my))),
             pltpu.SemaphoreType.DMA((3, n_ep)),
             pltpu.SemaphoreType.DMA((3, n_ep)),
+            pltpu.SemaphoreType.DMA((3, n_ep)),
+            pltpu.SemaphoreType.DMA((3, n_ep)),
             pltpu.SemaphoreType.DMA((3, max(n_mx, 4))),
             pltpu.SemaphoreType.DMA((3, max(n_mx, 4))),
             pltpu.SemaphoreType.DMA((3,)),
@@ -184,13 +207,10 @@
         ep_count, lax.axis_size("mx"), lax.axis_size("my"), replicas,
     )
     tokens_in = tok.reshape(slot_rows, D)
-    w_gate, w_up, w_down = (
-        w.reshape(ep_count * piece_units, D) for w in (w_gate, w_up, w_down)
-    )
-    gate_proj = jnp.dot(tokens_in, w_gate.T, preferred_element_type=jnp.float32)
-    up_proj = jnp.dot(tokens_in, w_up.T, preferred_element_type=jnp.float32)
+    gate_proj = jnp.einsum("rd,spd->rsp", tokens_in, w_gate, preferred_element_type=jnp.float32)
+    up_proj = jnp.einsum("rd,spd->rsp", tokens_in, w_up, preferred_element_type=jnp.float32)
     hidden = (jax.nn.silu(gate_proj) * up_proj).astype(jnp.bfloat16)
-    expert_out = jnp.dot(hidden, w_down, preferred_element_type=jnp.float32)
+    expert_out = jnp.einsum("rsp,spd->rd", hidden, w_down, preferred_element_type=jnp.float32)
     expert_out = expert_out.reshape(slot_dev, slot_rows, D)
     summed = lax.psum_scatter(
         expert_out.astype(jnp.bfloat16), "my", scatter_dimension=2, tiled=True

time: 350 us -> 328 us (0.937)
  Pallas kernels: 173 us -> 152 us
  local copies, waits for them, and re-layouts: 25.5 us -> 12.4 us
  waiting for transfers between devices: 58.2 us -> 65.5 us
  matrix products: 20.7 us -> 24.6 us
    pallas_call x1, Pallas kernels: 173 us -> 152 us  [move_all(): pl.pallas_call(functools.partial(move_kernel, n_ep, n_mx, n_my, replicas)...]
    reshape x3 -> x0, local copies, waits for them, and re-layouts: 13.1 us -> none  [shards(): w.reshape(ep_count * piece_units, D)]
    reduce_scatter x1, waiting for transfers between devices: 43.7 us -> 51 us  [shards(): lax.psum_scatter(expert_out.astype(jnp.bfloat16), 'my', scatter_dimension...]
    dot_general x2, matrix products: 18.9 us -> 22.9 us  [the longest x1 15.9 us: shards(): jnp.einsum('rsp,spd->rd', hidden, w_down, preferred_element_type=jnp.floa...]
where the time goes in v6:
time: 328 us; the launch traced here: 325 us
  Pallas kernels  152 us (46%)
  waiting for transfers between devices  65.5 us (20%)
  blocking collectives  40.5 us (12%)
  matrix products  24.6 us (8%)
  between operations  14.2 us (4%)
  local copies, waits for them, and re-layouts  12.4 us (4%)
  starting transfers between devices  11 us (3%)
  other arithmetic  4.42 us (1%)
    pallas_call x1, Pallas kernels, move_all(): pl.pallas_call(functools.partial(move_kernel, n_ep, n_mx, n_my, replicas)...  152 us
    reduce_scatter x1, waiting for transfers between devices, shards(): lax.psum_scatter(expert_out.astype(jnp.bfloat16), 'my', scatter_dimension...  51 us
    psum x2, blocking collectives, row_scale(): row_total = lax.psum(partial_sq, 'my')  40.5 us
    dot_general x1, matrix products, shards(): jnp.einsum('rsp,spd->rd', hidden, w_down, preferred_element_type=jnp.floa...  15.9 us
    all_to_all x1, waiting for transfers between devices, shards(): lax.all_to_all(sent_back, 'ep', split_axis=0, concat_axis=0, tiled=True)  14.5 us
    all_to_all x1, starting transfers between devices, shards(): lax.all_to_all(sent_back, 'ep', split_axis=0, concat_axis=0, tiled=True)  11 us
    dot_general x1, matrix products, shards(): jnp.einsum('rd,spd->rsp', tokens_in, w_up, preferred_element_type=jnp.flo...  6.91 us
  transfers between devices with their start and end apart: 2, of which 2 were waited for; matrix products, arithmetic and copies ran while one was open for 0% of the time, Pallas kernels for 0%

profile of v6, /device:TPU:1, one launch (start us, length us, event | category | flops | bytes accessed | tf_op | source)
XLA Modules:
  0.0 325.2 jit_solution(9593210512225140366)
XLA Ops:
  7.2 0.0 copy-start
  7.2 0.0 copy-start.1
  7.2 0.0 copy-start.2
  7.2 0.0 copy-start.3
  7.2 0.0 copy-start.5
  7.2 0.0 reduce-scatter.2.cloned.1.call-start
  7.3 0.9 copy.25
  8.2 0.1 eq.31
  8.4 0.1 eq.27
  8.5 0.7 broadcast_multiply_fusion
  9.2 1.1 reduce-window.6
  10.4 0.2 slice_reduce_fusion
  10.6 0.1 copy.24
  10.8 0.1 mul.95
  10.9 0.1 fusion.5
  11.0 2.4 scatter_custom_fusion
  13.5 0.0 copy-done
  13.5 1.7 multiply_reduce_fusion.2
  15.3 18.7 %psum.14 = f32[256]{0:T(256)S(1)} all-reduce(f32[256]{0:T(256)S(1)} %get-tuple-element.12), channel_id=1, replica_groups=mesh['ep'=16,'mx'=4,'my'=8] {'my'}, use_global_device_ids=true, to_apply=%region_2.0 | all-reduce | flops 256 | bytes 2048 | tf_op jit(solution)/shard_map/psum | solution.py:165
  33.9 0.0 copy-done.1
  33.9 0.9 copy.27.gate_ref
  34.8 0.0 copy-done.2
  34.8 0.9 copy.28.up_ref
  35.7 0.0 copy-done.3
  35.7 0.8 copy.29.down_ref
  36.5 0.0 copy-done.5
  36.5 0.1 multiply_convert_fusion.2
  36.7 3.3 %gather_fusion = bf16[768,256]{1,0:T(8,128)(2,1)} fusion(bf16[257,256]{1,0:T(8,128)(2,1)S(1)} %concatenate.3, s32[1024]{0:T(1024)S(1)} %pad_clamp_fusion.1), kind=kCustom, calls=%fused_computation | custom fusion | bytes 789504 | tf_op jit(solution)/shard_map/gather | solution.py:204
  39.9 152.4 %shard_map.113 = (bf16[16,48,2048]{2,1,0:T(8,128)(2,1)}, bf16[16,44,2048]{2,1,0:T(8,128)(2,1)}, bf16[16,44,2048]{2,1,0:T(8,128)(2,1)}, bf16[16,44,2048]{2,1,0:T(8,128)(2,1)}) custom-call(bf16[16,48,256]{2,1,0:T(8,128)(2,1)} %bitcast.32, bf16[8,44,512]{2,1,0:T(8,128)(2,1)} %copy.27.gate_ref, bf16[8,44,512]{2,1,0:T(8,128)(2,1)} %copy.28.up_ref, ...), custom_call_target="tpu_custom_call" | custom-call | tf_op jit(solution)/shard_map/pallas_call | solution.py:142
  192.4 6.9 %fusion.15 = f32[768,16,44]{0,2,1:T(8,128)} fusion(bf16[768,2048,1]{1,0,2:T(8,128)(2,1)} %bitcast.37, bf16[16,44,2048]{2,1,0:T(8,128)(2,1)} %get-tuple-element.8), kind=kOutput, calls=%fused_computation.47 | convolution fusion | flops 2214592512 | bytes 8192000 | tf_op jit(solution)/shard_map/rd,spd->rsp/dot_general | solution.py:211
  199.3 15.9 %fusion = bf16[1,768,2048]{2,1,0:T(8,128)(2,1)} fusion(bf16[16,44,2048]{2,1,0:T(8,128)(2,1)} %get-tuple-element.9, f32[768,16,44]{0,2,1:T(8,128)} %fusion.15, bf16[768,2048,1]{1,0,2:T(8,128)(2,1)} %bitcast.38, bf16[16,44,2048]{2,1,0:T(8,128)(2,1)} %get-tuple-element.7), kind=kOutput, calls=%fused_computation.4 | convolution fusion | flops 4434001920 | bytes 14221312 | tf_op jit(solution)/shard_map/rsp,spd->rd/dot_general | solution.py:213
  215.2 0.0 copy-start.4
  215.2 0.0 reduce-scatter.2.cloned.1.call-update
  215.3 0.0 copy-start.6
  215.3 51.0 %reduce-scatter.2.cloned.1.call-done = bf16[1,768,256]{2,1,0:T(8,128)(2,1)} async-done(((bf16[1,768,2048]{2,1,0:T(8,128)(2,1)}), bf16[1,768,256]{2,1,0:T(8,128)(2,1)}) %reduce-scatter.2.cloned.1.call-update) | async-done | bytes 393232 | tf_op jit(solution)/shard_map/reduce_scatter | solution.py:215
  266.3 11.0 %all-to-all-start = ((bf16[16,1,48,256]{3,2,1,0:T(8,128)(2,1)}), bf16[16,1,48,256]{3,2,1,0:T(8,128)(2,1)S(1)}, u32[]{:S(2)}, u32[]{:S(2)}) async-start(bf16[16,1,48,256]{3,2,1,0:T(8,128)(2,1)} %bitcast.33), calls=%async_computation.1 | async-start | bytes 786432 | tf_op jit(solution)/shard_map/all_to_all | solution.py:220
  277.3 0.0 copy-done.4
  277.3 0.1 copy.23
  277.5 14.5 %all-to-all-done = bf16[16,1,48,256]{3,2,1,0:T(8,128)(2,1)S(1)} async-done(((bf16[16,1,48,256]{3,2,1,0:T(8,128)(2,1)}), bf16[16,1,48,256]{3,2,1,0:T(8,128)(2,1)S(1)}, u32[]{:S(2)}, u32[]{:S(2)}) %all-to-all-start) | async-done | bytes 393248 | tf_op jit(solution)/shard_map/all_to_all | solution.py:220
  292.0 1.9 gather_fusion.1
  293.9 0.3 reshape.144
  294.2 0.7 multiply_reduce_fusion
  294.9 0.7 fusion.14
  295.6 0.1 multiply_reduce_fusion.1
  295.7 21.9 %psum.15 = f32[256]{0:T(256)S(1)} all-reduce(f32[256]{0:T(256)S(1)} %multiply_reduce_fusion.1), channel_id=1, replica_groups=mesh['ep'=16,'mx'=4,'my'=8] {'my'}, use_global_device_ids=true, to_apply=%region_10.11 | all-reduce | flops 256 | bytes 2048 | tf_op jit(solution)/shard_map/psum | solution.py:165
  317.6 0.0 copy-done.6
  317.6 0.8 multiply_convert_fusion.1
  (13 shorter events, 0.1 us)
Async XLA Ops:
  7.2 6.3 %copy-start = (bf16[256,2048]{1,0:T(8,128)(2,1)S(1)}, bf16[256,2048]{1,0:T(8,128)(2,1)}, u32[]{:S(2)}) copy-start(bf16[256,2048]{1,0:T(8,128)(2,1)} %param.10) | copy-start | bytes 3145732
  7.2 26.7 %copy-start.1 = (bf16[8,44,512]{2,0,1:T(8,128)(2,1)S(1)}, bf16[8,44,512]{2,0,1:T(8,128)(2,1)}, u32[]{:S(2)}) copy-start(bf16[8,44,512]{2,0,1:T(8,128)(2,1)} %param.14) | copy-start | bytes 1081348
  7.2 27.6 %copy-start.2 = (bf16[8,44,512]{2,0,1:T(8,128)(2,1)S(1)}, bf16[8,44,512]{2,0,1:T(8,128)(2,1)}, u32[]{:S(2)}) copy-start(bf16[8,44,512]{2,0,1:T(8,128)(2,1)} %param.15) | copy-start | bytes 1081348
  7.2 28.5 %copy-start.3 = (bf16[8,44,512]{2,0,1:T(8,128)(2,1)S(1)}, bf16[8,44,512]{2,0,1:T(8,128)(2,1)}, u32[]{:S(2)}) copy-start(bf16[8,44,512]{2,0,1:T(8,128)(2,1)} %param.16) | copy-start | bytes 1081348
  7.2 29.3 %copy-start.5 = (f32[256]{0:T(256)S(1)}, f32[256]{0:T(256)}, u32[]{:S(2)}) copy-start(f32[256]{0:T(256)} %param.13) | copy-start | bytes 3076
  7.2 259.0 %reduce-scatter.2.cloned.1.call-start = ((), (), s32[]{:S(2)}) async-start(), calls=%async_computation.2 | async-start | bytes 3538944 | tf_op jit(solution)/shard_map/reduce_scatter | solution.py:215
  215.2 62.0 %copy-start.4 = (f32[256,2]{0,1:T(2,128)S(1)}, f32[256,2]{0,1:T(2,128)}, u32[]{:S(2)}) copy-start(f32[256,2]{0,1:T(2,128)} %param.18) | copy-start | bytes 6148
  215.3 102.3 %copy-start.6 = (f32[256]{0:T(256)S(1)}, f32[256]{0:T(256)}, u32[]{:S(2)}) copy-start(f32[256]{0:T(256)} %param.19) | copy-start | bytes 3076
  266.3 25.7 %all-to-all-start = ((bf16[16,1,48,256]{3,2,1,0:T(8,128)(2,1)}), bf16[16,1,48,256]{3,2,1,0:T(8,128)(2,1)S(1)}, u32[]{:S(2)}, u32[]{:S(2)}) async-start(bf16[16,1,48,256]{3,2,1,0:T(8,128)(2,1)} %bitcast.33), calls=%async_computation.1 | async-start | bytes 786432 | tf_op jit(solution)/shard_map/all_to_all | solution.py:220
Sparse Core Ops, SparseCore 0:
  215.4 50.8 reduce-scatter.1

commit v7 on v6

--- a/solution.py
+++ b/solution.py
@@ -160,9 +160,45 @@
     )(packed, gate_weight, up_weight, down_weight)
 
 
+def sum_kernel(n_my, x_ref, o_ref, slots, send, recv):
+    j = lax.axis_index("ep")
+    a = lax.axis_index("mx")
+    m = lax.axis_index("my")
+    slots[m] = x_ref[...]
+    copies = []
+    for e in range(1, n_my):
+        b = lax.rem(m + e, n_my)
+        copy = remote(x_ref, slots.at[m], send.at[e], recv.at[e], (j, a, b))
+        copy.start()
+        copies.append(copy)
+    for copy in copies:
+        copy.wait_send()
+    for copy in copies:
+        copy.wait_recv()
+    o_ref[...] = jnp.sum(slots[...], axis=0)
+
+
+def sum_over_my(values):
+    n_my = lax.axis_size("my")
+    row = values.reshape(1, -1)
+    total = pl.pallas_call(
+        functools.partial(sum_kernel, n_my),
+        out_shape=jax.ShapeDtypeStruct(row.shape, row.dtype),
+        in_specs=[pl.BlockSpec(memory_space=pltpu.VMEM)],
+        out_specs=pl.BlockSpec(memory_space=pltpu.VMEM),
+        scratch_shapes=[
+            pltpu.VMEM((n_my,) + row.shape, row.dtype),
+            pltpu.SemaphoreType.DMA((n_my,)),
+            pltpu.SemaphoreType.DMA((n_my,)),
+        ],
+        compiler_params=pltpu.CompilerParams(has_side_effects=True),
+    )(row)
+    return total.reshape(values.shape)
+
+
 def row_scale(stream_f):
     partial_sq = jnp.sum(stream_f * stream_f, axis=1)
-    row_total = lax.psum(partial_sq, "my")
+    row_total = sum_over_my(partial_sq)
     return lax.rsqrt(row_total / D + EPSILON)
 
 

time: 328 us -> 344 us (1.049)
  Pallas kernels: 152 us -> 208 us
  blocking collectives: 40.5 us -> 0 us
    pallas_call x0 -> x2, Pallas kernels: none -> 54.3 us  [sum_over_my(): pl.pallas_call(functools.partial(sum_kernel, n_my), out_shape=jax.ShapeDt...]
    psum x2 -> x0, blocking collectives: 40.5 us -> none  [row_scale(): row_total = lax.psum(partial_sq, 'my')]
where the time goes in v7:
time: 344 us; the launch traced here: 343 us
  Pallas kernels  208 us (60%)
  waiting for transfers between devices  65.5 us (19%)
  matrix products  25.2 us (7%)
  between operations  14.2 us (4%)
  local copies, waits for them, and re-layouts  12.4 us (4%)
  starting transfers between devices  11.1 us (3%)
  other arithmetic  6.34 us (2%)
    pallas_call x1, Pallas kernels, move_all(): pl.pallas_call(functools.partial(move_kernel, n_ep, n_mx, n_my, replicas)...  154 us
    pallas_call x2, Pallas kernels, sum_over_my(): pl.pallas_call(functools.partial(sum_kernel, n_my), out_shape=jax.ShapeDt...  54.3 us
    reduce_scatter x1, waiting for transfers between devices, shards(): lax.psum_scatter(expert_out.astype(jnp.bfloat16), 'my', scatter_dimension...  51 us
    dot_general x1, matrix products, shards(): jnp.einsum('rsp,spd->rd', hidden, w_down, preferred_element_type=jnp.floa...  15.9 us
    all_to_all x1, waiting for transfers between devices, shards(): lax.all_to_all(sent_back, 'ep', split_axis=0, concat_axis=0, tiled=True)  14.5 us
    all_to_all x1, starting transfers between devices, shards(): lax.all_to_all(sent_back, 'ep', split_axis=0, concat_axis=0, tiled=True)  11 us
    dot_general x1, matrix products, shards(): jnp.einsum('rd,spd->rsp', tokens_in, w_up, preferred_element_type=jnp.flo...  6.92 us
  transfers between devices with their start and end apart: 2, of which 2 were waited for; matrix products, arithmetic and copies ran while one was open for 0% of the time, Pallas kernels for 0%

profile of v7, /device:TPU:1, one launch (start us, length us, event | category | flops | bytes accessed | tf_op | source)
XLA Modules:
  0.0 343.3 jit_solution(8962394294124998620)
XLA Ops:
  7.2 0.0 copy-start
  7.2 0.0 copy-start.1
  7.2 0.0 copy-start.2
  7.2 0.0 copy-start.3
  7.2 0.0 copy-start.5
  7.2 0.0 reduce-scatter.2.cloned.1.call-start
  7.3 0.9 copy.25
  8.2 0.1 eq.31
  8.4 0.1 eq.27
  8.5 0.7 broadcast_multiply_fusion
  9.2 1.1 reduce-window.6
  10.4 0.2 slice_reduce_fusion
  10.6 0.1 copy.24
  10.8 0.1 mul.95
  10.9 0.1 fusion.5
  11.0 2.4 scatter_custom_fusion
  13.5 0.0 copy-done
  13.5 2.3 multiply_reduce_fusion.2
  15.8 27.3 %shard_map.113 = f32[1,256]{1,0:T(1,128)} custom-call(f32[1,256]{1,0:T(1,128)} %bitcast.42), custom_call_target="tpu_custom_call" | custom-call | tf_op jit(solution)/shard_map/pallas_call | solution.py:184
  43.2 0.7 add_rsqrt_fusion.1
  43.8 0.0 copy-done.1
  43.9 0.9 copy.27.gate_ref
  44.7 0.0 copy-done.2
  44.7 0.9 copy.28.up_ref
  45.6 0.0 copy-done.3
  45.6 0.8 copy.29.down_ref
  46.5 0.0 copy-done.5
  46.5 0.1 multiply_convert_fusion.2
  46.6 3.3 gather_fusion
  49.9 154.2 %shard_map.114 = (bf16[16,48,2048]{2,1,0:T(8,128)(2,1)}, bf16[16,44,2048]{2,1,0:T(8,128)(2,1)}, bf16[16,44,2048]{2,1,0:T(8,128)(2,1)}, bf16[16,44,2048]{2,1,0:T(8,128)(2,1)}) custom-call(bf16[16,48,256]{2,1,0:T(8,128)(2,1)} %bitcast.36, bf16[8,44,512]{2,1,0:T(8,128)(2,1)} %copy.27.gate_ref, bf16[8,44,512]{2,1,0:T(8,128)(2,1)} %copy.28.up_ref, ...), custom_call_target="tpu_custom_call" | custom-call | tf_op jit(solution)/shard_map/pallas_call | solution.py:142
  204.0 6.9 %fusion.15 = f32[768,16,44]{0,2,1:T(8,128)} fusion(bf16[768,2048,1]{1,0,2:T(8,128)(2,1)} %bitcast.45, bf16[16,44,2048]{2,1,0:T(8,128)(2,1)} %get-tuple-element.8), kind=kOutput, calls=%fused_computation.47 | convolution fusion | flops 2214592512 | bytes 8192000 | tf_op jit(solution)/shard_map/rd,spd->rsp/dot_general | solution.py:247
  211.0 15.9 %fusion = bf16[1,768,2048]{2,1,0:T(8,128)(2,1)} fusion(bf16[16,44,2048]{2,1,0:T(8,128)(2,1)} %get-tuple-element.9, f32[768,16,44]{0,2,1:T(8,128)} %fusion.15, bf16[768,2048,1]{1,0,2:T(8,128)(2,1)} %bitcast.46, bf16[16,44,2048]{2,1,0:T(8,128)(2,1)} %get-tuple-element.7), kind=kOutput, calls=%fused_computation.4 | convolution fusion | flops 4434001920 | bytes 14221312 | tf_op jit(solution)/shard_map/rsp,spd->rd/dot_general | solution.py:249
  226.9 0.0 copy-start.4
  226.9 0.0 reduce-scatter.2.cloned.1.call-update
  226.9 0.0 copy-start.6
  226.9 51.0 %reduce-scatter.2.cloned.1.call-done = bf16[1,768,256]{2,1,0:T(8,128)(2,1)} async-done(((bf16[1,768,2048]{2,1,0:T(8,128)(2,1)}), bf16[1,768,256]{2,1,0:T(8,128)(2,1)}) %reduce-scatter.2.cloned.1.call-update) | async-done | bytes 393232 | tf_op jit(solution)/shard_map/reduce_scatter | solution.py:251
  278.0 11.0 %all-to-all-start = ((bf16[16,1,48,256]{3,2,1,0:T(8,128)(2,1)}), bf16[16,1,48,256]{3,2,1,0:T(8,128)(2,1)S(1)}, u32[]{:S(2)}, u32[]{:S(2)}) async-start(bf16[16,1,48,256]{3,2,1,0:T(8,128)(2,1)} %bitcast.37), calls=%async_computation.1 | async-start | bytes 786432 | tf_op jit(solution)/shard_map/all_to_all | solution.py:256
  289.0 0.0 copy-done.4
  289.0 0.1 copy.23
  289.2 14.5 %all-to-all-done = bf16[16,1,48,256]{3,2,1,0:T(8,128)(2,1)S(1)} async-done(((bf16[16,1,48,256]{3,2,1,0:T(8,128)(2,1)}), bf16[16,1,48,256]{3,2,1,0:T(8,128)(2,1)S(1)}, u32[]{:S(2)}, u32[]{:S(2)}) %all-to-all-start) | async-done | bytes 393248 | tf_op jit(solution)/shard_map/all_to_all | solution.py:256
  303.7 1.9 gather_fusion.1
  305.7 0.3 reshape.176
  305.9 0.7 multiply_reduce_fusion
  306.6 0.7 fusion.14
  307.3 0.7 multiply_reduce_fusion.1
  308.0 27.0 %shard_map.115 = f32[1,256]{1,0:T(1,128)} custom-call(f32[1,256]{1,0:T(1,128)} %bitcast.44), custom_call_target="tpu_custom_call" | custom-call | tf_op jit(solution)/shard_map/pallas_call | solution.py:184
  335.0 0.7 add_rsqrt_fusion
  335.7 0.0 copy-done.6
  335.7 0.8 multiply_convert_fusion.1
  (11 shorter events, 0.1 us)
Async XLA Ops:
  7.2 6.3 %copy-start = (bf16[256,2048]{1,0:T(8,128)(2,1)S(1)}, bf16[256,2048]{1,0:T(8,128)(2,1)}, u32[]{:S(2)}) copy-start(bf16[256,2048]{1,0:T(8,128)(2,1)} %param.10) | copy-start | bytes 3145732
  7.2 36.7 %copy-start.1 = (bf16[8,44,512]{2,0,1:T(8,128)(2,1)S(1)}, bf16[8,44,512]{2,0,1:T(8,128)(2,1)}, u32[]{:S(2)}) copy-start(bf16[8,44,512]{2,0,1:T(8,128)(2,1)} %param.14) | copy-start | bytes 1081348
  7.2 37.6 %copy-start.2 = (bf16[8,44,512]{2,0,1:T(8,128)(2,1)S(1)}, bf16[8,44,512]{2,0,1:T(8,128)(2,1)}, u32[]{:S(2)}) copy-start(bf16[8,44,512]{2,0,1:T(8,128)(2,1)} %param.15) | copy-start | bytes 1081348
  7.2 38.4 %copy-start.3 = (bf16[8,44,512]{2,0,1:T(8,128)(2,1)S(1)}, bf16[8,44,512]{2,0,1:T(8,128)(2,1)}, u32[]{:S(2)}) copy-start(bf16[8,44,512]{2,0,1:T(8,128)(2,1)} %param.16) | copy-start | bytes 1081348
  7.2 39.3 %copy-start.5 = (f32[256]{0:T(256)S(1)}, f32[256]{0:T(256)}, u32[]{:S(2)}) copy-start(f32[256]{0:T(256)} %param.13) | copy-start | bytes 3076
  7.2 270.7 %reduce-scatter.2.cloned.1.call-start = ((), (), s32[]{:S(2)}) async-start(), calls=%async_computation.2 | async-start | bytes 3538944 | tf_op jit(solution)/shard_map/reduce_scatter | solution.py:251
  226.9 62.1 %copy-start.4 = (f32[256,2]{0,1:T(2,128)S(1)}, f32[256,2]{0,1:T(2,128)}, u32[]{:S(2)}) copy-start(f32[256,2]{0,1:T(2,128)} %param.18) | copy-start | bytes 6148
  226.9 108.7 %copy-start.6 = (f32[256]{0:T(256)S(1)}, f32[256]{0:T(256)}, u32[]{:S(2)}) copy-start(f32[256]{0:T(256)} %param.19) | copy-start | bytes 3076
  278.0 25.7 %all-to-all-start = ((bf16[16,1,48,256]{3,2,1,0:T(8,128)(2,1)}), bf16[16,1,48,256]{3,2,1,0:T(8,128)(2,1)S(1)}, u32[]{:S(2)}, u32[]{:S(2)}) async-start(bf16[16,1,48,256]{3,2,1,0:T(8,128)(2,1)} %bitcast.37), calls=%async_computation.1 | async-start | bytes 786432 | tf_op jit(solution)/shard_map/all_to_all | solution.py:256
Sparse Core Ops, SparseCore 0:
  227.1 50.8 reduce-scatter.1

commit v8 on v6

--- a/solution.py
+++ b/solution.py
@@ -160,6 +160,86 @@
     )(packed, gate_weight, up_weight, down_weight)
 
 
+def back_kernel(n_ep, n_my, ex_ref, out_ref, rx_core, chip_part, rx_y, result, sems):
+    j = lax.axis_index("ep")
+    a = lax.axis_index("mx")
+    m = lax.axis_index("my")
+    fb = out_ref.shape[2]
+    cap = out_ref.shape[1]
+    chips = n_my // 2
+    core = lax.rem(m, 2)
+    y = m // 2
+    partner = m + 1 - 2 * core
+    barrier = pltpu.get_barrier_semaphore()
+    peers = [(j, a, partner)]
+    peers += [(j, a, lax.rem(y + e, chips) * 2 + core) for e in range(1, chips)]
+    peers += [(lax.rem(j + d, n_ep), a, m) for d in range(1, n_ep)]
+    for peer in peers:
+        pl.semaphore_signal(barrier, inc=1, device_id=peer, device_id_type=MESH)
+    pl.semaphore_wait(barrier, len(peers))
+
+    def cols(block):
+        return pl.ds(pl.multiple_of(block * fb, fb), fb)
+
+    to_core = []
+    for i in range(chips):
+        copy = remote(ex_ref.at[:, cols(1 - core + 2 * i)], rx_core.at[i],
+                      sems.at[0, i], sems.at[1, i], (j, a, partner))
+        copy.start()
+        to_core.append(copy)
+    for copy in to_core:
+        copy.wait_recv()
+    for i in range(chips):
+        own = ex_ref[:, cols(core + 2 * i)].astype(jnp.float32)
+        chip_part[i] = (own + rx_core[i].astype(jnp.float32)).astype(chip_part.dtype)
+    to_y = []
+    for e in range(1, chips):
+        other = lax.rem(y + e, chips)
+        copy = remote(chip_part.at[other], rx_y.at[e - 1],
+                      sems.at[2, e], sems.at[3, e], (j, a, other * 2 + core))
+        copy.start()
+        to_y.append(copy)
+    for copy in to_y:
+        copy.wait_recv()
+    total = chip_part[y].astype(jnp.float32)
+    for e in range(1, chips):
+        total = total + rx_y[e - 1].astype(jnp.float32)
+    result[...] = total.astype(result.dtype)
+    local = pltpu.make_async_copy(result.at[pl.ds(j * cap, cap)], out_ref.at[j], sems.at[4, 0])
+    local.start()
+    to_z = []
+    for d in range(1, n_ep):
+        t = lax.rem(j + d, n_ep)
+        copy = remote(result.at[pl.ds(t * cap, cap)], out_ref.at[j],
+                      sems.at[5, d], sems.at[6, d], (t, a, m))
+        copy.start()
+        to_z.append(copy)
+    local.wait()
+    for copy in to_core + to_y + to_z:
+        copy.wait_send()
+    for copy in to_z:
+        copy.wait_recv()
+
+
+def send_back(ex, n_ep, n_my, cap):
+    rows, width = ex.shape
+    fb = width // n_my
+    return pl.pallas_call(
+        functools.partial(back_kernel, n_ep, n_my),
+        out_shape=jax.ShapeDtypeStruct((n_ep, cap, fb), ex.dtype),
+        in_specs=[pl.BlockSpec(memory_space=pltpu.VMEM)],
+        out_specs=pl.BlockSpec(memory_space=pl.ANY),
+        scratch_shapes=[
+            pltpu.VMEM((n_my // 2, rows, fb), ex.dtype),
+            pltpu.VMEM((n_my // 2, rows, fb), ex.dtype),
+            pltpu.VMEM((n_my // 2 - 1, rows, fb), ex.dtype),
+            pltpu.VMEM((rows, fb), ex.dtype),
+            pltpu.SemaphoreType.DMA((7, max(n_ep, n_my))),
+        ],
+        compiler_params=pltpu.CompilerParams(has_side_effects=True, collective_id=1),
+    )(ex)
+
+
 def row_scale(stream_f):
     partial_sq = jnp.sum(stream_f * stream_f, axis=1)
     row_total = lax.psum(partial_sq, "my")
@@ -212,14 +292,9 @@
     hidden = (jax.nn.silu(gate_proj) * up_proj).astype(jnp.bfloat16)
     expert_out = jnp.einsum("rsp,spd->rd", hidden, w_down, preferred_element_type=jnp.float32)
     expert_out = expert_out.reshape(slot_dev, slot_rows, D)
-    summed = lax.psum_scatter(
-        expert_out.astype(jnp.bfloat16), "my", scatter_dimension=2, tiled=True
-    )
-    sent_back = summed.reshape(slot_dev, ep_count, capacity, feat_block)
-    sent_back = jnp.transpose(sent_back, (1, 0, 2, 3))
-    returned = lax.all_to_all(sent_back, "ep", split_axis=0, concat_axis=0, tiled=True).reshape(
-        slot_total * capacity, feat_block
-    )
+    returned = send_back(
+        expert_out.reshape(slot_rows, D).astype(jnp.bfloat16), ep_count, lax.axis_size("my"), capacity
+    ).reshape(slot_total * capacity, feat_block)
     picked = returned[target].reshape(tok_rows, TOPK, feat_block).astype(jnp.float32)
     weights_norm = gate_probs / jnp.sum(gate_probs, axis=1, keepdims=True)
     mixed = jnp.sum(weights_norm[:, :, None] * picked, axis=1)

time: 328 us -> 297 us (0.905)
  Pallas kernels: 152 us -> 223 us
  waiting for transfers between devices: 65.5 us -> 0 us
  between operations: 14.2 us -> 0.85 us
  blocking collectives: 40.5 us -> 28.9 us
  starting transfers between devices: 11 us -> 0 us
    pallas_call x0 -> x1, Pallas kernels: none -> 70.8 us  [send_back(): pl.pallas_call(functools.partial(back_kernel, n_ep, n_my), out_shape=jax....]
    reduce_scatter x1 -> x0, waiting for transfers between devices: 51 us -> none  [shards(): lax.psum_scatter(expert_out.astype(jnp.bfloat16), 'my', scatter_dimension...]
    all_to_all x1 -> x0, waiting for transfers between devices: 14.5 us -> none  [shards(): lax.all_to_all(sent_back, 'ep', split_axis=0, concat_axis=0, tiled=True)]
    psum x2, blocking collectives: 40.5 us -> 28.9 us  [row_scale(): row_total = lax.psum(partial_sq, 'my')]
    all_to_all x1 -> x0, starting transfers between devices: 11 us -> none  [shards(): lax.all_to_all(sent_back, 'ep', split_axis=0, concat_axis=0, tiled=True)]
  transfers between devices with their start and end apart: 2 -> 0, of which waited for: 2 -> 0; matrix products, arithmetic and copies ran while one was open for 0% -> 0% of each run, Pallas kernels for 0% -> 0%
where the time goes in v8:
time: 297 us; the launch traced here: 295 us
  Pallas kernels  223 us (75%)
  blocking collectives  28.9 us (10%)
  matrix products  24.7 us (8%)
  local copies, waits for them, and re-layouts  13.1 us (4%)
  other arithmetic  4.43 us (1%)
    pallas_call x1, Pallas kernels, move_all(): pl.pallas_call(functools.partial(move_kernel, n_ep, n_mx, n_my, replicas)...  152 us
    pallas_call x1, Pallas kernels, send_back(): pl.pallas_call(functools.partial(back_kernel, n_ep, n_my), out_shape=jax....  70.8 us
    psum x2, blocking collectives, row_scale(): row_total = lax.psum(partial_sq, 'my')  28.9 us
    dot_general x1, matrix products, shards(): jnp.einsum('rsp,spd->rd', hidden, w_down, preferred_element_type=jnp.floa...  15.9 us
    dot_general x1, matrix products, shards(): jnp.einsum('rd,spd->rsp', tokens_in, w_up, preferred_element_type=jnp.flo...  6.92 us

profile of v8, /device:TPU:1, one launch (start us, length us, event | category | flops | bytes accessed | tf_op | source)
XLA Modules:
  0.0 295.2 jit_solution(18423869501904649775)
XLA Ops:
  0.6 0.0 copy-start
  0.6 0.0 copy-start.5
  0.7 0.9 copy.18
  1.6 0.1 eq.31
  1.7 1.1 reduce-window.6
  2.9 0.2 slice_reduce_fusion
  3.1 0.1 eq.27
  3.3 0.1 fusion.4
  3.4 0.7 broadcast_multiply_fusion
  4.0 0.1 copy.17
  4.2 0.1 mul.95
  4.4 2.4 scatter_custom_fusion
  6.9 0.0 copy-done
  6.9 0.0 copy-start.1
  6.9 0.0 copy-start.2
  6.9 1.8 multiply_reduce_fusion.2
  8.7 0.0 copy-start.3
  8.7 18.8 %psum.14 = f32[256]{0:T(256)S(1)} all-reduce(f32[256]{0:T(256)S(1)} %get-tuple-element.12), channel_id=1, replica_groups=mesh['ep'=16,'mx'=4,'my'=8] {'my'}, use_global_device_ids=true, to_apply=%region_2.0 | all-reduce | flops 256 | bytes 2048 | tf_op jit(solution)/shard_map/psum | solution.py:245
  27.5 0.0 copy-done.5
  27.5 0.1 multiply_convert_fusion.2
  27.6 3.3 %gather_fusion = bf16[768,256]{1,0:T(8,128)(2,1)} fusion(bf16[257,256]{1,0:T(8,128)(2,1)S(1)} %concatenate.3, s32[1024]{0:T(1024)S(1)} %pad_clamp_fusion.1), kind=kCustom, calls=%fused_computation | custom fusion | bytes 789504 | tf_op jit(solution)/shard_map/gather | solution.py:284
  30.9 0.0 copy-done.1
  30.9 0.9 copy.20.gate_ref
  31.8 0.0 copy-done.2
  31.8 0.9 copy.21.up_ref
  32.7 0.0 copy-done.3
  32.7 0.8 copy.22.down_ref
  33.5 152.4 %shard_map.113 = (bf16[16,48,2048]{2,1,0:T(8,128)(2,1)}, bf16[16,44,2048]{2,1,0:T(8,128)(2,1)}, bf16[16,44,2048]{2,1,0:T(8,128)(2,1)}, bf16[16,44,2048]{2,1,0:T(8,128)(2,1)}) custom-call(bf16[16,48,256]{2,1,0:T(8,128)(2,1)} %bitcast.25, bf16[8,44,512]{2,1,0:T(8,128)(2,1)} %copy.20.gate_ref, bf16[8,44,512]{2,1,0:T(8,128)(2,1)} %copy.21.up_ref, ...), custom_call_target="tpu_custom_call" | custom-call | tf_op jit(solution)/shard_map/pallas_call | solution.py:142
  186.0 6.9 %fusion.14 = f32[768,16,44]{0,2,1:T(8,128)} fusion(bf16[768,2048,1]{1,0,2:T(8,128)(2,1)} %bitcast.29, bf16[16,44,2048]{2,1,0:T(8,128)(2,1)} %get-tuple-element.8), kind=kOutput, calls=%fused_computation.46 | convolution fusion | flops 2214592512 | bytes 8192000 | tf_op jit(solution)/shard_map/rd,spd->rsp/dot_general | solution.py:291
  192.9 15.9 %bitcast_convert_fusion.ex_ref = bf16[768,2048]{1,0:T(8,128)(2,1)} fusion(bf16[16,44,2048]{2,1,0:T(8,128)(2,1)} %get-tuple-element.9, f32[768,16,44]{0,2,1:T(8,128)} %fusion.14, bf16[768,2048,1]{1,0,2:T(8,128)(2,1)} %bitcast.30, bf16[16,44,2048]{2,1,0:T(8,128)(2,1)} %get-tuple-element.7), kind=kOutput, calls=%fused_computation.3 | convolution fusion | flops 4434001920 | bytes 14221312 | tf_op jit(solution)/shard_map/rsp,spd->rd/dot_general | solution.py:293
  208.8 0.0 copy-start.4
  208.8 70.8 %shard_map.114 = bf16[16,48,256]{2,1,0:T(8,128)(2,1)} custom-call(bf16[768,2048]{1,0:T(8,128)(2,1)} %bitcast_convert_fusion.ex_ref), custom_call_target="tpu_custom_call" | custom-call | tf_op jit(solution)/shard_map/pallas_call | solution.py:227
  279.7 0.0 copy-start.6
  279.7 2.6 gather_fusion.1
  282.3 0.3 reshape.142
  282.6 0.0 copy-done.4
  282.6 0.1 copy.16
  282.8 0.7 multiply_reduce_fusion
  283.5 0.7 fusion.13
  284.2 0.1 multiply_reduce_fusion.1
  284.3 10.1 %psum.15 = f32[256]{0:T(256)S(1)} all-reduce(f32[256]{0:T(256)S(1)} %multiply_reduce_fusion.1), channel_id=1, replica_groups=mesh['ep'=16,'mx'=4,'my'=8] {'my'}, use_global_device_ids=true, to_apply=%region_9.10 | all-reduce | flops 256 | bytes 2048 | tf_op jit(solution)/shard_map/psum | solution.py:245
  294.4 0.0 copy-done.6
  294.4 0.8 multiply_convert_fusion.1
  (13 shorter events, 0.1 us)
Async XLA Ops:
  0.6 6.2 %copy-start = (bf16[256,2048]{1,0:T(8,128)(2,1)S(1)}, bf16[256,2048]{1,0:T(8,128)(2,1)}, u32[]{:S(2)}) copy-start(bf16[256,2048]{1,0:T(8,128)(2,1)} %param.10) | copy-start | bytes 3145732
  0.6 26.9 %copy-start.5 = (f32[256]{0:T(256)S(1)}, f32[256]{0:T(256)}, u32[]{:S(2)}) copy-start(f32[256]{0:T(256)} %param.13) | copy-start | bytes 3076
  6.9 24.0 %copy-start.1 = (bf16[8,44,512]{2,0,1:T(8,128)(2,1)S(1)}, bf16[8,44,512]{2,0,1:T(8,128)(2,1)}, u32[]{:S(2)}) copy-start(bf16[8,44,512]{2,0,1:T(8,128)(2,1)} %param.14) | copy-start | bytes 1081348
  6.9 24.9 %copy-start.2 = (bf16[8,44,512]{2,0,1:T(8,128)(2,1)S(1)}, bf16[8,44,512]{2,0,1:T(8,128)(2,1)}, u32[]{:S(2)}) copy-start(bf16[8,44,512]{2,0,1:T(8,128)(2,1)} %param.15) | copy-start | bytes 1081348
  8.7 24.0 %copy-start.3 = (bf16[8,44,512]{2,0,1:T(8,128)(2,1)S(1)}, bf16[8,44,512]{2,0,1:T(8,128)(2,1)}, u32[]{:S(2)}) copy-start(bf16[8,44,512]{2,0,1:T(8,128)(2,1)} %param.16) | copy-start | bytes 1081348
  208.8 73.7 %copy-start.4 = (f32[256,2]{0,1:T(2,128)S(1)}, f32[256,2]{0,1:T(2,128)}, u32[]{:S(2)}) copy-start(f32[256,2]{0,1:T(2,128)} %param.18) | copy-start | bytes 6148
  279.7 14.7 %copy-start.6 = (f32[256]{0:T(256)S(1)}, f32[256]{0:T(256)}, u32[]{:S(2)}) copy-start(f32[256]{0:T(256)} %param.19) | copy-start | bytes 3076

commit v9 on v8

--- a/solution.py
+++ b/solution.py
@@ -35,6 +35,13 @@
     wb = gate_ref.shape[2]
     cols_m = pl.ds(pl.multiple_of(m * fb, fb), fb)
     cols_a = pl.ds(pl.multiple_of(a * wb, wb), wb)
+    barrier = pltpu.get_barrier_semaphore()
+    peers = [(lax.rem(j + d, n_ep), a, m) for d in range(1, n_ep)]
+    peers += [(j, lax.rem(a + e, n_mx), m) for e in range(1, n_mx)]
+    peers += [(j, a, lax.rem(m + e, n_my)) for e in range(1, n_my)]
+    for peer in peers:
+        pl.semaphore_signal(barrier, inc=1, device_id=peer, device_id_type=MESH)
+    pl.semaphore_wait(barrier, len(peers))
     pending = []
     tok_local = pltpu.make_async_copy(packed_ref.at[j], tok_ref.at[j, :, cols_m], tok_sems.at[0, 0])
     tok_local.start()
@@ -156,7 +163,7 @@
             pltpu.SemaphoreType.DMA((3, max(n_mx, 4))),
             pltpu.SemaphoreType.DMA((3,)),
         ],
-        compiler_params=pltpu.CompilerParams(has_side_effects=True),
+        compiler_params=pltpu.CompilerParams(has_side_effects=True, collective_id=0),
     )(packed, gate_weight, up_weight, down_weight)
 
 

time: 297 us -> 284 us (0.956)
  Pallas kernels: 223 us -> 209 us
    pallas_call x1, Pallas kernels: 152 us -> 139 us  [move_all(): pl.pallas_call(functools.partial(move_kernel, n_ep, n_mx, n_my, replicas)...]
where the time goes in v9:
time: 284 us; the launch traced here: 283 us
  Pallas kernels  209 us (74%)
  blocking collectives  31 us (11%)
  matrix products  24.7 us (9%)
  local copies, waits for them, and re-layouts  13.1 us (5%)
  other arithmetic  4.43 us (2%)
    pallas_call x1, Pallas kernels, move_all(): pl.pallas_call(functools.partial(move_kernel, n_ep, n_mx, n_my, replicas)...  139 us
    pallas_call x1, Pallas kernels, send_back(): pl.pallas_call(functools.partial(back_kernel, n_ep, n_my), out_shape=jax....  70 us
    psum x2, blocking collectives, row_scale(): row_total = lax.psum(partial_sq, 'my')  31 us
    dot_general x1, matrix products, shards(): jnp.einsum('rsp,spd->rd', hidden, w_down, preferred_element_type=jnp.floa...  15.9 us
    dot_general x1, matrix products, shards(): jnp.einsum('rd,spd->rsp', tokens_in, w_up, preferred_element_type=jnp.flo...  6.92 us

profile of v9, /device:TPU:1, one launch (start us, length us, event | category | flops | bytes accessed | tf_op | source)
XLA Modules:
  0.0 283.0 jit_solution(17801641322770757149)
XLA Ops:
  0.6 0.0 copy-start
  0.6 0.0 copy-start.5
  0.7 0.9 copy.18
  1.6 0.1 eq.31
  1.7 1.1 reduce-window.6
  2.9 0.2 slice_reduce_fusion
  3.1 0.1 eq.27
  3.3 0.1 fusion.4
  3.4 0.7 broadcast_multiply_fusion
  4.0 0.1 copy.17
  4.2 0.1 mul.95
  4.4 2.4 scatter_custom_fusion
  6.9 0.0 copy-done
  6.9 0.0 copy-start.1
  6.9 0.0 copy-start.2
  6.9 1.8 multiply_reduce_fusion.2
  8.7 0.0 copy-start.3
  8.7 18.8 %psum.14 = f32[256]{0:T(256)S(1)} all-reduce(f32[256]{0:T(256)S(1)} %get-tuple-element.12), channel_id=1, replica_groups=mesh['ep'=16,'mx'=4,'my'=8] {'my'}, use_global_device_ids=true, to_apply=%region_2.0 | all-reduce | flops 256 | bytes 2048 | tf_op jit(solution)/shard_map/psum | solution.py:252
  27.5 0.0 copy-done.5
  27.5 0.1 multiply_convert_fusion.2
  27.6 3.3 %gather_fusion = bf16[768,256]{1,0:T(8,128)(2,1)} fusion(bf16[257,256]{1,0:T(8,128)(2,1)S(1)} %concatenate.3, s32[1024]{0:T(1024)S(1)} %pad_clamp_fusion.1), kind=kCustom, calls=%fused_computation | custom fusion | bytes 789504 | tf_op jit(solution)/shard_map/gather | solution.py:291
  30.9 0.0 copy-done.1
  30.9 0.9 copy.20.gate_ref
  31.8 0.0 copy-done.2
  31.8 0.9 copy.21.up_ref
  32.7 0.0 copy-done.3
  32.7 0.8 copy.22.down_ref
  33.5 139.0 %shard_map.113 = (bf16[16,48,2048]{2,1,0:T(8,128)(2,1)}, bf16[16,44,2048]{2,1,0:T(8,128)(2,1)}, bf16[16,44,2048]{2,1,0:T(8,128)(2,1)}, bf16[16,44,2048]{2,1,0:T(8,128)(2,1)}) custom-call(bf16[16,48,256]{2,1,0:T(8,128)(2,1)} %bitcast.25, bf16[8,44,512]{2,1,0:T(8,128)(2,1)} %copy.20.gate_ref, bf16[8,44,512]{2,1,0:T(8,128)(2,1)} %copy.21.up_ref, ...), custom_call_target="tpu_custom_call" | custom-call | tf_op jit(solution)/shard_map/pallas_call | solution.py:149
  172.6 6.9 %fusion.14 = f32[768,16,44]{0,2,1:T(8,128)} fusion(bf16[768,2048,1]{1,0,2:T(8,128)(2,1)} %bitcast.29, bf16[16,44,2048]{2,1,0:T(8,128)(2,1)} %get-tuple-element.8), kind=kOutput, calls=%fused_computation.46 | convolution fusion | flops 2214592512 | bytes 8192000 | tf_op jit(solution)/shard_map/rd,spd->rsp/dot_general | solution.py:298
  179.5 15.9 %bitcast_convert_fusion.ex_ref = bf16[768,2048]{1,0:T(8,128)(2,1)} fusion(bf16[16,44,2048]{2,1,0:T(8,128)(2,1)} %get-tuple-element.9, f32[768,16,44]{0,2,1:T(8,128)} %fusion.14, bf16[768,2048,1]{1,0,2:T(8,128)(2,1)} %bitcast.30, bf16[16,44,2048]{2,1,0:T(8,128)(2,1)} %get-tuple-element.7), kind=kOutput, calls=%fused_computation.3 | convolution fusion | flops 4434001920 | bytes 14221312 | tf_op jit(solution)/shard_map/rsp,spd->rd/dot_general | solution.py:300
  195.4 0.0 copy-start.4
  195.4 70.0 %shard_map.114 = bf16[16,48,256]{2,1,0:T(8,128)(2,1)} custom-call(bf16[768,2048]{1,0:T(8,128)(2,1)} %bitcast_convert_fusion.ex_ref), custom_call_target="tpu_custom_call" | custom-call | tf_op jit(solution)/shard_map/pallas_call | solution.py:234
  265.5 0.0 copy-start.6
  265.5 2.6 gather_fusion.1
  268.1 0.3 reshape.142
  268.4 0.0 copy-done.4
  268.4 0.1 copy.16
  268.6 0.7 multiply_reduce_fusion
  269.3 0.7 fusion.13
  270.0 0.1 multiply_reduce_fusion.1
  270.1 12.2 %psum.15 = f32[256]{0:T(256)S(1)} all-reduce(f32[256]{0:T(256)S(1)} %multiply_reduce_fusion.1), channel_id=1, replica_groups=mesh['ep'=16,'mx'=4,'my'=8] {'my'}, use_global_device_ids=true, to_apply=%region_9.10 | all-reduce | flops 256 | bytes 2048 | tf_op jit(solution)/shard_map/psum | solution.py:252
  282.3 0.0 copy-done.6
  282.3 0.8 multiply_convert_fusion.1
  (13 shorter events, 0.1 us)
Async XLA Ops:
  0.6 6.2 %copy-start = (bf16[256,2048]{1,0:T(8,128)(2,1)S(1)}, bf16[256,2048]{1,0:T(8,128)(2,1)}, u32[]{:S(2)}) copy-start(bf16[256,2048]{1,0:T(8,128)(2,1)} %param.10) | copy-start | bytes 3145732
  0.6 26.9 %copy-start.5 = (f32[256]{0:T(256)S(1)}, f32[256]{0:T(256)}, u32[]{:S(2)}) copy-start(f32[256]{0:T(256)} %param.13) | copy-start | bytes 3076
  6.9 24.0 %copy-start.1 = (bf16[8,44,512]{2,0,1:T(8,128)(2,1)S(1)}, bf16[8,44,512]{2,0,1:T(8,128)(2,1)}, u32[]{:S(2)}) copy-start(bf16[8,44,512]{2,0,1:T(8,128)(2,1)} %param.14) | copy-start | bytes 1081348
  6.9 24.9 %copy-start.2 = (bf16[8,44,512]{2,0,1:T(8,128)(2,1)S(1)}, bf16[8,44,512]{2,0,1:T(8,128)(2,1)}, u32[]{:S(2)}) copy-start(bf16[8,44,512]{2,0,1:T(8,128)(2,1)} %param.15) | copy-start | bytes 1081348
  8.7 24.0 %copy-start.3 = (bf16[8,44,512]{2,0,1:T(8,128)(2,1)S(1)}, bf16[8,44,512]{2,0,1:T(8,128)(2,1)}, u32[]{:S(2)}) copy-start(bf16[8,44,512]{2,0,1:T(8,128)(2,1)} %param.16) | copy-start | bytes 1081348
  195.4 72.9 %copy-start.4 = (f32[256,2]{0,1:T(2,128)S(1)}, f32[256,2]{0,1:T(2,128)}, u32[]{:S(2)}) copy-start(f32[256,2]{0,1:T(2,128)} %param.18) | copy-start | bytes 6148
  265.5 16.8 %copy-start.6 = (f32[256]{0:T(256)S(1)}, f32[256]{0:T(256)}, u32[]{:S(2)}) copy-start(f32[256]{0:T(256)} %param.19) | copy-start | bytes 3076

commit v10 on v9

--- a/solution.py
+++ b/solution.py
@@ -247,9 +247,49 @@
     )(ex)
 
 
-def row_scale(stream_f):
+def sum_kernel(n_my, x_ref, o_ref, slots, send, recv):
+    j = lax.axis_index("ep")
+    a = lax.axis_index("mx")
+    m = lax.axis_index("my")
+    barrier = pltpu.get_barrier_semaphore()
+    for e in range(1, n_my):
+        pl.semaphore_signal(barrier, inc=1, device_id=(j, a, lax.rem(m + e, n_my)), device_id_type=MESH)
+    pl.semaphore_wait(barrier, n_my - 1)
+    slots[m] = x_ref[...]
+    copies = []
+    for e in range(1, n_my):
+        b = lax.rem(m + e, n_my)
+        copy = remote(x_ref, slots.at[m], send.at[e], recv.at[e], (j, a, b))
+        copy.start()
+        copies.append(copy)
+    for copy in copies:
+        copy.wait_send()
+    for copy in copies:
+        copy.wait_recv()
+    o_ref[...] = jnp.sum(slots[...], axis=0)
+
+
+def sum_over_my(values, kernel_id):
+    n_my = lax.axis_size("my")
+    row = values.reshape(1, -1)
+    total = pl.pallas_call(
+        functools.partial(sum_kernel, n_my),
+        out_shape=jax.ShapeDtypeStruct(row.shape, row.dtype),
+        in_specs=[pl.BlockSpec(memory_space=pltpu.VMEM)],
+        out_specs=pl.BlockSpec(memory_space=pltpu.VMEM),
+        scratch_shapes=[
+            pltpu.VMEM((n_my,) + row.shape, row.dtype),
+            pltpu.SemaphoreType.DMA((n_my,)),
+            pltpu.SemaphoreType.DMA((n_my,)),
+        ],
+        compiler_params=pltpu.CompilerParams(has_side_effects=True, collective_id=kernel_id),
+    )(row)
+    return total.reshape(values.shape)
+
+
+def row_scale(stream_f, kernel_id):
     partial_sq = jnp.sum(stream_f * stream_f, axis=1)
-    row_total = lax.psum(partial_sq, "my")
+    row_total = sum_over_my(partial_sq, kernel_id)
     return lax.rsqrt(row_total / D + EPSILON)
 
 
@@ -278,7 +318,7 @@
     projected = jnp.dot(context, out_weight, preferred_element_type=jnp.float32)
     stream = (projected + resid_in.astype(jnp.float32)).astype(jnp.bfloat16)
     stream_f = stream.astype(jnp.float32)
-    normed = (stream_f * row_scale(stream_f)[:, None] * norm_gain[None, :]).astype(jnp.bfloat16)
+    normed = (stream_f * row_scale(stream_f, 2)[:, None] * norm_gain[None, :]).astype(jnp.bfloat16)
     chosen = routes.reshape(-1)
     onehot = (chosen[:, None] == jnp.arange(EXPERTS, dtype=jnp.int32)[None, :]).astype(jnp.int32)
     before = jnp.cumsum(onehot, axis=0) - onehot
@@ -306,7 +346,7 @@
     weights_norm = gate_probs / jnp.sum(gate_probs, axis=1, keepdims=True)
     mixed = jnp.sum(weights_norm[:, :, None] * picked, axis=1)
     updated = stream_f + mixed
-    normed_out = (updated * row_scale(updated)[:, None] * final_gain[None, :]).astype(jnp.bfloat16)
+    normed_out = (updated * row_scale(updated, 3)[:, None] * final_gain[None, :]).astype(jnp.bfloat16)
     return (normed_out, updated.astype(jnp.bfloat16))
 
 

time: 284 us -> 273 us (0.961)
  blocking collectives: 31 us -> 0 us
  Pallas kernels: 209 us -> 227 us
    psum x2 -> x0, blocking collectives: 31 us -> none  [row_scale(): row_total = lax.psum(partial_sq, 'my')]
    pallas_call x0 -> x2, Pallas kernels: none -> 21 us  [sum_over_my(): pl.pallas_call(functools.partial(sum_kernel, n_my), out_shape=jax.ShapeDt...]
    pallas_call x1, Pallas kernels: 70 us -> 54.2 us  [send_back(): pl.pallas_call(functools.partial(back_kernel, n_ep, n_my), out_shape=jax....]
    pallas_call x1, Pallas kernels: 139 us -> 151 us  [move_all(): pl.pallas_call(functools.partial(move_kernel, n_ep, n_mx, n_my, replicas)...]
where the time goes in v10:
time: 273 us; the launch traced here: 272 us
  Pallas kernels  227 us (83%)
  matrix products  25.2 us (9%)
  local copies, waits for them, and re-layouts  13.1 us (5%)
  other arithmetic  6.35 us (2%)
    pallas_call x1, Pallas kernels, move_all(): pl.pallas_call(functools.partial(move_kernel, n_ep, n_mx, n_my, replicas)...  151 us
    pallas_call x1, Pallas kernels, send_back(): pl.pallas_call(functools.partial(back_kernel, n_ep, n_my), out_shape=jax....  54.2 us
    pallas_call x2, Pallas kernels, sum_over_my(): pl.pallas_call(functools.partial(sum_kernel, n_my), out_shape=jax.ShapeDt...  21 us
    dot_general x1, matrix products, shards(): jnp.einsum('rsp,spd->rd', hidden, w_down, preferred_element_type=jnp.floa...  15.9 us
    dot_general x1, matrix products, shards(): jnp.einsum('rd,spd->rsp', tokens_in, w_up, preferred_element_type=jnp.flo...  6.92 us

profile of v10, /device:TPU:1, one launch (start us, length us, event | category | flops | bytes accessed | tf_op | source)
XLA Modules:
  0.0 272.2 jit_solution(1907201437092330012)
XLA Ops:
  0.6 0.0 copy-start
  0.6 0.0 copy-start.5
  0.7 0.9 copy.18
  1.6 0.1 eq.31
  1.7 1.1 reduce-window.6
  2.9 0.2 slice_reduce_fusion
  3.1 0.1 eq.27
  3.3 0.1 fusion.4
  3.4 0.7 broadcast_multiply_fusion
  4.0 0.1 copy.17
  4.2 0.1 mul.95
  4.4 2.4 scatter_custom_fusion
  6.9 0.0 copy-done
  6.9 0.0 copy-start.1
  6.9 0.0 copy-start.2
  6.9 2.4 multiply_reduce_fusion.2
  9.3 0.0 copy-start.3
  9.3 13.8 %shard_map.113 = f32[1,256]{1,0:T(1,128)} custom-call(f32[1,256]{1,0:T(1,128)} %bitcast.33), custom_call_target="tpu_custom_call" | custom-call | tf_op jit(solution)/shard_map/pallas_call | solution.py:275
  23.1 0.7 add_rsqrt_fusion.1
  23.8 0.0 copy-done.5
  23.8 0.1 multiply_convert_fusion.2
  23.9 3.3 %gather_fusion = bf16[768,256]{1,0:T(8,128)(2,1)} fusion(bf16[257,256]{1,0:T(8,128)(2,1)S(1)} %concatenate.3, s32[1024]{0:T(1024)S(1)} %pad_clamp_fusion.1), kind=kCustom, calls=%fused_computation | custom fusion | bytes 789504 | tf_op jit(solution)/shard_map/gather | solution.py:331
  27.2 0.0 copy-done.1
  27.2 0.9 copy.20.gate_ref
  28.1 0.0 copy-done.2
  28.1 0.9 copy.21.up_ref
  29.0 0.0 copy-done.3
  29.0 0.8 copy.22.down_ref
  29.8 151.4 %shard_map.114 = (bf16[16,48,2048]{2,1,0:T(8,128)(2,1)}, bf16[16,44,2048]{2,1,0:T(8,128)(2,1)}, bf16[16,44,2048]{2,1,0:T(8,128)(2,1)}, bf16[16,44,2048]{2,1,0:T(8,128)(2,1)}) custom-call(bf16[16,48,256]{2,1,0:T(8,128)(2,1)} %bitcast.29, bf16[8,44,512]{2,1,0:T(8,128)(2,1)} %copy.20.gate_ref, bf16[8,44,512]{2,1,0:T(8,128)(2,1)} %copy.21.up_ref, ...), custom_call_target="tpu_custom_call" | custom-call | tf_op jit(solution)/shard_map/pallas_call | solution.py:149
  181.2 6.9 %fusion.14 = f32[768,16,44]{0,2,1:T(8,128)} fusion(bf16[768,2048,1]{1,0,2:T(8,128)(2,1)} %bitcast.37, bf16[16,44,2048]{2,1,0:T(8,128)(2,1)} %get-tuple-element.8), kind=kOutput, calls=%fused_computation.46 | convolution fusion | flops 2214592512 | bytes 8192000 | tf_op jit(solution)/shard_map/rd,spd->rsp/dot_general | solution.py:338
  188.2 15.9 %bitcast_convert_fusion.ex_ref = bf16[768,2048]{1,0:T(8,128)(2,1)} fusion(bf16[16,44,2048]{2,1,0:T(8,128)(2,1)} %get-tuple-element.9, f32[768,16,44]{0,2,1:T(8,128)} %fusion.14, bf16[768,2048,1]{1,0,2:T(8,128)(2,1)} %bitcast.38, bf16[16,44,2048]{2,1,0:T(8,128)(2,1)} %get-tuple-element.7), kind=kOutput, calls=%fused_computation.3 | convolution fusion | flops 4434001920 | bytes 14221312 | tf_op jit(solution)/shard_map/rsp,spd->rd/dot_general | solution.py:340
  204.1 0.0 copy-start.4
  204.1 54.2 %shard_map.115 = bf16[16,48,256]{2,1,0:T(8,128)(2,1)} custom-call(bf16[768,2048]{1,0:T(8,128)(2,1)} %bitcast_convert_fusion.ex_ref), custom_call_target="tpu_custom_call" | custom-call | tf_op jit(solution)/shard_map/pallas_call | solution.py:234
  258.3 0.0 copy-start.6
  258.3 2.6 gather_fusion.1
  260.9 0.3 reshape.174
  261.2 0.0 copy-done.4
  261.3 0.1 copy.16
  261.4 0.7 multiply_reduce_fusion
  262.1 0.7 fusion.13
  262.8 0.7 multiply_reduce_fusion.1
  263.5 7.2 %shard_map.116 = f32[1,256]{1,0:T(1,128)} custom-call(f32[1,256]{1,0:T(1,128)} %bitcast.36), custom_call_target="tpu_custom_call" | custom-call | tf_op jit(solution)/shard_map/pallas_call | solution.py:275
  270.7 0.7 add_rsqrt_fusion
  271.4 0.0 copy-done.6
  271.4 0.8 multiply_convert_fusion.1
  (11 shorter events, 0.1 us)
Async XLA Ops:
  0.6 6.2 %copy-start = (bf16[256,2048]{1,0:T(8,128)(2,1)S(1)}, bf16[256,2048]{1,0:T(8,128)(2,1)}, u32[]{:S(2)}) copy-start(bf16[256,2048]{1,0:T(8,128)(2,1)} %param.10) | copy-start | bytes 3145732
  0.6 23.1 %copy-start.5 = (f32[256]{0:T(256)S(1)}, f32[256]{0:T(256)}, u32[]{:S(2)}) copy-start(f32[256]{0:T(256)} %param.13) | copy-start | bytes 3076
  6.9 20.3 %copy-start.1 = (bf16[8,44,512]{2,0,1:T(8,128)(2,1)S(1)}, bf16[8,44,512]{2,0,1:T(8,128)(2,1)}, u32[]{:S(2)}) copy-start(bf16[8,44,512]{2,0,1:T(8,128)(2,1)} %param.14) | copy-start | bytes 1081348
  6.9 21.2 %copy-start.2 = (bf16[8,44,512]{2,0,1:T(8,128)(2,1)S(1)}, bf16[8,44,512]{2,0,1:T(8,128)(2,1)}, u32[]{:S(2)}) copy-start(bf16[8,44,512]{2,0,1:T(8,128)(2,1)} %param.15) | copy-start | bytes 1081348
  9.3 19.7 %copy-start.3 = (bf16[8,44,512]{2,0,1:T(8,128)(2,1)S(1)}, bf16[8,44,512]{2,0,1:T(8,128)(2,1)}, u32[]{:S(2)}) copy-start(bf16[8,44,512]{2,0,1:T(8,128)(2,1)} %param.16) | copy-start | bytes 1081348
  204.1 57.1 %copy-start.4 = (f32[256,2]{0,1:T(2,128)S(1)}, f32[256,2]{0,1:T(2,128)}, u32[]{:S(2)}) copy-start(f32[256,2]{0,1:T(2,128)} %param.18) | copy-start | bytes 6148
  258.3 13.1 %copy-start.6 = (f32[256]{0:T(256)S(1)}, f32[256]{0:T(256)}, u32[]{:S(2)}) copy-start(f32[256]{0:T(256)} %param.19) | copy-start | bytes 3076

commit v11 on v10

--- a/solution.py
+++ b/solution.py
@@ -43,14 +43,6 @@
         pl.semaphore_signal(barrier, inc=1, device_id=peer, device_id_type=MESH)
     pl.semaphore_wait(barrier, len(peers))
     pending = []
-    tok_local = pltpu.make_async_copy(packed_ref.at[j], tok_ref.at[j, :, cols_m], tok_sems.at[0, 0])
-    tok_local.start()
-    tok_z = []
-    for d in range(1, n_ep):
-        t = lax.rem(j + d, n_ep)
-        copy = remote(packed_ref.at[t], tok_ref.at[j, :, cols_m], tok_sems.at[1, d], tok_sems.at[2, d], (t, a, m))
-        copy.start()
-        tok_z.append(copy)
     weights = (gate_ref, up_ref, down_ref)
     outs = (gate_out, up_out, down_out)
 
@@ -84,17 +76,15 @@
         return forward
 
     local, direct = start_direct(0)
-    tok_local.wait()
-    for copy in tok_z:
-        copy.wait_recv()
-    pending.extend(tok_z)
+    tok_local = pltpu.make_async_copy(packed_ref.at[j], tok_ref.at[j, :, cols_m], tok_sems.at[0, 0])
+    tok_local.start()
+    tok_z = []
+    for d in range(1, n_ep):
+        t = lax.rem(j + d, n_ep)
+        copy = remote(packed_ref.at[t], tok_ref.at[j, :, cols_m], tok_sems.at[1, d], tok_sems.at[2, d], (t, a, m))
+        copy.start()
+        tok_z.append(copy)
     tok_my = []
-    for e in range(1, n_my):
-        b = lax.rem(m + e, n_my)
-        copy = remote(tok_ref.at[:, :, cols_m], tok_ref.at[:, :, cols_m], tok_sems.at[3, e], tok_sems.at[4, e], (j, a, b))
-        copy.start()
-        tok_my.append(copy)
-    pending.extend(tok_my)
     x_copies = []
     for k in range(3):
         local.wait()
@@ -136,6 +126,17 @@
                               send_x.at[k, e], recv_x.at[k, e], (j, b, m))
                 copy.start()
                 x_copies.append(copy)
+        if k == 0:
+            tok_local.wait()
+            for copy in tok_z:
+                copy.wait_recv()
+            pending.extend(tok_z)
+            for e in range(1, n_my):
+                b = lax.rem(m + e, n_my)
+                copy = remote(tok_ref.at[:, :, cols_m], tok_ref.at[:, :, cols_m], tok_sems.at[3, e], tok_sems.at[4, e], (j, a, b))
+                copy.start()
+                tok_my.append(copy)
+            pending.extend(tok_my)
     pending.extend(x_copies)
     for copy in pending:
         copy.wait_send()

time: 273 us -> 270 us (0.989)
  Pallas kernels: 227 us -> 224 us
    pallas_call x1, Pallas kernels: 151 us -> 144 us  [move_all(): pl.pallas_call(functools.partial(move_kernel, n_ep, n_mx, n_my, replicas)...]
    pallas_call x1, Pallas kernels: 54.2 us -> 58.4 us  [send_back(): pl.pallas_call(functools.partial(back_kernel, n_ep, n_my), out_shape=jax....]
where the time goes in v11:
time: 270 us
  Pallas kernels  224 us (83%)
  matrix products  25.2 us (9%)
  local copies, waits for them, and re-layouts  13.1 us (5%)
  other arithmetic  6.35 us (2%)
    pallas_call x1, Pallas kernels, move_all(): pl.pallas_call(functools.partial(move_kernel, n_ep, n_mx, n_my, replicas)...  144 us
    pallas_call x1, Pallas kernels, send_back(): pl.pallas_call(functools.partial(back_kernel, n_ep, n_my), out_shape=jax....  58.4 us
    pallas_call x2, Pallas kernels, sum_over_my(): pl.pallas_call(functools.partial(sum_kernel, n_my), out_shape=jax.ShapeDt...  21.7 us
    dot_general x1, matrix products, shards(): jnp.einsum('rsp,spd->rd', hidden, w_down, preferred_element_type=jnp.floa...  15.9 us
    dot_general x1, matrix products, shards(): jnp.einsum('rd,spd->rsp', tokens_in, w_up, preferred_element_type=jnp.flo...  6.91 us

profile of v11, /device:TPU:1, one launch (start us, length us, event | category | flops | bytes accessed | tf_op | source)
XLA Modules:
  0.0 269.5 jit_solution(10863302366528745934)
XLA Ops:
  0.6 0.0 copy-start
  0.6 0.0 copy-start.5
  0.7 0.9 copy.18
  1.6 0.1 eq.31
  1.7 1.1 reduce-window.6
  2.9 0.2 slice_reduce_fusion
  3.1 0.1 eq.27
  3.3 0.1 fusion.4
  3.4 0.7 broadcast_multiply_fusion
  4.0 0.1 copy.17
  4.2 0.1 mul.95
  4.4 2.4 scatter_custom_fusion
  6.9 0.0 copy-done
  6.9 0.0 copy-start.1
  6.9 0.0 copy-start.2
  6.9 2.4 multiply_reduce_fusion.2
  9.3 0.0 copy-start.3
  9.3 13.8 %shard_map.113 = f32[1,256]{1,0:T(1,128)} custom-call(f32[1,256]{1,0:T(1,128)} %bitcast.33), custom_call_target="tpu_custom_call" | custom-call | tf_op jit(solution)/shard_map/pallas_call | solution.py:276
  23.1 0.7 add_rsqrt_fusion.1
  23.8 0.0 copy-done.5
  23.8 0.1 multiply_convert_fusion.2
  23.9 3.3 %gather_fusion = bf16[768,256]{1,0:T(8,128)(2,1)} fusion(bf16[257,256]{1,0:T(8,128)(2,1)S(1)} %concatenate.3, s32[1024]{0:T(1024)S(1)} %pad_clamp_fusion.1), kind=kCustom, calls=%fused_computation | custom fusion | bytes 789504 | tf_op jit(solution)/shard_map/gather | solution.py:332
  27.2 0.0 copy-done.1
  27.2 0.9 copy.20.gate_ref
  28.1 0.0 copy-done.2
  28.1 0.9 copy.21.up_ref
  29.0 0.0 copy-done.3
  29.0 0.8 copy.22.down_ref
  29.8 143.9 %shard_map.114 = (bf16[16,48,2048]{2,1,0:T(8,128)(2,1)}, bf16[16,44,2048]{2,1,0:T(8,128)(2,1)}, bf16[16,44,2048]{2,1,0:T(8,128)(2,1)}, bf16[16,44,2048]{2,1,0:T(8,128)(2,1)}) custom-call(bf16[16,48,256]{2,1,0:T(8,128)(2,1)} %bitcast.29, bf16[8,44,512]{2,1,0:T(8,128)(2,1)} %copy.20.gate_ref, bf16[8,44,512]{2,1,0:T(8,128)(2,1)} %copy.21.up_ref, ...), custom_call_target="tpu_custom_call" | custom-call | tf_op jit(solution)/shard_map/pallas_call | solution.py:150
  173.8 6.9 %fusion.14 = f32[768,16,44]{0,2,1:T(8,128)} fusion(bf16[768,2048,1]{1,0,2:T(8,128)(2,1)} %bitcast.37, bf16[16,44,2048]{2,1,0:T(8,128)(2,1)} %get-tuple-element.8), kind=kOutput, calls=%fused_computation.46 | convolution fusion | flops 2214592512 | bytes 8192000 | tf_op jit(solution)/shard_map/rd,spd->rsp/dot_general | solution.py:339
  180.7 15.9 %bitcast_convert_fusion.ex_ref = bf16[768,2048]{1,0:T(8,128)(2,1)} fusion(bf16[16,44,2048]{2,1,0:T(8,128)(2,1)} %get-tuple-element.9, f32[768,16,44]{0,2,1:T(8,128)} %fusion.14, bf16[768,2048,1]{1,0,2:T(8,128)(2,1)} %bitcast.38, bf16[16,44,2048]{2,1,0:T(8,128)(2,1)} %get-tuple-element.7), kind=kOutput, calls=%fused_computation.3 | convolution fusion | flops 4434001920 | bytes 14221312 | tf_op jit(solution)/shard_map/rsp,spd->rd/dot_general | solution.py:341
  196.6 0.0 copy-start.4
  196.6 58.4 %shard_map.115 = bf16[16,48,256]{2,1,0:T(8,128)(2,1)} custom-call(bf16[768,2048]{1,0:T(8,128)(2,1)} %bitcast_convert_fusion.ex_ref), custom_call_target="tpu_custom_call" | custom-call | tf_op jit(solution)/shard_map/pallas_call | solution.py:235
  255.0 0.0 copy-start.6
  255.1 2.6 gather_fusion.1
  257.7 0.3 reshape.174
  257.9 0.0 copy-done.4
  258.0 0.1 copy.16
  258.1 0.7 multiply_reduce_fusion
  258.8 0.7 fusion.13
  259.5 0.7 multiply_reduce_fusion.1
  260.2 7.8 %shard_map.116 = f32[1,256]{1,0:T(1,128)} custom-call(f32[1,256]{1,0:T(1,128)} %bitcast.36), custom_call_target="tpu_custom_call" | custom-call | tf_op jit(solution)/shard_map/pallas_call | solution.py:276
  268.1 0.7 add_rsqrt_fusion
  268.7 0.0 copy-done.6
  268.7 0.8 multiply_convert_fusion.1
  (11 shorter events, 0.1 us)
Async XLA Ops:
  0.6 6.2 %copy-start = (bf16[256,2048]{1,0:T(8,128)(2,1)S(1)}, bf16[256,2048]{1,0:T(8,128)(2,1)}, u32[]{:S(2)}) copy-start(bf16[256,2048]{1,0:T(8,128)(2,1)} %param.10) | copy-start | bytes 3145732
  0.6 23.1 %copy-start.5 = (f32[256]{0:T(256)S(1)}, f32[256]{0:T(256)}, u32[]{:S(2)}) copy-start(f32[256]{0:T(256)} %param.13) | copy-start | bytes 3076
  6.9 20.3 %copy-start.1 = (bf16[8,44,512]{2,0,1:T(8,128)(2,1)S(1)}, bf16[8,44,512]{2,0,1:T(8,128)(2,1)}, u32[]{:S(2)}) copy-start(bf16[8,44,512]{2,0,1:T(8,128)(2,1)} %param.14) | copy-start | bytes 1081348
  6.9 21.2 %copy-start.2 = (bf16[8,44,512]{2,0,1:T(8,128)(2,1)S(1)}, bf16[8,44,512]{2,0,1:T(8,128)(2,1)}, u32[]{:S(2)}) copy-start(bf16[8,44,512]{2,0,1:T(8,128)(2,1)} %param.15) | copy-start | bytes 1081348
  9.3 19.7 %copy-start.3 = (bf16[8,44,512]{2,0,1:T(8,128)(2,1)S(1)}, bf16[8,44,512]{2,0,1:T(8,128)(2,1)}, u32[]{:S(2)}) copy-start(bf16[8,44,512]{2,0,1:T(8,128)(2,1)} %param.16) | copy-start | bytes 1081348
  196.6 61.3 %copy-start.4 = (f32[256,2]{0,1:T(2,128)S(1)}, f32[256,2]{0,1:T(2,128)}, u32[]{:S(2)}) copy-start(f32[256,2]{0,1:T(2,128)} %param.18) | copy-start | bytes 6148
  255.0 13.7 %copy-start.6 = (f32[256]{0:T(256)S(1)}, f32[256]{0:T(256)}, u32[]{:S(2)}) copy-start(f32[256]{0:T(256)} %param.19) | copy-start | bytes 3076

commit v12 on v11

--- a/solution.py
+++ b/solution.py
@@ -200,33 +200,55 @@
     for i in range(chips):
         own = ex_ref[:, cols(core + 2 * i)].astype(jnp.float32)
         chip_part[i] = (own + rx_core[i].astype(jnp.float32)).astype(chip_part.dtype)
+    rows = result.shape[0]
+    half_rows = rows // 2
+    half_slots = n_ep // 2
     to_y = []
-    for e in range(1, chips):
-        other = lax.rem(y + e, chips)
-        copy = remote(chip_part.at[other], rx_y.at[e - 1],
-                      sems.at[2, e], sems.at[3, e], (j, a, other * 2 + core))
-        copy.start()
-        to_y.append(copy)
-    for copy in to_y:
-        copy.wait_recv()
-    total = chip_part[y].astype(jnp.float32)
-    for e in range(1, chips):
-        total = total + rx_y[e - 1].astype(jnp.float32)
-    result[...] = total.astype(result.dtype)
-    local = pltpu.make_async_copy(result.at[pl.ds(j * cap, cap)], out_ref.at[j], sems.at[4, 0])
-    local.start()
+    for h in range(2):
+        part = pl.ds(h * half_rows, half_rows)
+        for e in range(1, chips):
+            other = lax.rem(y + e, chips)
+            copy = remote(chip_part.at[other, part], rx_y.at[e - 1, part],
+                          sems.at[2 + 2 * h, e], sems.at[3 + 2 * h, e], (j, a, other * 2 + core))
+            copy.start()
+            to_y.append(copy)
     to_z = []
-    for d in range(1, n_ep):
-        t = lax.rem(j + d, n_ep)
-        copy = remote(result.at[pl.ds(t * cap, cap)], out_ref.at[j],
-                      sems.at[5, d], sems.at[6, d], (t, a, m))
-        copy.start()
-        to_z.append(copy)
-    local.wait()
-    for copy in to_core + to_y + to_z:
+    for h in range(2):
+        part = pl.ds(h * half_rows, half_rows)
+        for copy in to_y[h * (chips - 1):(h + 1) * (chips - 1)]:
+            copy.wait_recv()
+        total = chip_part[y, part].astype(jnp.float32)
+        for e in range(1, chips):
+            total = total + rx_y[e - 1, part].astype(jnp.float32)
+        result[part] = total.astype(result.dtype)
+        for t in range(h * half_slots, (h + 1) * half_slots):
+            rows_t = result.at[pl.ds(t * cap, cap)]
+
+            @pl.when(t == j)
+            def _():
+                local = pltpu.make_async_copy(rows_t, out_ref.at[j], sems.at[6, t])
+                local.start()
+                local.wait()
+
+            copy = remote(rows_t, out_ref.at[j], sems.at[7, t], sems.at[8, j], (t, a, m))
+
+            @pl.when(t != j)
+            def _():
+                copy.start()
+
+            to_z.append((t, copy))
+    for copy in to_core + to_y:
         copy.wait_send()
-    for copy in to_z:
-        copy.wait_recv()
+    for t, copy in to_z:
+        @pl.when(t != j)
+        def _():
+            copy.wait_send()
+    for s in range(n_ep):
+        incoming = remote(result.at[pl.ds(0, cap)], out_ref.at[s], sems.at[7, s], sems.at[8, s], (s, a, m))
+
+        @pl.when(s != j)
+        def _():
+            incoming.wait_recv()
 
 
 def send_back(ex, n_ep, n_my, cap):
@@ -242,7 +264,7 @@
             pltpu.VMEM((n_my // 2, rows, fb), ex.dtype),
             pltpu.VMEM((n_my // 2 - 1, rows, fb), ex.dtype),
             pltpu.VMEM((rows, fb), ex.dtype),
-            pltpu.SemaphoreType.DMA((7, max(n_ep, n_my))),
+            pltpu.SemaphoreType.DMA((9, max(n_ep, n_my))),
         ],
         compiler_params=pltpu.CompilerParams(has_side_effects=True, collective_id=1),
     )(ex)

time: 270 us -> 267 us (0.989)
  Pallas kernels: 224 us -> 221 us
    pallas_call x1, Pallas kernels: 58.4 us -> 55.1 us  [send_back(): pl.pallas_call(functools.partial(back_kernel, n_ep, n_my), out_shape=jax....]
where the time goes in v12:
time: 267 us; the launch traced here: 266 us
  Pallas kernels  221 us (83%)
  matrix products  25.2 us (9%)
  local copies, waits for them, and re-layouts  13.1 us (5%)
  other arithmetic  6.35 us (2%)
    pallas_call x1, Pallas kernels, move_all(): pl.pallas_call(functools.partial(move_kernel, n_ep, n_mx, n_my, replicas)...  144 us
    pallas_call x1, Pallas kernels, send_back(): pl.pallas_call(functools.partial(back_kernel, n_ep, n_my), out_shape=jax....  55.1 us
    pallas_call x2, Pallas kernels, sum_over_my(): pl.pallas_call(functools.partial(sum_kernel, n_my), out_shape=jax.ShapeDt...  21.9 us
    dot_general x1, matrix products, shards(): jnp.einsum('rsp,spd->rd', hidden, w_down, preferred_element_type=jnp.floa...  15.9 us
    dot_general x1, matrix products, shards(): jnp.einsum('rd,spd->rsp', tokens_in, w_up, preferred_element_type=jnp.flo...  6.91 us

profile of v12, /device:TPU:1, one launch (start us, length us, event | category | flops | bytes accessed | tf_op | source)
XLA Modules:
  0.0 266.4 jit_solution(16539854075701113734)
XLA Ops:
  0.6 0.0 copy-start
  0.6 0.0 copy-start.5
  0.7 0.9 copy.18
  1.6 0.1 eq.31
  1.7 1.1 reduce-window.6
  2.9 0.2 slice_reduce_fusion
  3.1 0.1 eq.27
  3.3 0.1 fusion.4
  3.4 0.7 broadcast_multiply_fusion
  4.0 0.1 copy.17
  4.2 0.1 mul.95
  4.4 2.4 scatter_custom_fusion
  6.9 0.0 copy-done
  6.9 0.0 copy-start.1
  6.9 0.0 copy-start.2
  6.9 2.4 multiply_reduce_fusion.2
  9.3 0.0 copy-start.3
  9.3 13.8 %shard_map.113 = f32[1,256]{1,0:T(1,128)} custom-call(f32[1,256]{1,0:T(1,128)} %bitcast.33), custom_call_target="tpu_custom_call" | custom-call | tf_op jit(solution)/shard_map/pallas_call | solution.py:298
  23.1 0.7 add_rsqrt_fusion.1
  23.8 0.0 copy-done.5
  23.8 0.1 multiply_convert_fusion.2
  23.9 3.3 %gather_fusion = bf16[768,256]{1,0:T(8,128)(2,1)} fusion(bf16[257,256]{1,0:T(8,128)(2,1)S(1)} %concatenate.3, s32[1024]{0:T(1024)S(1)} %pad_clamp_fusion.1), kind=kCustom, calls=%fused_computation | custom fusion | bytes 789504 | tf_op jit(solution)/shard_map/gather | solution.py:354
  27.2 0.0 copy-done.1
  27.2 0.9 copy.20.gate_ref
  28.1 0.0 copy-done.2
  28.1 0.9 copy.21.up_ref
  29.0 0.0 copy-done.3
  29.0 0.8 copy.22.down_ref
  29.8 143.9 %shard_map.114 = (bf16[16,48,2048]{2,1,0:T(8,128)(2,1)}, bf16[16,44,2048]{2,1,0:T(8,128)(2,1)}, bf16[16,44,2048]{2,1,0:T(8,128)(2,1)}, bf16[16,44,2048]{2,1,0:T(8,128)(2,1)}) custom-call(bf16[16,48,256]{2,1,0:T(8,128)(2,1)} %bitcast.29, bf16[8,44,512]{2,1,0:T(8,128)(2,1)} %copy.20.gate_ref, bf16[8,44,512]{2,1,0:T(8,128)(2,1)} %copy.21.up_ref, ...), custom_call_target="tpu_custom_call" | custom-call | tf_op jit(solution)/shard_map/pallas_call | solution.py:150
  173.8 6.9 %fusion.14 = f32[768,16,44]{0,2,1:T(8,128)} fusion(bf16[768,2048,1]{1,0,2:T(8,128)(2,1)} %bitcast.37, bf16[16,44,2048]{2,1,0:T(8,128)(2,1)} %get-tuple-element.8), kind=kOutput, calls=%fused_computation.46 | convolution fusion | flops 2214592512 | bytes 8192000 | tf_op jit(solution)/shard_map/rd,spd->rsp/dot_general | solution.py:361
  180.7 15.9 %bitcast_convert_fusion.ex_ref = bf16[768,2048]{1,0:T(8,128)(2,1)} fusion(bf16[16,44,2048]{2,1,0:T(8,128)(2,1)} %get-tuple-element.9, f32[768,16,44]{0,2,1:T(8,128)} %fusion.14, bf16[768,2048,1]{1,0,2:T(8,128)(2,1)} %bitcast.38, bf16[16,44,2048]{2,1,0:T(8,128)(2,1)} %get-tuple-element.7), kind=kOutput, calls=%fused_computation.3 | convolution fusion | flops 4434001920 | bytes 14221312 | tf_op jit(solution)/shard_map/rsp,spd->rd/dot_general | solution.py:363
  196.6 0.0 copy-start.4
  196.6 55.1 %shard_map.115 = bf16[16,48,256]{2,1,0:T(8,128)(2,1)} custom-call(bf16[768,2048]{1,0:T(8,128)(2,1)} %bitcast_convert_fusion.ex_ref), custom_call_target="tpu_custom_call" | custom-call | tf_op jit(solution)/shard_map/pallas_call | solution.py:257
  251.8 0.0 copy-start.6
  251.8 2.6 gather_fusion.1
  254.4 0.3 reshape.174
  254.7 0.0 copy-done.4
  254.7 0.1 copy.16
  254.8 0.7 multiply_reduce_fusion
  255.6 0.7 fusion.13
  256.2 0.7 multiply_reduce_fusion.1
  256.9 8.1 %shard_map.116 = f32[1,256]{1,0:T(1,128)} custom-call(f32[1,256]{1,0:T(1,128)} %bitcast.36), custom_call_target="tpu_custom_call" | custom-call | tf_op jit(solution)/shard_map/pallas_call | solution.py:298
  265.0 0.7 add_rsqrt_fusion
  265.7 0.0 copy-done.6
  265.7 0.8 multiply_convert_fusion.1
  (11 shorter events, 0.1 us)
Async XLA Ops:
  0.6 6.2 %copy-start = (bf16[256,2048]{1,0:T(8,128)(2,1)S(1)}, bf16[256,2048]{1,0:T(8,128)(2,1)}, u32[]{:S(2)}) copy-start(bf16[256,2048]{1,0:T(8,128)(2,1)} %param.10) | copy-start | bytes 3145732
  0.6 23.1 %copy-start.5 = (f32[256]{0:T(256)S(1)}, f32[256]{0:T(256)}, u32[]{:S(2)}) copy-start(f32[256]{0:T(256)} %param.13) | copy-start | bytes 3076
  6.9 20.3 %copy-start.1 = (bf16[8,44,512]{2,0,1:T(8,128)(2,1)S(1)}, bf16[8,44,512]{2,0,1:T(8,128)(2,1)}, u32[]{:S(2)}) copy-start(bf16[8,44,512]{2,0,1:T(8,128)(2,1)} %param.14) | copy-start | bytes 1081348
  6.9 21.2 %copy-start.2 = (bf16[8,44,512]{2,0,1:T(8,128)(2,1)S(1)}, bf16[8,44,512]{2,0,1:T(8,128)(2,1)}, u32[]{:S(2)}) copy-start(bf16[8,44,512]{2,0,1:T(8,128)(2,1)} %param.15) | copy-start | bytes 1081348
  9.3 19.7 %copy-start.3 = (bf16[8,44,512]{2,0,1:T(8,128)(2,1)S(1)}, bf16[8,44,512]{2,0,1:T(8,128)(2,1)}, u32[]{:S(2)}) copy-start(bf16[8,44,512]{2,0,1:T(8,128)(2,1)} %param.16) | copy-start | bytes 1081348
  196.6 58.0 %copy-start.4 = (f32[256,2]{0,1:T(2,128)S(1)}, f32[256,2]{0,1:T(2,128)}, u32[]{:S(2)}) copy-start(f32[256,2]{0,1:T(2,128)} %param.18) | copy-start | bytes 6148
  251.8 13.9 %copy-start.6 = (f32[256]{0:T(256)S(1)}, f32[256]{0:T(256)}, u32[]{:S(2)}) copy-start(f32[256]{0:T(256)} %param.19) | copy-start | bytes 3076

commit v13 on v12

--- a/solution.py
+++ b/solution.py
@@ -75,7 +75,7 @@
             forward.append(copy)
         return forward
 
-    local, direct = start_direct(0)
+    waves = [start_direct(0), start_direct(1)]
     tok_local = pltpu.make_async_copy(packed_ref.at[j], tok_ref.at[j, :, cols_m], tok_sems.at[0, 0])
     tok_local.start()
     tok_z = []
@@ -87,13 +87,14 @@
     tok_my = []
     x_copies = []
     for k in range(3):
+        local, direct = waves[k]
         local.wait()
         for copy in direct:
             copy.wait_recv()
         pending.extend(direct)
         forward = start_forward(k)
-        if k + 1 < 3:
-            local, direct = start_direct(k + 1)
+        if k + 2 < 3:
+            waves.append(start_direct(k + 2))
         for copy in forward:
             copy.wait_recv()
         pending.extend(forward)

time: 267 us -> 268 us (level)
    pallas_call x1, Pallas kernels: 144 us -> 149 us  [move_all(): pl.pallas_call(functools.partial(move_kernel, n_ep, n_mx, n_my, replicas)...]
    pallas_call x1, Pallas kernels: 55.1 us -> 52 us  [send_back(): pl.pallas_call(functools.partial(back_kernel, n_ep, n_my), out_shape=jax....]
where the time goes in v13:
time: 268 us
  Pallas kernels  223 us (83%)
  matrix products  25.2 us (9%)
  local copies, waits for them, and re-layouts  13.1 us (5%)
  other arithmetic  6.35 us (2%)
    pallas_call x1, Pallas kernels, move_all(): pl.pallas_call(functools.partial(move_kernel, n_ep, n_mx, n_my, replicas)...  149 us
    pallas_call x1, Pallas kernels, send_back(): pl.pallas_call(functools.partial(back_kernel, n_ep, n_my), out_shape=jax....  52 us
    pallas_call x2, Pallas kernels, sum_over_my(): pl.pallas_call(functools.partial(sum_kernel, n_my), out_shape=jax.ShapeDt...  21.8 us
    dot_general x1, matrix products, shards(): jnp.einsum('rsp,spd->rd', hidden, w_down, preferred_element_type=jnp.floa...  15.9 us
    dot_general x1, matrix products, shards(): jnp.einsum('rd,spd->rsp', tokens_in, w_up, preferred_element_type=jnp.flo...  6.92 us

profile of v13, /device:TPU:1, one launch (start us, length us, event | category | flops | bytes accessed | tf_op | source)
XLA Modules:
  0.0 268.0 jit_solution(9934275649256224195)
XLA Ops:
  0.6 0.0 copy-start
  0.6 0.0 copy-start.5
  0.7 0.9 copy.18
  1.6 0.1 eq.31
  1.7 1.1 reduce-window.6
  2.9 0.2 slice_reduce_fusion
  3.1 0.1 eq.27
  3.3 0.1 fusion.4
  3.4 0.7 broadcast_multiply_fusion
  4.0 0.1 copy.17
  4.2 0.1 mul.95
  4.4 2.4 scatter_custom_fusion
  6.9 0.0 copy-done
  6.9 0.0 copy-start.1
  6.9 0.0 copy-start.2
  6.9 2.4 multiply_reduce_fusion.2
  9.3 0.0 copy-start.3
  9.3 13.8 %shard_map.113 = f32[1,256]{1,0:T(1,128)} custom-call(f32[1,256]{1,0:T(1,128)} %bitcast.33), custom_call_target="tpu_custom_call" | custom-call | tf_op jit(solution)/shard_map/pallas_call | solution.py:299
  23.1 0.7 add_rsqrt_fusion.1
  23.8 0.0 copy-done.5
  23.8 0.1 multiply_convert_fusion.2
  23.9 3.3 %gather_fusion = bf16[768,256]{1,0:T(8,128)(2,1)} fusion(bf16[257,256]{1,0:T(8,128)(2,1)S(1)} %concatenate.3, s32[1024]{0:T(1024)S(1)} %pad_clamp_fusion.1), kind=kCustom, calls=%fused_computation | custom fusion | bytes 789504 | tf_op jit(solution)/shard_map/gather | solution.py:355
  27.2 0.0 copy-done.1
  27.2 0.9 copy.20.gate_ref
  28.1 0.0 copy-done.2
  28.1 0.9 copy.21.up_ref
  29.0 0.0 copy-done.3
  29.0 0.8 copy.22.down_ref
  29.8 148.7 %shard_map.114 = (bf16[16,48,2048]{2,1,0:T(8,128)(2,1)}, bf16[16,44,2048]{2,1,0:T(8,128)(2,1)}, bf16[16,44,2048]{2,1,0:T(8,128)(2,1)}, bf16[16,44,2048]{2,1,0:T(8,128)(2,1)}) custom-call(bf16[16,48,256]{2,1,0:T(8,128)(2,1)} %bitcast.29, bf16[8,44,512]{2,1,0:T(8,128)(2,1)} %copy.20.gate_ref, bf16[8,44,512]{2,1,0:T(8,128)(2,1)} %copy.21.up_ref, ...), custom_call_target="tpu_custom_call" | custom-call | tf_op jit(solution)/shard_map/pallas_call | solution.py:151
  178.5 6.9 %fusion.14 = f32[768,16,44]{0,2,1:T(8,128)} fusion(bf16[768,2048,1]{1,0,2:T(8,128)(2,1)} %bitcast.37, bf16[16,44,2048]{2,1,0:T(8,128)(2,1)} %get-tuple-element.8), kind=kOutput, calls=%fused_computation.46 | convolution fusion | flops 2214592512 | bytes 8192000 | tf_op jit(solution)/shard_map/rd,spd->rsp/dot_general | solution.py:362
  185.5 15.9 %bitcast_convert_fusion.ex_ref = bf16[768,2048]{1,0:T(8,128)(2,1)} fusion(bf16[16,44,2048]{2,1,0:T(8,128)(2,1)} %get-tuple-element.9, f32[768,16,44]{0,2,1:T(8,128)} %fusion.14, bf16[768,2048,1]{1,0,2:T(8,128)(2,1)} %bitcast.38, bf16[16,44,2048]{2,1,0:T(8,128)(2,1)} %get-tuple-element.7), kind=kOutput, calls=%fused_computation.3 | convolution fusion | flops 4434001920 | bytes 14221312 | tf_op jit(solution)/shard_map/rsp,spd->rd/dot_general | solution.py:364
  201.4 0.0 copy-start.4
  201.4 52.0 %shard_map.115 = bf16[16,48,256]{2,1,0:T(8,128)(2,1)} custom-call(bf16[768,2048]{1,0:T(8,128)(2,1)} %bitcast_convert_fusion.ex_ref), custom_call_target="tpu_custom_call" | custom-call | tf_op jit(solution)/shard_map/pallas_call | solution.py:258
  253.4 0.0 copy-start.6
  253.4 2.6 gather_fusion.1
  256.0 0.3 reshape.174
  256.3 0.0 copy-done.4
  256.3 0.1 copy.16
  256.5 0.7 multiply_reduce_fusion
  257.2 0.7 fusion.13
  257.9 0.7 multiply_reduce_fusion.1
  258.6 8.0 %shard_map.116 = f32[1,256]{1,0:T(1,128)} custom-call(f32[1,256]{1,0:T(1,128)} %bitcast.36), custom_call_target="tpu_custom_call" | custom-call | tf_op jit(solution)/shard_map/pallas_call | solution.py:299
  266.6 0.7 add_rsqrt_fusion
  267.3 0.0 copy-done.6
  267.3 0.8 multiply_convert_fusion.1
  (11 shorter events, 0.1 us)
Async XLA Ops:
  0.6 6.2 %copy-start = (bf16[256,2048]{1,0:T(8,128)(2,1)S(1)}, bf16[256,2048]{1,0:T(8,128)(2,1)}, u32[]{:S(2)}) copy-start(bf16[256,2048]{1,0:T(8,128)(2,1)} %param.10) | copy-start | bytes 3145732
  0.6 23.1 %copy-start.5 = (f32[256]{0:T(256)S(1)}, f32[256]{0:T(256)}, u32[]{:S(2)}) copy-start(f32[256]{0:T(256)} %param.13) | copy-start | bytes 3076
  6.9 20.3 %copy-start.1 = (bf16[8,44,512]{2,0,1:T(8,128)(2,1)S(1)}, bf16[8,44,512]{2,0,1:T(8,128)(2,1)}, u32[]{:S(2)}) copy-start(bf16[8,44,512]{2,0,1:T(8,128)(2,1)} %param.14) | copy-start | bytes 1081348
  6.9 21.2 %copy-start.2 = (bf16[8,44,512]{2,0,1:T(8,128)(2,1)S(1)}, bf16[8,44,512]{2,0,1:T(8,128)(2,1)}, u32[]{:S(2)}) copy-start(bf16[8,44,512]{2,0,1:T(8,128)(2,1)} %param.15) | copy-start | bytes 1081348
  9.3 19.7 %copy-start.3 = (bf16[8,44,512]{2,0,1:T(8,128)(2,1)S(1)}, bf16[8,44,512]{2,0,1:T(8,128)(2,1)}, u32[]{:S(2)}) copy-start(bf16[8,44,512]{2,0,1:T(8,128)(2,1)} %param.16) | copy-start | bytes 1081348
  201.4 54.9 %copy-start.4 = (f32[256,2]{0,1:T(2,128)S(1)}, f32[256,2]{0,1:T(2,128)}, u32[]{:S(2)}) copy-start(f32[256,2]{0,1:T(2,128)} %param.18) | copy-start | bytes 6148
  253.4 13.9 %copy-start.6 = (f32[256]{0:T(256)S(1)}, f32[256]{0:T(256)}, u32[]{:S(2)}) copy-start(f32[256]{0:T(256)} %param.19) | copy-start | bytes 3076

commit v14 on v12

--- a/solution.py
+++ b/solution.py
@@ -189,23 +189,25 @@
     def cols(block):
         return pl.ds(pl.multiple_of(block * fb, fb), fb)
 
-    to_core = []
-    for i in range(chips):
-        copy = remote(ex_ref.at[:, cols(1 - core + 2 * i)], rx_core.at[i],
-                      sems.at[0, i], sems.at[1, i], (j, a, partner))
-        copy.start()
-        to_core.append(copy)
-    for copy in to_core:
-        copy.wait_recv()
-    for i in range(chips):
-        own = ex_ref[:, cols(core + 2 * i)].astype(jnp.float32)
-        chip_part[i] = (own + rx_core[i].astype(jnp.float32)).astype(chip_part.dtype)
     rows = result.shape[0]
     half_rows = rows // 2
     half_slots = n_ep // 2
+    to_core = []
+    for h in range(2):
+        part = pl.ds(h * half_rows, half_rows)
+        for i in range(chips):
+            copy = remote(ex_ref.at[part, cols(1 - core + 2 * i)], rx_core.at[i, part],
+                          sems.at[0, i + chips * h], sems.at[1, i + chips * h], (j, a, partner))
+            copy.start()
+            to_core.append(copy)
     to_y = []
     for h in range(2):
         part = pl.ds(h * half_rows, half_rows)
+        for copy in to_core[h * chips:(h + 1) * chips]:
+            copy.wait_recv()
+        for i in range(chips):
+            own = ex_ref[part, cols(core + 2 * i)].astype(jnp.float32)
+            chip_part[i, part] = (own + rx_core[i, part].astype(jnp.float32)).astype(chip_part.dtype)
         for e in range(1, chips):
             other = lax.rem(y + e, chips)
             copy = remote(chip_part.at[other, part], rx_y.at[e - 1, part],

time: 267 us -> 267 us (level)
  no operation moved by 1% of the time
where the time goes in v14:
time: 267 us; the launch traced here: 266 us
  Pallas kernels  221 us (83%)
  matrix products  25.2 us (9%)
  local copies, waits for them, and re-layouts  13.1 us (5%)
  other arithmetic  6.35 us (2%)
    pallas_call x1, Pallas kernels, move_all(): pl.pallas_call(functools.partial(move_kernel, n_ep, n_mx, n_my, replicas)...  144 us
    pallas_call x1, Pallas kernels, send_back(): pl.pallas_call(functools.partial(back_kernel, n_ep, n_my), out_shape=jax....  55.8 us
    pallas_call x2, Pallas kernels, sum_over_my(): pl.pallas_call(functools.partial(sum_kernel, n_my), out_shape=jax.ShapeDt...  20.9 us
    dot_general x1, matrix products, shards(): jnp.einsum('rsp,spd->rd', hidden, w_down, preferred_element_type=jnp.floa...  15.9 us
    dot_general x1, matrix products, shards(): jnp.einsum('rd,spd->rsp', tokens_in, w_up, preferred_element_type=jnp.flo...  6.91 us

profile of v14, /device:TPU:1, one launch (start us, length us, event | category | flops | bytes accessed | tf_op | source)
XLA Modules:
  0.0 266.1 jit_solution(12048837577145635985)
XLA Ops:
  0.6 0.0 copy-start
  0.6 0.0 copy-start.5
  0.7 0.9 copy.18
  1.6 0.1 eq.31
  1.7 1.1 reduce-window.6
  2.9 0.2 slice_reduce_fusion
  3.1 0.1 eq.27
  3.3 0.1 fusion.4
  3.4 0.7 broadcast_multiply_fusion
  4.0 0.1 copy.17
  4.2 0.1 mul.95
  4.4 2.4 scatter_custom_fusion
  6.9 0.0 copy-done
  6.9 0.0 copy-start.1
  6.9 0.0 copy-start.2
  6.9 2.4 multiply_reduce_fusion.2
  9.3 0.0 copy-start.3
  9.3 13.8 %shard_map.113 = f32[1,256]{1,0:T(1,128)} custom-call(f32[1,256]{1,0:T(1,128)} %bitcast.33), custom_call_target="tpu_custom_call" | custom-call | tf_op jit(solution)/shard_map/pallas_call | solution.py:300
  23.1 0.7 add_rsqrt_fusion.1
  23.8 0.0 copy-done.5
  23.8 0.1 multiply_convert_fusion.2
  23.9 3.3 %gather_fusion = bf16[768,256]{1,0:T(8,128)(2,1)} fusion(bf16[257,256]{1,0:T(8,128)(2,1)S(1)} %concatenate.3, s32[1024]{0:T(1024)S(1)} %pad_clamp_fusion.1), kind=kCustom, calls=%fused_computation | custom fusion | bytes 789504 | tf_op jit(solution)/shard_map/gather | solution.py:356
  27.2 0.0 copy-done.1
  27.2 0.9 copy.20.gate_ref
  28.1 0.0 copy-done.2
  28.1 0.9 copy.21.up_ref
  29.0 0.0 copy-done.3
  29.0 0.8 copy.22.down_ref
  29.8 143.9 %shard_map.114 = (bf16[16,48,2048]{2,1,0:T(8,128)(2,1)}, bf16[16,44,2048]{2,1,0:T(8,128)(2,1)}, bf16[16,44,2048]{2,1,0:T(8,128)(2,1)}, bf16[16,44,2048]{2,1,0:T(8,128)(2,1)}) custom-call(bf16[16,48,256]{2,1,0:T(8,128)(2,1)} %bitcast.29, bf16[8,44,512]{2,1,0:T(8,128)(2,1)} %copy.20.gate_ref, bf16[8,44,512]{2,1,0:T(8,128)(2,1)} %copy.21.up_ref, ...), custom_call_target="tpu_custom_call" | custom-call | tf_op jit(solution)/shard_map/pallas_call | solution.py:150
  173.8 6.9 %fusion.14 = f32[768,16,44]{0,2,1:T(8,128)} fusion(bf16[768,2048,1]{1,0,2:T(8,128)(2,1)} %bitcast.37, bf16[16,44,2048]{2,1,0:T(8,128)(2,1)} %get-tuple-element.8), kind=kOutput, calls=%fused_computation.46 | convolution fusion | flops 2214592512 | bytes 8192000 | tf_op jit(solution)/shard_map/rd,spd->rsp/dot_general | solution.py:363
  180.7 15.9 %bitcast_convert_fusion.ex_ref = bf16[768,2048]{1,0:T(8,128)(2,1)} fusion(bf16[16,44,2048]{2,1,0:T(8,128)(2,1)} %get-tuple-element.9, f32[768,16,44]{0,2,1:T(8,128)} %fusion.14, bf16[768,2048,1]{1,0,2:T(8,128)(2,1)} %bitcast.38, bf16[16,44,2048]{2,1,0:T(8,128)(2,1)} %get-tuple-element.7), kind=kOutput, calls=%fused_computation.3 | convolution fusion | flops 4434001920 | bytes 14221312 | tf_op jit(solution)/shard_map/rsp,spd->rd/dot_general | solution.py:365
  196.6 0.0 copy-start.4
  196.6 55.8 %shard_map.115 = bf16[16,48,256]{2,1,0:T(8,128)(2,1)} custom-call(bf16[768,2048]{1,0:T(8,128)(2,1)} %bitcast_convert_fusion.ex_ref), custom_call_target="tpu_custom_call" | custom-call | tf_op jit(solution)/shard_map/pallas_call | solution.py:259
  252.4 0.0 copy-start.6
  252.5 2.6 gather_fusion.1
  255.1 0.3 reshape.174
  255.3 0.0 copy-done.4
  255.4 0.1 copy.16
  255.5 0.7 multiply_reduce_fusion
  256.2 0.7 fusion.13
  256.9 0.7 multiply_reduce_fusion.1
  257.6 7.1 %shard_map.116 = f32[1,256]{1,0:T(1,128)} custom-call(f32[1,256]{1,0:T(1,128)} %bitcast.36), custom_call_target="tpu_custom_call" | custom-call | tf_op jit(solution)/shard_map/pallas_call | solution.py:300
  264.7 0.7 add_rsqrt_fusion
  265.4 0.0 copy-done.6
  265.4 0.8 multiply_convert_fusion.1
  (11 shorter events, 0.1 us)
Async XLA Ops:
  0.6 6.2 %copy-start = (bf16[256,2048]{1,0:T(8,128)(2,1)S(1)}, bf16[256,2048]{1,0:T(8,128)(2,1)}, u32[]{:S(2)}) copy-start(bf16[256,2048]{1,0:T(8,128)(2,1)} %param.10) | copy-start | bytes 3145732
  0.6 23.1 %copy-start.5 = (f32[256]{0:T(256)S(1)}, f32[256]{0:T(256)}, u32[]{:S(2)}) copy-start(f32[256]{0:T(256)} %param.13) | copy-start | bytes 3076
  6.9 20.3 %copy-start.1 = (bf16[8,44,512]{2,0,1:T(8,128)(2,1)S(1)}, bf16[8,44,512]{2,0,1:T(8,128)(2,1)}, u32[]{:S(2)}) copy-start(bf16[8,44,512]{2,0,1:T(8,128)(2,1)} %param.14) | copy-start | bytes 1081348
  6.9 21.2 %copy-start.2 = (bf16[8,44,512]{2,0,1:T(8,128)(2,1)S(1)}, bf16[8,44,512]{2,0,1:T(8,128)(2,1)}, u32[]{:S(2)}) copy-start(bf16[8,44,512]{2,0,1:T(8,128)(2,1)} %param.15) | copy-start | bytes 1081348
  9.3 19.7 %copy-start.3 = (bf16[8,44,512]{2,0,1:T(8,128)(2,1)S(1)}, bf16[8,44,512]{2,0,1:T(8,128)(2,1)}, u32[]{:S(2)}) copy-start(bf16[8,44,512]{2,0,1:T(8,128)(2,1)} %param.16) | copy-start | bytes 1081348
  196.6 58.7 %copy-start.4 = (f32[256,2]{0,1:T(2,128)S(1)}, f32[256,2]{0,1:T(2,128)}, u32[]{:S(2)}) copy-start(f32[256,2]{0,1:T(2,128)} %param.18) | copy-start | bytes 6148
  252.4 12.9 %copy-start.6 = (f32[256]{0:T(256)S(1)}, f32[256]{0:T(256)}, u32[]{:S(2)}) copy-start(f32[256]{0:T(256)} %param.19) | copy-start | bytes 3076

commit v15 on v14

--- a/solution.py
+++ b/solution.py
@@ -86,6 +86,25 @@
         tok_z.append(copy)
     tok_my = []
     x_copies = []
+    right = lax.rem(a + 1, n_mx)
+    left = lax.rem(a + n_mx - 1, n_mx)
+    half = n_ep // 2
+    cols_l = pl.ds(pl.multiple_of(left * wb, wb), wb)
+    cols_r = pl.ds(pl.multiple_of(right * wb, wb), wb)
+
+    def relay(k, to_right, to_left):
+        to_right.wait_recv()
+        fwd_right = remote(outs[k].at[pl.ds(0, half), :, cols_l], outs[k].at[pl.ds(0, half), :, cols_l],
+                           send_x.at[k, 2], recv_x.at[k, 2], (j, right, m))
+        fwd_right.start()
+        to_left.wait_recv()
+        fwd_left = remote(outs[k].at[pl.ds(half, half), :, cols_r], outs[k].at[pl.ds(half, half), :, cols_r],
+                          send_x.at[k, 3], recv_x.at[k, 3], (j, left, m))
+        fwd_left.start()
+        pending.extend([to_right, to_left])
+        x_copies.extend([fwd_right, fwd_left])
+
+    waiting = None
     for k in range(3):
         local.wait()
         for copy in direct:
@@ -94,38 +113,18 @@
         forward = start_forward(k)
         if k + 1 < 3:
             local, direct = start_direct(k + 1)
+        if waiting is not None:
+            relay(*waiting)
         for copy in forward:
             copy.wait_recv()
         pending.extend(forward)
-        if n_mx == 4:
-            right = lax.rem(a + 1, n_mx)
-            left = lax.rem(a + n_mx - 1, n_mx)
-            half = n_ep // 2
-            to_right = remote(outs[k].at[:, :, cols_a], outs[k].at[:, :, cols_a],
-                              send_x.at[k, 0], recv_x.at[k, 0], (j, right, m))
-            to_left = remote(outs[k].at[:, :, cols_a], outs[k].at[:, :, cols_a],
-                             send_x.at[k, 1], recv_x.at[k, 1], (j, left, m))
-            to_right.start()
-            to_left.start()
-            cols_l = pl.ds(pl.multiple_of(left * wb, wb), wb)
-            cols_r = pl.ds(pl.multiple_of(right * wb, wb), wb)
-            to_right.wait_recv()
-            fwd_right = remote(outs[k].at[pl.ds(0, half), :, cols_l], outs[k].at[pl.ds(0, half), :, cols_l],
-                               send_x.at[k, 2], recv_x.at[k, 2], (j, right, m))
-            fwd_right.start()
-            to_left.wait_recv()
-            fwd_left = remote(outs[k].at[pl.ds(half, half), :, cols_r], outs[k].at[pl.ds(half, half), :, cols_r],
-                              send_x.at[k, 3], recv_x.at[k, 3], (j, left, m))
-            fwd_left.start()
-            pending.extend([to_right, to_left])
-            x_copies.extend([fwd_right, fwd_left])
-        else:
-            for e in range(1, n_mx):
-                b = lax.rem(a + e, n_mx)
-                copy = remote(outs[k].at[:, :, cols_a], outs[k].at[:, :, cols_a],
-                              send_x.at[k, e], recv_x.at[k, e], (j, b, m))
-                copy.start()
-                x_copies.append(copy)
+        to_right = remote(outs[k].at[:, :, cols_a], outs[k].at[:, :, cols_a],
+                          send_x.at[k, 0], recv_x.at[k, 0], (j, right, m))
+        to_left = remote(outs[k].at[:, :, cols_a], outs[k].at[:, :, cols_a],
+                         send_x.at[k, 1], recv_x.at[k, 1], (j, left, m))
+        to_right.start()
+        to_left.start()
+        waiting = (k, to_right, to_left)
         if k == 0:
             tok_local.wait()
             for copy in tok_z:
@@ -137,6 +136,7 @@
                 copy.start()
                 tok_my.append(copy)
             pending.extend(tok_my)
+    relay(*waiting)
     pending.extend(x_copies)
     for copy in pending:
         copy.wait_send()

time: 267 us -> 257 us (0.963)
  Pallas kernels: 221 us -> 212 us
    pallas_call x1, Pallas kernels: 55.8 us -> 50.3 us  [send_back(): pl.pallas_call(functools.partial(back_kernel, n_ep, n_my), out_shape=jax....]
    pallas_call x1, Pallas kernels: 144 us -> 140 us  [move_all(): pl.pallas_call(functools.partial(move_kernel, n_ep, n_mx, n_my, replicas)...]
where the time goes in v15:
time: 257 us
  Pallas kernels  212 us (82%)
  matrix products  25.2 us (10%)
  local copies, waits for them, and re-layouts  13.1 us (5%)
  other arithmetic  6.35 us (2%)
    pallas_call x1, Pallas kernels, move_all(): pl.pallas_call(functools.partial(move_kernel, n_ep, n_mx, n_my, replicas)...  140 us
    pallas_call x1, Pallas kernels, send_back(): pl.pallas_call(functools.partial(back_kernel, n_ep, n_my), out_shape=jax....  50.3 us
    pallas_call x2, Pallas kernels, sum_over_my(): pl.pallas_call(functools.partial(sum_kernel, n_my), out_shape=jax.ShapeDt...  21.5 us
    dot_general x1, matrix products, shards(): jnp.einsum('rsp,spd->rd', hidden, w_down, preferred_element_type=jnp.floa...  15.9 us
    dot_general x1, matrix products, shards(): jnp.einsum('rd,spd->rsp', tokens_in, w_up, preferred_element_type=jnp.flo...  6.92 us

profile of v15, /device:TPU:1, one launch (start us, length us, event | category | flops | bytes accessed | tf_op | source)
XLA Modules:
  0.0 257.0 jit_solution(3681994449862252413)
XLA Ops:
  0.6 0.0 copy-start
  0.6 0.0 copy-start.5
  0.7 0.9 copy.18
  1.6 0.1 eq.31
  1.7 1.1 reduce-window.6
  2.9 0.2 slice_reduce_fusion
  3.1 0.1 eq.27
  3.3 0.1 fusion.4
  3.4 0.7 broadcast_multiply_fusion
  4.0 0.1 copy.17
  4.2 0.1 mul.95
  4.4 2.4 scatter_custom_fusion
  6.9 0.0 copy-done
  6.9 0.0 copy-start.1
  6.9 0.0 copy-start.2
  6.9 2.4 multiply_reduce_fusion.2
  9.3 0.0 copy-start.3
  9.3 13.8 %shard_map.113 = f32[1,256]{1,0:T(1,128)} custom-call(f32[1,256]{1,0:T(1,128)} %bitcast.33), custom_call_target="tpu_custom_call" | custom-call | tf_op jit(solution)/shard_map/pallas_call | solution.py:300
  23.1 0.7 add_rsqrt_fusion.1
  23.8 0.0 copy-done.5
  23.8 0.1 multiply_convert_fusion.2
  23.9 3.3 %gather_fusion = bf16[768,256]{1,0:T(8,128)(2,1)} fusion(bf16[257,256]{1,0:T(8,128)(2,1)S(1)} %concatenate.3, s32[1024]{0:T(1024)S(1)} %pad_clamp_fusion.1), kind=kCustom, calls=%fused_computation | custom fusion | bytes 789504 | tf_op jit(solution)/shard_map/gather | solution.py:356
  27.2 0.0 copy-done.1
  27.2 0.9 copy.20.gate_ref
  28.1 0.0 copy-done.2
  28.1 0.9 copy.21.up_ref
  29.0 0.0 copy-done.3
  29.0 0.8 copy.22.down_ref
  29.8 139.7 %shard_map.114 = (bf16[16,48,2048]{2,1,0:T(8,128)(2,1)}, bf16[16,44,2048]{2,1,0:T(8,128)(2,1)}, bf16[16,44,2048]{2,1,0:T(8,128)(2,1)}, bf16[16,44,2048]{2,1,0:T(8,128)(2,1)}) custom-call(bf16[16,48,256]{2,1,0:T(8,128)(2,1)} %bitcast.29, bf16[8,44,512]{2,1,0:T(8,128)(2,1)} %copy.20.gate_ref, bf16[8,44,512]{2,1,0:T(8,128)(2,1)} %copy.21.up_ref, ...), custom_call_target="tpu_custom_call" | custom-call | tf_op jit(solution)/shard_map/pallas_call | solution.py:150
  169.6 6.9 %fusion.14 = f32[768,16,44]{0,2,1:T(8,128)} fusion(bf16[768,2048,1]{1,0,2:T(8,128)(2,1)} %bitcast.37, bf16[16,44,2048]{2,1,0:T(8,128)(2,1)} %get-tuple-element.8), kind=kOutput, calls=%fused_computation.46 | convolution fusion | flops 2214592512 | bytes 8192000 | tf_op jit(solution)/shard_map/rd,spd->rsp/dot_general | solution.py:363
  176.5 15.9 %bitcast_convert_fusion.ex_ref = bf16[768,2048]{1,0:T(8,128)(2,1)} fusion(bf16[16,44,2048]{2,1,0:T(8,128)(2,1)} %get-tuple-element.9, f32[768,16,44]{0,2,1:T(8,128)} %fusion.14, bf16[768,2048,1]{1,0,2:T(8,128)(2,1)} %bitcast.38, bf16[16,44,2048]{2,1,0:T(8,128)(2,1)} %get-tuple-element.7), kind=kOutput, calls=%fused_computation.3 | convolution fusion | flops 4434001920 | bytes 14221312 | tf_op jit(solution)/shard_map/rsp,spd->rd/dot_general | solution.py:365
  192.4 0.0 copy-start.4
  192.4 50.3 %shard_map.115 = bf16[16,48,256]{2,1,0:T(8,128)(2,1)} custom-call(bf16[768,2048]{1,0:T(8,128)(2,1)} %bitcast_convert_fusion.ex_ref), custom_call_target="tpu_custom_call" | custom-call | tf_op jit(solution)/shard_map/pallas_call | solution.py:259
  242.7 0.0 copy-start.6
  242.7 2.6 %gather_fusion.1 = bf16[512,256]{1,0:T(8,128)(2,1)S(1)} fusion(bf16[768,256]{1,0:T(8,128)(2,1)} %bitcast.28, s32[1024]{0:T(1024)S(1)} %pad_clamp_fusion), kind=kCustom, calls=%fused_computation.1 | custom fusion | bytes 526336 | tf_op jit(solution)/shard_map/gather | solution.py:370
  245.4 0.3 reshape.174
  245.6 0.0 copy-done.4
  245.7 0.1 copy.16
  245.8 0.7 multiply_reduce_fusion
  246.5 0.7 fusion.13
  247.2 0.7 multiply_reduce_fusion.1
  247.9 7.7 %shard_map.116 = f32[1,256]{1,0:T(1,128)} custom-call(f32[1,256]{1,0:T(1,128)} %bitcast.36), custom_call_target="tpu_custom_call" | custom-call | tf_op jit(solution)/shard_map/pallas_call | solution.py:300
  255.6 0.7 add_rsqrt_fusion
  256.3 0.0 copy-done.6
  256.3 0.8 multiply_convert_fusion.1
  (11 shorter events, 0.1 us)
Async XLA Ops:
  0.6 6.2 %copy-start = (bf16[256,2048]{1,0:T(8,128)(2,1)S(1)}, bf16[256,2048]{1,0:T(8,128)(2,1)}, u32[]{:S(2)}) copy-start(bf16[256,2048]{1,0:T(8,128)(2,1)} %param.10) | copy-start | bytes 3145732
  0.6 23.1 %copy-start.5 = (f32[256]{0:T(256)S(1)}, f32[256]{0:T(256)}, u32[]{:S(2)}) copy-start(f32[256]{0:T(256)} %param.13) | copy-start | bytes 3076
  6.9 20.3 %copy-start.1 = (bf16[8,44,512]{2,0,1:T(8,128)(2,1)S(1)}, bf16[8,44,512]{2,0,1:T(8,128)(2,1)}, u32[]{:S(2)}) copy-start(bf16[8,44,512]{2,0,1:T(8,128)(2,1)} %param.14) | copy-start | bytes 1081348
  6.9 21.2 %copy-start.2 = (bf16[8,44,512]{2,0,1:T(8,128)(2,1)S(1)}, bf16[8,44,512]{2,0,1:T(8,128)(2,1)}, u32[]{:S(2)}) copy-start(bf16[8,44,512]{2,0,1:T(8,128)(2,1)} %param.15) | copy-start | bytes 1081348
  9.3 19.7 %copy-start.3 = (bf16[8,44,512]{2,0,1:T(8,128)(2,1)S(1)}, bf16[8,44,512]{2,0,1:T(8,128)(2,1)}, u32[]{:S(2)}) copy-start(bf16[8,44,512]{2,0,1:T(8,128)(2,1)} %param.16) | copy-start | bytes 1081348
  192.4 53.2 %copy-start.4 = (f32[256,2]{0,1:T(2,128)S(1)}, f32[256,2]{0,1:T(2,128)}, u32[]{:S(2)}) copy-start(f32[256,2]{0,1:T(2,128)} %param.18) | copy-start | bytes 6148
  242.7 13.6 %copy-start.6 = (f32[256]{0:T(256)S(1)}, f32[256]{0:T(256)}, u32[]{:S(2)}) copy-start(f32[256]{0:T(256)} %param.19) | copy-start | bytes 3076

commit v16 on v15

--- a/solution.py
+++ b/solution.py
@@ -125,7 +125,7 @@
         to_right.start()
         to_left.start()
         waiting = (k, to_right, to_left)
-        if k == 0:
+        if k == 1:
             tok_local.wait()
             for copy in tok_z:
                 copy.wait_recv()

time: 257 us -> 257 us (level)
  no operation moved by 1% of the time
where the time goes in v16:
time: 257 us
  Pallas kernels  212 us (82%)
  matrix products  25.2 us (10%)
  local copies, waits for them, and re-layouts  13.1 us (5%)
  other arithmetic  6.35 us (2%)
    pallas_call x1, Pallas kernels, move_all(): pl.pallas_call(functools.partial(move_kernel, n_ep, n_mx, n_my, replicas)...  140 us
    pallas_call x1, Pallas kernels, send_back(): pl.pallas_call(functools.partial(back_kernel, n_ep, n_my), out_shape=jax....  50.3 us
    pallas_call x2, Pallas kernels, sum_over_my(): pl.pallas_call(functools.partial(sum_kernel, n_my), out_shape=jax.ShapeDt...  21.5 us
    dot_general x1, matrix products, shards(): jnp.einsum('rsp,spd->rd', hidden, w_down, preferred_element_type=jnp.floa...  15.9 us
    dot_general x1, matrix products, shards(): jnp.einsum('rd,spd->rsp', tokens_in, w_up, preferred_element_type=jnp.flo...  6.92 us

profile of v16, /device:TPU:1, one launch (start us, length us, event | category | flops | bytes accessed | tf_op | source)
XLA Modules:
  0.0 257.0 jit_solution(3772709847301956932)
XLA Ops:
  0.6 0.0 copy-start
  0.6 0.0 copy-start.5
  0.7 0.9 copy.18
  1.6 0.1 eq.31
  1.7 1.1 reduce-window.6
  2.9 0.2 slice_reduce_fusion
  3.1 0.1 eq.27
  3.3 0.1 fusion.4
  3.4 0.7 broadcast_multiply_fusion
  4.0 0.1 copy.17
  4.2 0.1 mul.95
  4.4 2.4 scatter_custom_fusion
  6.9 0.0 copy-done
  6.9 0.0 copy-start.1
  6.9 0.0 copy-start.2
  6.9 2.4 multiply_reduce_fusion.2
  9.3 0.0 copy-start.3
  9.3 13.8 %shard_map.113 = f32[1,256]{1,0:T(1,128)} custom-call(f32[1,256]{1,0:T(1,128)} %bitcast.33), custom_call_target="tpu_custom_call" | custom-call | tf_op jit(solution)/shard_map/pallas_call | solution.py:300
  23.1 0.7 add_rsqrt_fusion.1
  23.8 0.0 copy-done.5
  23.8 0.1 multiply_convert_fusion.2
  23.9 3.3 %gather_fusion = bf16[768,256]{1,0:T(8,128)(2,1)} fusion(bf16[257,256]{1,0:T(8,128)(2,1)S(1)} %concatenate.3, s32[1024]{0:T(1024)S(1)} %pad_clamp_fusion.1), kind=kCustom, calls=%fused_computation | custom fusion | bytes 789504 | tf_op jit(solution)/shard_map/gather | solution.py:356
  27.2 0.0 copy-done.1
  27.2 0.9 copy.20.gate_ref
  28.1 0.0 copy-done.2
  28.1 0.9 copy.21.up_ref
  29.0 0.0 copy-done.3
  29.0 0.8 copy.22.down_ref
  29.8 139.7 %shard_map.114 = (bf16[16,48,2048]{2,1,0:T(8,128)(2,1)}, bf16[16,44,2048]{2,1,0:T(8,128)(2,1)}, bf16[16,44,2048]{2,1,0:T(8,128)(2,1)}, bf16[16,44,2048]{2,1,0:T(8,128)(2,1)}) custom-call(bf16[16,48,256]{2,1,0:T(8,128)(2,1)} %bitcast.29, bf16[8,44,512]{2,1,0:T(8,128)(2,1)} %copy.20.gate_ref, bf16[8,44,512]{2,1,0:T(8,128)(2,1)} %copy.21.up_ref, ...), custom_call_target="tpu_custom_call" | custom-call | tf_op jit(solution)/shard_map/pallas_call | solution.py:150
  169.6 6.9 %fusion.14 = f32[768,16,44]{0,2,1:T(8,128)} fusion(bf16[768,2048,1]{1,0,2:T(8,128)(2,1)} %bitcast.37, bf16[16,44,2048]{2,1,0:T(8,128)(2,1)} %get-tuple-element.8), kind=kOutput, calls=%fused_computation.46 | convolution fusion | flops 2214592512 | bytes 8192000 | tf_op jit(solution)/shard_map/rd,spd->rsp/dot_general | solution.py:363
  176.5 15.9 %bitcast_convert_fusion.ex_ref = bf16[768,2048]{1,0:T(8,128)(2,1)} fusion(bf16[16,44,2048]{2,1,0:T(8,128)(2,1)} %get-tuple-element.9, f32[768,16,44]{0,2,1:T(8,128)} %fusion.14, bf16[768,2048,1]{1,0,2:T(8,128)(2,1)} %bitcast.38, bf16[16,44,2048]{2,1,0:T(8,128)(2,1)} %get-tuple-element.7), kind=kOutput, calls=%fused_computation.3 | convolution fusion | flops 4434001920 | bytes 14221312 | tf_op jit(solution)/shard_map/rsp,spd->rd/dot_general | solution.py:365
  192.4 0.0 copy-start.4
  192.4 50.3 %shard_map.115 = bf16[16,48,256]{2,1,0:T(8,128)(2,1)} custom-call(bf16[768,2048]{1,0:T(8,128)(2,1)} %bitcast_convert_fusion.ex_ref), custom_call_target="tpu_custom_call" | custom-call | tf_op jit(solution)/shard_map/pallas_call | solution.py:259
  242.7 0.0 copy-start.6
  242.7 2.6 %gather_fusion.1 = bf16[512,256]{1,0:T(8,128)(2,1)S(1)} fusion(bf16[768,256]{1,0:T(8,128)(2,1)} %bitcast.28, s32[1024]{0:T(1024)S(1)} %pad_clamp_fusion), kind=kCustom, calls=%fused_computation.1 | custom fusion | bytes 526336 | tf_op jit(solution)/shard_map/gather | solution.py:370
  245.4 0.3 reshape.174
  245.6 0.0 copy-done.4
  245.7 0.1 copy.16
  245.8 0.7 multiply_reduce_fusion
  246.5 0.7 fusion.13
  247.2 0.7 multiply_reduce_fusion.1
  247.9 7.7 %shard_map.116 = f32[1,256]{1,0:T(1,128)} custom-call(f32[1,256]{1,0:T(1,128)} %bitcast.36), custom_call_target="tpu_custom_call" | custom-call | tf_op jit(solution)/shard_map/pallas_call | solution.py:300
  255.6 0.7 add_rsqrt_fusion
  256.3 0.0 copy-done.6
  256.3 0.8 multiply_convert_fusion.1
  (11 shorter events, 0.1 us)
Async XLA Ops:
  0.6 6.2 %copy-start = (bf16[256,2048]{1,0:T(8,128)(2,1)S(1)}, bf16[256,2048]{1,0:T(8,128)(2,1)}, u32[]{:S(2)}) copy-start(bf16[256,2048]{1,0:T(8,128)(2,1)} %param.10) | copy-start | bytes 3145732
  0.6 23.1 %copy-start.5 = (f32[256]{0:T(256)S(1)}, f32[256]{0:T(256)}, u32[]{:S(2)}) copy-start(f32[256]{0:T(256)} %param.13) | copy-start | bytes 3076
  6.9 20.3 %copy-start.1 = (bf16[8,44,512]{2,0,1:T(8,128)(2,1)S(1)}, bf16[8,44,512]{2,0,1:T(8,128)(2,1)}, u32[]{:S(2)}) copy-start(bf16[8,44,512]{2,0,1:T(8,128)(2,1)} %param.14) | copy-start | bytes 1081348
  6.9 21.2 %copy-start.2 = (bf16[8,44,512]{2,0,1:T(8,128)(2,1)S(1)}, bf16[8,44,512]{2,0,1:T(8,128)(2,1)}, u32[]{:S(2)}) copy-start(bf16[8,44,512]{2,0,1:T(8,128)(2,1)} %param.15) | copy-start | bytes 1081348
  9.3 19.7 %copy-start.3 = (bf16[8,44,512]{2,0,1:T(8,128)(2,1)S(1)}, bf16[8,44,512]{2,0,1:T(8,128)(2,1)}, u32[]{:S(2)}) copy-start(bf16[8,44,512]{2,0,1:T(8,128)(2,1)} %param.16) | copy-start | bytes 1081348
  192.4 53.2 %copy-start.4 = (f32[256,2]{0,1:T(2,128)S(1)}, f32[256,2]{0,1:T(2,128)}, u32[]{:S(2)}) copy-start(f32[256,2]{0,1:T(2,128)} %param.18) | copy-start | bytes 6148
  242.7 13.6 %copy-start.6 = (f32[256]{0:T(256)S(1)}, f32[256]{0:T(256)}, u32[]{:S(2)}) copy-start(f32[256]{0:T(256)} %param.19) | copy-start | bytes 3076

commit v17 on v15

--- a/solution.py
+++ b/solution.py
@@ -106,6 +106,8 @@
 
     waiting = None
     for k in range(3):
+        if waiting is not None:
+            relay(*waiting)
         local.wait()
         for copy in direct:
             copy.wait_recv()
@@ -113,8 +115,6 @@
         forward = start_forward(k)
         if k + 1 < 3:
             local, direct = start_direct(k + 1)
-        if waiting is not None:
-            relay(*waiting)
         for copy in forward:
             copy.wait_recv()
         pending.extend(forward)

time: 257 us -> 266 us (1.035)
  Pallas kernels: 212 us -> 220 us
    pallas_call x1, Pallas kernels: 50.3 us -> 55.8 us  [send_back(): pl.pallas_call(functools.partial(back_kernel, n_ep, n_my), out_shape=jax....]
    pallas_call x1, Pallas kernels: 140 us -> 144 us  [move_all(): pl.pallas_call(functools.partial(move_kernel, n_ep, n_mx, n_my, replicas)...]
where the time goes in v17:
time: 266 us
  Pallas kernels  220 us (83%)
  matrix products  25.2 us (9%)
  local copies, waits for them, and re-layouts  13.1 us (5%)
  other arithmetic  6.35 us (2%)
    pallas_call x1, Pallas kernels, move_all(): pl.pallas_call(functools.partial(move_kernel, n_ep, n_mx, n_my, replicas)...  144 us
    pallas_call x1, Pallas kernels, send_back(): pl.pallas_call(functools.partial(back_kernel, n_ep, n_my), out_shape=jax....  55.8 us
    pallas_call x2, Pallas kernels, sum_over_my(): pl.pallas_call(functools.partial(sum_kernel, n_my), out_shape=jax.ShapeDt...  20.8 us
    dot_general x1, matrix products, shards(): jnp.einsum('rsp,spd->rd', hidden, w_down, preferred_element_type=jnp.floa...  15.9 us
    dot_general x1, matrix products, shards(): jnp.einsum('rd,spd->rsp', tokens_in, w_up, preferred_element_type=jnp.flo...  6.92 us

profile of v17, /device:TPU:1, one launch (start us, length us, event | category | flops | bytes accessed | tf_op | source)
XLA Modules:
  0.0 266.0 jit_solution(1628734520864368285)
XLA Ops:
  0.6 0.0 copy-start
  0.6 0.0 copy-start.5
  0.7 0.9 copy.18
  1.6 0.1 eq.31
  1.7 1.1 reduce-window.6
  2.9 0.2 slice_reduce_fusion
  3.1 0.1 eq.27
  3.3 0.1 fusion.4
  3.4 0.7 broadcast_multiply_fusion
  4.0 0.1 copy.17
  4.2 0.1 mul.95
  4.4 2.4 scatter_custom_fusion
  6.9 0.0 copy-done
  6.9 0.0 copy-start.1
  6.9 0.0 copy-start.2
  6.9 2.4 multiply_reduce_fusion.2
  9.3 0.0 copy-start.3
  9.3 13.8 %shard_map.113 = f32[1,256]{1,0:T(1,128)} custom-call(f32[1,256]{1,0:T(1,128)} %bitcast.33), custom_call_target="tpu_custom_call" | custom-call | tf_op jit(solution)/shard_map/pallas_call | solution.py:300
  23.1 0.7 add_rsqrt_fusion.1
  23.8 0.0 copy-done.5
  23.8 0.1 multiply_convert_fusion.2
  23.9 3.3 %gather_fusion = bf16[768,256]{1,0:T(8,128)(2,1)} fusion(bf16[257,256]{1,0:T(8,128)(2,1)S(1)} %concatenate.3, s32[1024]{0:T(1024)S(1)} %pad_clamp_fusion.1), kind=kCustom, calls=%fused_computation | custom fusion | bytes 789504 | tf_op jit(solution)/shard_map/gather | solution.py:356
  27.2 0.0 copy-done.1
  27.2 0.9 copy.20.gate_ref
  28.1 0.0 copy-done.2
  28.1 0.9 copy.21.up_ref
  29.0 0.0 copy-done.3
  29.0 0.8 copy.22.down_ref
  29.8 143.9 %shard_map.114 = (bf16[16,48,2048]{2,1,0:T(8,128)(2,1)}, bf16[16,44,2048]{2,1,0:T(8,128)(2,1)}, bf16[16,44,2048]{2,1,0:T(8,128)(2,1)}, bf16[16,44,2048]{2,1,0:T(8,128)(2,1)}) custom-call(bf16[16,48,256]{2,1,0:T(8,128)(2,1)} %bitcast.29, bf16[8,44,512]{2,1,0:T(8,128)(2,1)} %copy.20.gate_ref, bf16[8,44,512]{2,1,0:T(8,128)(2,1)} %copy.21.up_ref, ...), custom_call_target="tpu_custom_call" | custom-call | tf_op jit(solution)/shard_map/pallas_call | solution.py:150
  173.7 6.9 %fusion.14 = f32[768,16,44]{0,2,1:T(8,128)} fusion(bf16[768,2048,1]{1,0,2:T(8,128)(2,1)} %bitcast.37, bf16[16,44,2048]{2,1,0:T(8,128)(2,1)} %get-tuple-element.8), kind=kOutput, calls=%fused_computation.46 | convolution fusion | flops 2214592512 | bytes 8192000 | tf_op jit(solution)/shard_map/rd,spd->rsp/dot_general | solution.py:363
  180.6 15.9 %bitcast_convert_fusion.ex_ref = bf16[768,2048]{1,0:T(8,128)(2,1)} fusion(bf16[16,44,2048]{2,1,0:T(8,128)(2,1)} %get-tuple-element.9, f32[768,16,44]{0,2,1:T(8,128)} %fusion.14, bf16[768,2048,1]{1,0,2:T(8,128)(2,1)} %bitcast.38, bf16[16,44,2048]{2,1,0:T(8,128)(2,1)} %get-tuple-element.7), kind=kOutput, calls=%fused_computation.3 | convolution fusion | flops 4434001920 | bytes 14221312 | tf_op jit(solution)/shard_map/rsp,spd->rd/dot_general | solution.py:365
  196.5 0.0 copy-start.4
  196.5 55.8 %shard_map.115 = bf16[16,48,256]{2,1,0:T(8,128)(2,1)} custom-call(bf16[768,2048]{1,0:T(8,128)(2,1)} %bitcast_convert_fusion.ex_ref), custom_call_target="tpu_custom_call" | custom-call | tf_op jit(solution)/shard_map/pallas_call | solution.py:259
  252.4 0.0 copy-start.6
  252.4 2.6 gather_fusion.1
  255.0 0.3 reshape.174
  255.3 0.0 copy-done.4
  255.3 0.1 copy.16
  255.4 0.7 multiply_reduce_fusion
  256.2 0.7 fusion.13
  256.8 0.7 multiply_reduce_fusion.1
  257.5 7.0 %shard_map.116 = f32[1,256]{1,0:T(1,128)} custom-call(f32[1,256]{1,0:T(1,128)} %bitcast.36), custom_call_target="tpu_custom_call" | custom-call | tf_op jit(solution)/shard_map/pallas_call | solution.py:300
  264.5 0.7 add_rsqrt_fusion
  265.2 0.0 copy-done.6
  265.2 0.8 multiply_convert_fusion.1
  (11 shorter events, 0.1 us)
Async XLA Ops:
  0.6 6.2 %copy-start = (bf16[256,2048]{1,0:T(8,128)(2,1)S(1)}, bf16[256,2048]{1,0:T(8,128)(2,1)}, u32[]{:S(2)}) copy-start(bf16[256,2048]{1,0:T(8,128)(2,1)} %param.10) | copy-start | bytes 3145732
  0.6 23.1 %copy-start.5 = (f32[256]{0:T(256)S(1)}, f32[256]{0:T(256)}, u32[]{:S(2)}) copy-start(f32[256]{0:T(256)} %param.13) | copy-start | bytes 3076
  6.9 20.3 %copy-start.1 = (bf16[8,44,512]{2,0,1:T(8,128)(2,1)S(1)}, bf16[8,44,512]{2,0,1:T(8,128)(2,1)}, u32[]{:S(2)}) copy-start(bf16[8,44,512]{2,0,1:T(8,128)(2,1)} %param.14) | copy-start | bytes 1081348
  6.9 21.2 %copy-start.2 = (bf16[8,44,512]{2,0,1:T(8,128)(2,1)S(1)}, bf16[8,44,512]{2,0,1:T(8,128)(2,1)}, u32[]{:S(2)}) copy-start(bf16[8,44,512]{2,0,1:T(8,128)(2,1)} %param.15) | copy-start | bytes 1081348
  9.3 19.7 %copy-start.3 = (bf16[8,44,512]{2,0,1:T(8,128)(2,1)S(1)}, bf16[8,44,512]{2,0,1:T(8,128)(2,1)}, u32[]{:S(2)}) copy-start(bf16[8,44,512]{2,0,1:T(8,128)(2,1)} %param.16) | copy-start | bytes 1081348
  196.5 58.7 %copy-start.4 = (f32[256,2]{0,1:T(2,128)S(1)}, f32[256,2]{0,1:T(2,128)}, u32[]{:S(2)}) copy-start(f32[256,2]{0,1:T(2,128)} %param.18) | copy-start | bytes 6148
  252.4 12.9 %copy-start.6 = (f32[256]{0:T(256)S(1)}, f32[256]{0:T(256)}, u32[]{:S(2)}) copy-start(f32[256]{0:T(256)} %param.19) | copy-start | bytes 3076

commit v18 on v15

--- a/solution.py
+++ b/solution.py
@@ -65,9 +65,9 @@
             direct.append(copy)
         return local, direct
 
-    def start_forward(k):
+    def start_forward(k, first, last):
         forward = []
-        for d in range(0, side + 1):
+        for d in range(first, last):
             src = lax.rem(j + n_ep - d + 2 * parity * d, n_ep)
             copy = remote(outs[k].at[src, :, cols_a], outs[k].at[src, :, cols_a],
                           fwd_send.at[k, d], fwd_recv.at[k, d], (partner, a, m))
@@ -107,10 +107,11 @@
     waiting = None
     for k in range(3):
         local.wait()
+        forward = start_forward(k, 0, 1)
         for copy in direct:
             copy.wait_recv()
         pending.extend(direct)
-        forward = start_forward(k)
+        forward += start_forward(k, 1, side + 1)
         if k + 1 < 3:
             local, direct = start_direct(k + 1)
         if waiting is not None:

time: 257 us -> 256 us (level)
  no operation moved by 1% of the time
where the time goes in v18:
time: 256 us
  Pallas kernels  210 us (82%)
  matrix products  25.2 us (10%)
  local copies, waits for them, and re-layouts  13.1 us (5%)
  other arithmetic  6.35 us (2%)
    pallas_call x1, Pallas kernels, move_all(): pl.pallas_call(functools.partial(move_kernel, n_ep, n_mx, n_my, replicas)...  138 us
    pallas_call x1, Pallas kernels, send_back(): pl.pallas_call(functools.partial(back_kernel, n_ep, n_my), out_shape=jax....  50.7 us
    pallas_call x2, Pallas kernels, sum_over_my(): pl.pallas_call(functools.partial(sum_kernel, n_my), out_shape=jax.ShapeDt...  21.8 us
    dot_general x1, matrix products, shards(): jnp.einsum('rsp,spd->rd', hidden, w_down, preferred_element_type=jnp.floa...  15.9 us
    dot_general x1, matrix products, shards(): jnp.einsum('rd,spd->rsp', tokens_in, w_up, preferred_element_type=jnp.flo...  6.92 us

profile of v18, /device:TPU:1, one launch (start us, length us, event | category | flops | bytes accessed | tf_op | source)
XLA Modules:
  0.0 255.8 jit_solution(13996168638713363471)
XLA Ops:
  0.6 0.0 copy-start
  0.6 0.0 copy-start.5
  0.7 0.9 copy.18
  1.6 0.1 eq.31
  1.7 1.1 reduce-window.6
  2.9 0.2 slice_reduce_fusion
  3.1 0.1 eq.27
  3.3 0.1 fusion.4
  3.4 0.7 broadcast_multiply_fusion
  4.0 0.1 copy.17
  4.2 0.1 mul.95
  4.4 2.4 scatter_custom_fusion
  6.9 0.0 copy-done
  6.9 0.0 copy-start.1
  6.9 0.0 copy-start.2
  6.9 2.4 multiply_reduce_fusion.2
  9.3 0.0 copy-start.3
  9.3 13.8 %shard_map.113 = f32[1,256]{1,0:T(1,128)} custom-call(f32[1,256]{1,0:T(1,128)} %bitcast.33), custom_call_target="tpu_custom_call" | custom-call | tf_op jit(solution)/shard_map/pallas_call | solution.py:301
  23.1 0.7 add_rsqrt_fusion.1
  23.8 0.0 copy-done.5
  23.8 0.1 multiply_convert_fusion.2
  23.9 3.3 %gather_fusion = bf16[768,256]{1,0:T(8,128)(2,1)} fusion(bf16[257,256]{1,0:T(8,128)(2,1)S(1)} %concatenate.3, s32[1024]{0:T(1024)S(1)} %pad_clamp_fusion.1), kind=kCustom, calls=%fused_computation | custom fusion | bytes 789504 | tf_op jit(solution)/shard_map/gather | solution.py:357
  27.2 0.0 copy-done.1
  27.2 0.9 copy.20.gate_ref
  28.1 0.0 copy-done.2
  28.1 0.9 copy.21.up_ref
  29.0 0.0 copy-done.3
  29.0 0.8 copy.22.down_ref
  29.8 137.8 %shard_map.114 = (bf16[16,48,2048]{2,1,0:T(8,128)(2,1)}, bf16[16,44,2048]{2,1,0:T(8,128)(2,1)}, bf16[16,44,2048]{2,1,0:T(8,128)(2,1)}, bf16[16,44,2048]{2,1,0:T(8,128)(2,1)}) custom-call(bf16[16,48,256]{2,1,0:T(8,128)(2,1)} %bitcast.29, bf16[8,44,512]{2,1,0:T(8,128)(2,1)} %copy.20.gate_ref, bf16[8,44,512]{2,1,0:T(8,128)(2,1)} %copy.21.up_ref, ...), custom_call_target="tpu_custom_call" | custom-call | tf_op jit(solution)/shard_map/pallas_call | solution.py:151
  167.6 6.9 %fusion.14 = f32[768,16,44]{0,2,1:T(8,128)} fusion(bf16[768,2048,1]{1,0,2:T(8,128)(2,1)} %bitcast.37, bf16[16,44,2048]{2,1,0:T(8,128)(2,1)} %get-tuple-element.8), kind=kOutput, calls=%fused_computation.46 | convolution fusion | flops 2214592512 | bytes 8192000 | tf_op jit(solution)/shard_map/rd,spd->rsp/dot_general | solution.py:364
  174.5 15.9 %bitcast_convert_fusion.ex_ref = bf16[768,2048]{1,0:T(8,128)(2,1)} fusion(bf16[16,44,2048]{2,1,0:T(8,128)(2,1)} %get-tuple-element.9, f32[768,16,44]{0,2,1:T(8,128)} %fusion.14, bf16[768,2048,1]{1,0,2:T(8,128)(2,1)} %bitcast.38, bf16[16,44,2048]{2,1,0:T(8,128)(2,1)} %get-tuple-element.7), kind=kOutput, calls=%fused_computation.3 | convolution fusion | flops 4434001920 | bytes 14221312 | tf_op jit(solution)/shard_map/rsp,spd->rd/dot_general | solution.py:366
  190.5 0.0 copy-start.4
  190.5 50.7 %shard_map.115 = bf16[16,48,256]{2,1,0:T(8,128)(2,1)} custom-call(bf16[768,2048]{1,0:T(8,128)(2,1)} %bitcast_convert_fusion.ex_ref), custom_call_target="tpu_custom_call" | custom-call | tf_op jit(solution)/shard_map/pallas_call | solution.py:260
  241.1 0.0 copy-start.6
  241.2 2.6 %gather_fusion.1 = bf16[512,256]{1,0:T(8,128)(2,1)S(1)} fusion(bf16[768,256]{1,0:T(8,128)(2,1)} %bitcast.28, s32[1024]{0:T(1024)S(1)} %pad_clamp_fusion), kind=kCustom, calls=%fused_computation.1 | custom fusion | bytes 526336 | tf_op jit(solution)/shard_map/gather | solution.py:371
  243.8 0.3 reshape.174
  244.0 0.0 copy-done.4
  244.1 0.1 copy.16
  244.2 0.7 multiply_reduce_fusion
  244.9 0.7 fusion.13
  245.6 0.7 multiply_reduce_fusion.1
  246.3 8.0 %shard_map.116 = f32[1,256]{1,0:T(1,128)} custom-call(f32[1,256]{1,0:T(1,128)} %bitcast.36), custom_call_target="tpu_custom_call" | custom-call | tf_op jit(solution)/shard_map/pallas_call | solution.py:301
  254.3 0.7 add_rsqrt_fusion
  255.0 0.0 copy-done.6
  255.0 0.8 multiply_convert_fusion.1
  (11 shorter events, 0.1 us)
Async XLA Ops:
  0.6 6.2 %copy-start = (bf16[256,2048]{1,0:T(8,128)(2,1)S(1)}, bf16[256,2048]{1,0:T(8,128)(2,1)}, u32[]{:S(2)}) copy-start(bf16[256,2048]{1,0:T(8,128)(2,1)} %param.10) | copy-start | bytes 3145732
  0.6 23.1 %copy-start.5 = (f32[256]{0:T(256)S(1)}, f32[256]{0:T(256)}, u32[]{:S(2)}) copy-start(f32[256]{0:T(256)} %param.13) | copy-start | bytes 3076
  6.9 20.3 %copy-start.1 = (bf16[8,44,512]{2,0,1:T(8,128)(2,1)S(1)}, bf16[8,44,512]{2,0,1:T(8,128)(2,1)}, u32[]{:S(2)}) copy-start(bf16[8,44,512]{2,0,1:T(8,128)(2,1)} %param.14) | copy-start | bytes 1081348
  6.9 21.2 %copy-start.2 = (bf16[8,44,512]{2,0,1:T(8,128)(2,1)S(1)}, bf16[8,44,512]{2,0,1:T(8,128)(2,1)}, u32[]{:S(2)}) copy-start(bf16[8,44,512]{2,0,1:T(8,128)(2,1)} %param.15) | copy-start | bytes 1081348
  9.3 19.7 %copy-start.3 = (bf16[8,44,512]{2,0,1:T(8,128)(2,1)S(1)}, bf16[8,44,512]{2,0,1:T(8,128)(2,1)}, u32[]{:S(2)}) copy-start(bf16[8,44,512]{2,0,1:T(8,128)(2,1)} %param.16) | copy-start | bytes 1081348
  190.5 53.6 %copy-start.4 = (f32[256,2]{0,1:T(2,128)S(1)}, f32[256,2]{0,1:T(2,128)}, u32[]{:S(2)}) copy-start(f32[256,2]{0,1:T(2,128)} %param.18) | copy-start | bytes 6148
  241.1 13.9 %copy-start.6 = (f32[256]{0:T(256)S(1)}, f32[256]{0:T(256)}, u32[]{:S(2)}) copy-start(f32[256]{0:T(256)} %param.19) | copy-start | bytes 3076

commit v19 on v18

--- a/solution.py
+++ b/solution.py
@@ -108,12 +108,13 @@
     for k in range(3):
         local.wait()
         forward = start_forward(k, 0, 1)
-        for copy in direct:
-            copy.wait_recv()
-        pending.extend(direct)
-        forward += start_forward(k, 1, side + 1)
+        arriving = direct
         if k + 1 < 3:
             local, direct = start_direct(k + 1)
+        for copy in arriving:
+            copy.wait_recv()
+        pending.extend(arriving)
+        forward += start_forward(k, 1, side + 1)
         if waiting is not None:
             relay(*waiting)
         for copy in forward:

time: 256 us -> 265 us (1.035)
  Pallas kernels: 210 us -> 219 us
    pallas_call x1, Pallas kernels: 138 us -> 143 us  [move_all(): pl.pallas_call(functools.partial(move_kernel, n_ep, n_mx, n_my, replicas)...]
    pallas_call x1, Pallas kernels: 50.7 us -> 53.5 us  [send_back(): pl.pallas_call(functools.partial(back_kernel, n_ep, n_my), out_shape=jax....]
where the time goes in v19:
time: 265 us; the launch traced here: 264 us
  Pallas kernels  219 us (83%)
  matrix products  25.2 us (10%)
  local copies, waits for them, and re-layouts  13.1 us (5%)
  other arithmetic  6.35 us (2%)
    pallas_call x1, Pallas kernels, move_all(): pl.pallas_call(functools.partial(move_kernel, n_ep, n_mx, n_my, replicas)...  143 us
    pallas_call x1, Pallas kernels, send_back(): pl.pallas_call(functools.partial(back_kernel, n_ep, n_my), out_shape=jax....  53.5 us
    pallas_call x2, Pallas kernels, sum_over_my(): pl.pallas_call(functools.partial(sum_kernel, n_my), out_shape=jax.ShapeDt...  22.4 us
    dot_general x1, matrix products, shards(): jnp.einsum('rsp,spd->rd', hidden, w_down, preferred_element_type=jnp.floa...  15.9 us
    dot_general x1, matrix products, shards(): jnp.einsum('rd,spd->rsp', tokens_in, w_up, preferred_element_type=jnp.flo...  6.92 us

profile of v19, /device:TPU:1, one launch (start us, length us, event | category | flops | bytes accessed | tf_op | source)
XLA Modules:
  0.0 264.3 jit_solution(958796649126870518)
XLA Ops:
  0.6 0.0 copy-start
  0.6 0.0 copy-start.5
  0.7 0.9 copy.18
  1.6 0.1 eq.31
  1.7 1.1 reduce-window.6
  2.9 0.2 slice_reduce_fusion
  3.1 0.1 eq.27
  3.3 0.1 fusion.4
  3.4 0.7 broadcast_multiply_fusion
  4.0 0.1 copy.17
  4.2 0.1 mul.95
  4.4 2.4 scatter_custom_fusion
  6.9 0.0 copy-done
  6.9 0.0 copy-start.1
  6.9 0.0 copy-start.2
  6.9 2.4 multiply_reduce_fusion.2
  9.3 0.0 copy-start.3
  9.3 13.8 %shard_map.113 = f32[1,256]{1,0:T(1,128)} custom-call(f32[1,256]{1,0:T(1,128)} %bitcast.33), custom_call_target="tpu_custom_call" | custom-call | tf_op jit(solution)/shard_map/pallas_call | solution.py:302
  23.1 0.7 add_rsqrt_fusion.1
  23.8 0.0 copy-done.5
  23.8 0.1 multiply_convert_fusion.2
  23.9 3.3 %gather_fusion = bf16[768,256]{1,0:T(8,128)(2,1)} fusion(bf16[257,256]{1,0:T(8,128)(2,1)S(1)} %concatenate.3, s32[1024]{0:T(1024)S(1)} %pad_clamp_fusion.1), kind=kCustom, calls=%fused_computation | custom fusion | bytes 789504 | tf_op jit(solution)/shard_map/gather | solution.py:358
  27.2 0.0 copy-done.1
  27.2 0.9 copy.20.gate_ref
  28.1 0.0 copy-done.2
  28.1 0.9 copy.21.up_ref
  29.0 0.0 copy-done.3
  29.0 0.8 copy.22.down_ref
  29.8 142.9 %shard_map.114 = (bf16[16,48,2048]{2,1,0:T(8,128)(2,1)}, bf16[16,44,2048]{2,1,0:T(8,128)(2,1)}, bf16[16,44,2048]{2,1,0:T(8,128)(2,1)}, bf16[16,44,2048]{2,1,0:T(8,128)(2,1)}) custom-call(bf16[16,48,256]{2,1,0:T(8,128)(2,1)} %bitcast.29, bf16[8,44,512]{2,1,0:T(8,128)(2,1)} %copy.20.gate_ref, bf16[8,44,512]{2,1,0:T(8,128)(2,1)} %copy.21.up_ref, ...), custom_call_target="tpu_custom_call" | custom-call | tf_op jit(solution)/shard_map/pallas_call | solution.py:152
  172.7 6.9 %fusion.14 = f32[768,16,44]{0,2,1:T(8,128)} fusion(bf16[768,2048,1]{1,0,2:T(8,128)(2,1)} %bitcast.37, bf16[16,44,2048]{2,1,0:T(8,128)(2,1)} %get-tuple-element.8), kind=kOutput, calls=%fused_computation.46 | convolution fusion | flops 2214592512 | bytes 8192000 | tf_op jit(solution)/shard_map/rd,spd->rsp/dot_general | solution.py:365
  179.6 15.9 %bitcast_convert_fusion.ex_ref = bf16[768,2048]{1,0:T(8,128)(2,1)} fusion(bf16[16,44,2048]{2,1,0:T(8,128)(2,1)} %get-tuple-element.9, f32[768,16,44]{0,2,1:T(8,128)} %fusion.14, bf16[768,2048,1]{1,0,2:T(8,128)(2,1)} %bitcast.38, bf16[16,44,2048]{2,1,0:T(8,128)(2,1)} %get-tuple-element.7), kind=kOutput, calls=%fused_computation.3 | convolution fusion | flops 4434001920 | bytes 14221312 | tf_op jit(solution)/shard_map/rsp,spd->rd/dot_general | solution.py:367
  195.6 0.0 copy-start.4
  195.6 53.5 %shard_map.115 = bf16[16,48,256]{2,1,0:T(8,128)(2,1)} custom-call(bf16[768,2048]{1,0:T(8,128)(2,1)} %bitcast_convert_fusion.ex_ref), custom_call_target="tpu_custom_call" | custom-call | tf_op jit(solution)/shard_map/pallas_call | solution.py:261
  249.1 0.0 copy-start.6
  249.1 2.6 gather_fusion.1
  251.7 0.3 reshape.174
  252.0 0.0 copy-done.4
  252.0 0.1 copy.16
  252.2 0.7 multiply_reduce_fusion
  252.9 0.7 fusion.13
  253.6 0.7 multiply_reduce_fusion.1
  254.2 8.6 %shard_map.116 = f32[1,256]{1,0:T(1,128)} custom-call(f32[1,256]{1,0:T(1,128)} %bitcast.36), custom_call_target="tpu_custom_call" | custom-call | tf_op jit(solution)/shard_map/pallas_call | solution.py:302
  262.8 0.7 add_rsqrt_fusion
  263.5 0.0 copy-done.6
  263.5 0.8 multiply_convert_fusion.1
  (11 shorter events, 0.1 us)
Async XLA Ops:
  0.6 6.2 %copy-start = (bf16[256,2048]{1,0:T(8,128)(2,1)S(1)}, bf16[256,2048]{1,0:T(8,128)(2,1)}, u32[]{:S(2)}) copy-start(bf16[256,2048]{1,0:T(8,128)(2,1)} %param.10) | copy-start | bytes 3145732
  0.6 23.1 %copy-start.5 = (f32[256]{0:T(256)S(1)}, f32[256]{0:T(256)}, u32[]{:S(2)}) copy-start(f32[256]{0:T(256)} %param.13) | copy-start | bytes 3076
  6.9 20.3 %copy-start.1 = (bf16[8,44,512]{2,0,1:T(8,128)(2,1)S(1)}, bf16[8,44,512]{2,0,1:T(8,128)(2,1)}, u32[]{:S(2)}) copy-start(bf16[8,44,512]{2,0,1:T(8,128)(2,1)} %param.14) | copy-start | bytes 1081348
  6.9 21.2 %copy-start.2 = (bf16[8,44,512]{2,0,1:T(8,128)(2,1)S(1)}, bf16[8,44,512]{2,0,1:T(8,128)(2,1)}, u32[]{:S(2)}) copy-start(bf16[8,44,512]{2,0,1:T(8,128)(2,1)} %param.15) | copy-start | bytes 1081348
  9.3 19.7 %copy-start.3 = (bf16[8,44,512]{2,0,1:T(8,128)(2,1)S(1)}, bf16[8,44,512]{2,0,1:T(8,128)(2,1)}, u32[]{:S(2)}) copy-start(bf16[8,44,512]{2,0,1:T(8,128)(2,1)} %param.16) | copy-start | bytes 1081348
  195.6 56.4 %copy-start.4 = (f32[256,2]{0,1:T(2,128)S(1)}, f32[256,2]{0,1:T(2,128)}, u32[]{:S(2)}) copy-start(f32[256,2]{0,1:T(2,128)} %param.18) | copy-start | bytes 6148
  249.1 14.4 %copy-start.6 = (f32[256]{0:T(256)S(1)}, f32[256]{0:T(256)}, u32[]{:S(2)}) copy-start(f32[256]{0:T(256)} %param.19) | copy-start | bytes 3076
